TPU v7x, 256 devices: a whole 4x4x8 slice. The times are simulated.
256 devices in a mesh: sec: 4 (over z_lo, core), lat: 16 (over x, y), col: 4 (over z_hi).
Axes of the slice: x: 4, y: 4, z: 8 (z_hi: 4, z_lo: 2; z = z_hi * 2 + z_lo), core: 2. Of those that a mesh axis runs over, the one named last changes fastest.
Arguments:
- state: float32 [1, 4, 28, 192, 384], P(None, 'sec', None, 'lat', 'col'), may hold values from -6 to 6
- forcing: float32 [1, 4, 28, 192, 384], P(None, 'sec', None, 'lat', 'col'), may hold values from -4 to 4
- crm_moisture: bfloat16 [1, 32, 28, 64, 4, 288], P(None, None, None, ('sec', 'lat'), 'col'), may hold values from -6 to 6
- cloud_order: int32 [4, 16, 1152], P('col', 'lat'), may hold values from 0 to 1151, each once within a row
- wave_table: int32 [128], replicated, may hold values from 0 to 127, each once
Outputs:
- state_out: float32 [1, 4, 28, 192, 384], P(None, 'sec', None, 'lat', 'col')
- spectral: float32 [4, 1, 28, 128, 2, 128], P('sec', None, 'col', 'lat')
Inputs may be any that keep to these rules, and one draw needn't show every extreme that they name: `cloud_order`: every row lists each of the 1152 columns of a band block once. `wave_table`: each wavenumber stands in exactly one slot.
All inputs are finite; a program needn't handle non-finite values.
Results may differ from a plain program's by a relative error of at most 0.0003.
Values sent between devices are 32-bit elements; how exact they have to be, the bound alone decides.
No kernel may reach another device: no remote copies, remote signals or barrier semaphores. Data moves between devices by JAX's collectives and lax.ppermute only.
A program may use at most 64 MiB of HBM per device.

v0:
```python
import math

import jax
import jax.numpy as jnp
from jax import lax
from jax.sharding import PartitionSpec as P

NLON = 384
NLAT = 192
MMAX = 128
NSUB = 4


COURANT_SCALE = 0.4
CONDENSE = 0.5


def transport(values, courant, mixing):
    forward = jnp.roll(values, -1, axis=0)
    behind = jnp.roll(values, 1, axis=0)
    return -0.5 * courant * (forward - behind) + mixing * (forward - 2.0 * values + behind)


def cloud_model(vertical_state_stack, forcing, vapour_mass_fraction):
    wind_u = vertical_state_stack[0]
    wind_v = vertical_state_stack[1]
    atmospheric_warmth = vertical_state_stack[2]
    humidity = vertical_state_stack[3]
    courant = COURANT_SCALE * jnp.tanh(wind_u)
    mixing = 0.2 + 0.5 * jnp.abs(courant)
    convective_warming_rate = jnp.broadcast_to(atmospheric_warmth, vapour_mass_fraction.shape)
    crm_water = humidity + vapour_mass_fraction
    start_water = crm_water
    ground_precipitation = jnp.zeros_like(atmospheric_warmth)
    for substep in range(NSUB):
        heat_move = transport(convective_warming_rate, courant, mixing)
        water_move = transport(crm_water, courant, mixing)
        condensed = CONDENSE * jnp.maximum(crm_water - convective_warming_rate, 0.0)
        convective_warming_rate = (
            convective_warming_rate + heat_move + condensed + forcing[2] / NSUB
        )
        crm_water = crm_water + water_move - condensed + forcing[3] / NSUB
        ground_precipitation = ground_precipitation + jnp.mean(condensed, axis=0)
    ground_precipitation = ground_precipitation / NSUB
    zonal_velocity_rate = -ground_precipitation * wind_u + forcing[0]
    meridional_velocity_rate = -ground_precipitation * wind_v + forcing[1]
    warming_rate_change = jnp.mean(convective_warming_rate, axis=0) - atmospheric_warmth
    vapour_rate_change = jnp.mean(crm_water - start_water, axis=0)
    return jnp.stack(
        (zonal_velocity_rate, meridional_velocity_rate, warming_rate_change, vapour_rate_change)
    )


def trig_table(longitudes, wave_numbers):
    phase = (longitudes[:, None] * wave_numbers[None, :] % NLON).astype(jnp.float32) * (
        2.0 * math.pi / NLON
    )
    return jnp.stack((jnp.cos(phase), jnp.sin(phase)), axis=1) / math.sqrt(NLON)


def legendre_table(orders):
    colatitude = (jnp.arange(NLAT, dtype=jnp.int32).astype(jnp.float32) + 0.5) * (math.pi / NLAT)
    cosine = jnp.cos(colatitude)[None, :]
    sine_lat = jnp.sin(colatitude)
    order_col = orders.astype(jnp.float32)[:, None]
    log_diag = 0.5 * (
        lax.lgamma(order_col + 1.5) - lax.lgamma(jnp.float32(1.5)) - lax.lgamma(order_col + 1.0)
    )
    log_diag = log_diag + order_col * jnp.log(sine_lat)[None, :] - 0.5 * math.log(2.0)
    diagonal = jnp.exp(log_diag)
    empty = jnp.zeros_like(diagonal)

    def march_forward(carried, degree):
        previous, current = carried
        deg_float = degree.astype(jnp.float32)
        active = deg_float > order_col
        numerator = jnp.where(active, 4.0 * deg_float * deg_float - 1.0, 1.0)
        bottom = jnp.where(active, deg_float * deg_float - order_col * order_col, 1.0)
        lower_deg = deg_float - 1.0
        retreat = jnp.sqrt(
            jnp.maximum(lower_deg * lower_deg - order_col * order_col, 0.0)
            / (4.0 * lower_deg * lower_deg - 1.0)
        )
        grown = jnp.sqrt(numerator / bottom) * (cosine * current - retreat * previous)
        fresh_row = jnp.where(active, grown, jnp.where(deg_float == order_col, diagonal, 0.0))
        return ((current, fresh_row), fresh_row)

    _, legendre_rows = lax.scan(
        march_forward, (empty, empty), jnp.arange(MMAX, dtype=jnp.int32), unroll=8
    )
    weights = sine_lat / math.sqrt(NLAT)
    return legendre_rows * weights[None, None, :]


def shards(state, forcing, crm_moisture, cloud_order, wave_table):
    members, _, levels, band_rows, lon_block = state.shape
    sections = lax.axis_size("sec")
    lat_bands = lax.axis_size("lat")
    block_cols = band_rows * lon_block
    targets = sections * lat_bands
    per_target = block_cols // targets
    run_cols = lat_bands * per_target
    slot_list = cloud_order[0, 0]
    flat_state = state[:, 0].reshape(members, levels, block_cols)
    flat_force = forcing[:, 0].reshape(members, levels, block_cols)
    stacked = jnp.stack((flat_state, flat_force))
    column_ids = jnp.arange(block_cols, dtype=jnp.int32)
    selector = (slot_list[:, None] == column_ids[None, :]).astype(jnp.float32)
    selector = selector.reshape(targets, per_target, block_cols)
    by_target = jnp.einsum("xelc,tpc->txelp", stacked, selector, precision=lax.Precision.HIGHEST)
    send_width = 2 * members * levels * per_target
    outgoing = by_target.reshape(targets, 1, send_width)
    arrived = lax.all_to_all(outgoing, ("sec", "lat"), split_axis=0, concat_axis=1, tiled=True)
    arrived = arrived.reshape(sections, lat_bands, 2, members, levels, per_target)
    arrived = arrived.transpose(2, 3, 0, 4, 1, 5).reshape(2, members, sections, levels, run_cols)
    vapour_mass_fraction = crm_moisture[:, :, :, 0, 0, :].astype(jnp.float32)
    tendency = jax.vmap(cloud_model)(arrived[0], arrived[1], vapour_mass_fraction)
    back_width = members * levels * per_target
    parted = tendency.reshape(members, sections, levels, lat_bands, per_target).transpose(
        1, 3, 0, 2, 4
    )
    homeward = parted.reshape(targets, 1, back_width)
    returned = lax.all_to_all(homeward, ("sec", "lat"), split_axis=0, concat_axis=1, tiled=True)
    returned = returned.reshape(targets, members, levels, per_target)
    column_tend = jnp.einsum("telp,tpc->elc", returned, selector, precision=lax.Precision.HIGHEST)
    new_state = state + column_tend.reshape(members, 1, levels, band_rows, lon_block)
    fields_now = new_state[:, 0]
    lon_start = lax.axis_index("col") * lon_block
    trig_rows = trig_table(lon_start + jnp.arange(lon_block, dtype=jnp.int32), wave_table)
    spectra = lax.psum_scatter(
        jnp.einsum("elay,ycs->leacs", fields_now, trig_rows, precision=lax.Precision.HIGHEST),
        "col",
        scatter_dimension=0,
        tiled=True,
    )
    owner_count = MMAX // lat_bands
    owned_waves = lax.dynamic_slice_in_dim(
        wave_table, lax.axis_index("lat") * owner_count, owner_count
    )
    weighted = legendre_table(owned_waves)
    coeffs = jnp.einsum(
        "leacs,nsa->lescn",
        lax.all_to_all(spectra, "lat", split_axis=4, concat_axis=2, tiled=True),
        weighted,
        precision=lax.Precision.HIGHEST,
    )
    return (new_state, coeffs.transpose(1, 0, 2, 3, 4)[None])


def solution(mesh):
    placed = (
        P(None, "sec", None, "lat", "col"),
        P(None, "sec", None, "lat", "col"),
        P(None, None, None, ("sec", "lat"), "col", None),
        P("col", "lat", None),
        P(),
    )
    return jax.shard_map(
        shards,
        mesh=mesh,
        in_specs=placed,
        out_specs=(P(None, "sec", None, "lat", "col"), P("sec", None, "col", "lat", None, None)),
        check_vma=False,
    )
```

profile of v0, /device:TPU:2, one launch (start us, length us, event | category | flops | bytes accessed | tf_op | source)
XLA Modules:
  0.0 212.8 jit_solution(3303707262347530788)
XLA Ops:
  7.2 0.7 reduce.6
  8.1 1.4 reduce.8
  9.6 1.4 reduce.7
  11.0 4.3 %fusion.56 = f32[64,2,1,28,18]{0,3,1,4,2:T(8,128)S(1)} fusion(s32[64,18]{0,1:T(8,128)S(1)} %copy.55, f32[1,1,28,1152]{3,2,0,1:T(8,128)S(1)} %stack_reshape_squeeze.9, f32[1,1,28,1152]{3,2,0,1:T(8,128)S(1)} %stack_reshape_squeeze.8), kind=kOutput, calls=%fused_computation.126 | convolution fusion | flops 893205504 | bytes 520704 | tf_op jit(solution)/shard_map/xelc,tpc->txelp/dot_general | solution.py:110
  15.9 1.3 copy.59
  17.3 9.4 %all-to-all-start = ((f32[64,1,1008]{2,1,0:T(1,128)}), f32[64,1,1008]{2,1,0:T(1,128)S(1)}, u32[]{:S(2)}, u32[]{:S(2)}) async-start(f32[64,1,1008]{2,1,0:T(1,128)} %copy.59), calls=%async_computation | async-start | bytes 524288 | tf_op jit(solution)/shard_map/all_to_all | solution.py:113
  26.9 8.5 %all-to-all-done = f32[64,1,1008]{2,1,0:T(1,128)S(1)} async-done(((f32[64,1,1008]{2,1,0:T(1,128)}), f32[64,1,1008]{2,1,0:T(1,128)S(1)}, u32[]{:S(2)}, u32[]{:S(2)}) %all-to-all-start) | async-done | bytes 258080 | tf_op jit(solution)/shard_map/all_to_all | solution.py:113
  35.4 0.6 reduce.9
  36.0 2.1 reshape.4329
  40.8 0.7 copy-done
  41.6 0.9 fusion.52
  42.8 2.9 %fusion.65 = (f32[28,288]{1,0:T(8,128)S(1)}, f32[28,288]{1,0:T(8,128)S(1)}, f32[1,32,28,288]{3,1,2,0:T(8,128)S(1)}) fusion(f32[28,288]{1,0:T(8,128)S(1)} %get-tuple-element.406, bf16[1,32,28,1,1,288]{5,1,4,3,2,0:T(8,128)(2,1)S(1)} %copy-done, f32[28,288]{1,0:T(8,128)S(1)} %get-tuple-element.411, f32[28,288]{1,0:T(8,128)S(1)} %broadcast_multiply_fusion.2, ...), kind=kLoop, calls=%fused_computation.133 | loop fusion | flops 8499456 | bytes 4935168 | tf_op jit(solution)/shard_map/vmap()/reduce_sum | solution.py:43
  46.3 3.4 %fusion.66 = (f32[28,288]{1,0:T(8,128)S(1)}, f32[1,32,28,288]{3,1,2,0:T(8,128)S(1)}, f32[1,32,28,288]{3,1,2,0:T(8,128)S(1)}) fusion(f32[28,288]{1,0:T(8,128)S(1)} %get-tuple-element.407, f32[1,32,28,288]{3,1,2,0:T(8,128)S(1)} %get-tuple-element.324, f32[28,288]{1,0:T(8,128)S(1)} %get-tuple-element.406, bf16[1,32,28,1,1,288]{5,1,4,3,2,0:T(8,128)(2,1)S(1)} %copy-done, ...), kind=kLoop, calls=%fused_computation.134 | loop fusion | flops 12120192 | bytes 9031680 | tf_op jit(solution)/shard_map/vmap()/reduce_sum | solution.py:43
  50.4 2.0 subtract_add_fusion
  53.1 3.1 %add_reduce_fusion = (f32[28,288]{1,0:T(8,128)S(1)}, f32[28,288]{1,0:T(8,128)S(1)}, f32[28,288]{1,0:T(8,128)S(1)}) fusion(f32[1,32,28,288]{3,1,2,0:T(8,128)S(1)} %get-tuple-element.365, f32[1,31,28,288]{3,1,2,0:T(8,128)S(1)} %get-tuple-element.377, f32[1,1,28,288]{3,1,2,0:T(1,128)S(1)} %get-tuple-element.379, f32[1,1,28,288]{3,1,2,0:T(1,128)S(1)} %get-tuple-element.378, ...), kind=kLoop, calls=%fused_computation.115 | loop fusion | flops 8491392 | bytes 6967296 | tf_op jit(solution)/shard_map/vmap()/reduce_sum | solution.py:47
  57.9 1.9 reshape.4347
  59.8 5.6 %all-to-all-start.1 = ((f32[64,1,504]{2,1,0:T(1,128)}), f32[64,1,504]{2,1,0:T(1,128)S(1)}, u32[]{:S(2)}, u32[]{:S(2)}) async-start(f32[64,1,504]{2,1,0:T(1,128)} %reshape.4347), calls=%async_computation.1 | async-start | bytes 262144 | tf_op jit(solution)/shard_map/all_to_all | solution.py:123
  65.9 7.0 %all-to-all-done.1 = f32[64,1,504]{2,1,0:T(1,128)S(1)} async-done(((f32[64,1,504]{2,1,0:T(1,128)}), f32[64,1,504]{2,1,0:T(1,128)S(1)}, u32[]{:S(2)}, u32[]{:S(2)}) %all-to-all-start.1) | async-done | bytes 129056 | tf_op jit(solution)/shard_map/all_to_all | solution.py:123
  73.1 2.5 %fusion.62 = f32[1,1,28,12,96]{4,2,3,1,0:T(8,128)S(1)} fusion(s32[12,96]{1,0:T(8,128)S(1)} %multiply_add_fusion.1, s32[18,64]{1,0:T(8,128)S(1)} %copy.67, f32[64,28,18]{0,2,1:T(8,128)S(1)} %reshape.4331, f32[1,1,28,12,96]{4,1,3,2,0:T(1,128)S(1)} %copy-done.1), kind=kOutput, calls=%fused_computation.129 | convolution fusion | flops 447266304 | bytes 396288 | tf_op jit(solution)/shard_map/telp,tpc->elc/dot_general | solution.py:125
  76.1 1.0 copy.70
  77.1 106.6 %while.19 = (s32[]{:T(128)}, f32[8,192]{1,0:T(8,128)S(1)}, f32[8,192]{1,0:T(8,128)S(1)}, f32[16,8,8,192]{3,2,1,0:T(8,128)S(1)}, s32[16,8]{0,1:T(8,128)S(1)}, /*i...) while((s32[]{:T(128)}, f32[8,192]{1,0:T(8,128)S(1)}, ...), condition=%wide.region_7.8_spmd.clone.clone, body=%wide.region_6.7_spmd.clone.clone.sunk | while | flops 228562 | bytes 435795 | solution.py:88
  123.8 0.6 fusion.125
  185.6 0.9 constant_dynamic-slice_fusion.1
  186.5 1.1 copy.71
  187.6 2.0 reshape.4361
  189.7 4.9 %all-to-all-start.2 = ((f32[16,1,1344]{2,1,0:T(1,128)}), f32[16,1,1344]{2,1,0:T(1,128)S(1)}, u32[]{:S(2)}, u32[]{:S(2)}) async-start(f32[16,1,1344]{2,1,0:T(1,128)} %reshape.4361), calls=%async_computation.2 | async-start | bytes 180224 | tf_op jit(solution)/shard_map/all_to_all | solution.py:143
  194.6 0.8 copy.75
  195.5 5.5 %all-to-all-done.2 = f32[16,1,1344]{2,1,0:T(1,128)S(1)} async-done(((f32[16,1,1344]{2,1,0:T(1,128)}), f32[16,1,1344]{2,1,0:T(1,128)S(1)}, u32[]{:S(2)}, u32[]{:S(2)}) %all-to-all-start.2) | async-done | bytes 86048 | tf_op jit(solution)/shard_map/all_to_all | solution.py:143
  201.4 0.9 reduce.16
  202.3 1.4 reshape.4362
  204.4 0.9 convolution_bitcast_fusion.1
  205.3 0.7 copy.76
  (326 shorter events, 35.4 us)
Async XLA Ops:
  15.4 11.3 %copy-start.2 = (s32[128]{0:T(128)S(1)}, s32[128]{0:T(128)}, u32[]{:S(2)}) copy-start(s32[128]{0:T(128)} %param.11) | copy-start | bytes 1540
  17.3 18.1 %all-to-all-start = ((f32[64,1,1008]{2,1,0:T(1,128)}), f32[64,1,1008]{2,1,0:T(1,128)S(1)}, u32[]{:S(2)}, u32[]{:S(2)}) async-start(f32[64,1,1008]{2,1,0:T(1,128)} %copy.59), calls=%async_computation | async-start | bytes 524288 | tf_op jit(solution)/shard_map/all_to_all | solution.py:113
  40.5 1.1 copy-start
  57.9 15.2 %copy-start.1 = (f32[1,1,28,12,96]{4,1,3,2,0:T(1,128)S(1)}, f32[1,1,28,12,96]{4,1,3,2,0:T(1,128)}, u32[]{:S(2)}) copy-start(f32[1,1,28,12,96]{4,1,3,2,0:T(1,128)} %param.7) | copy-start | bytes 387076
  59.8 13.1 %all-to-all-start.1 = ((f32[64,1,504]{2,1,0:T(1,128)}), f32[64,1,504]{2,1,0:T(1,128)S(1)}, u32[]{:S(2)}, u32[]{:S(2)}) async-start(f32[64,1,504]{2,1,0:T(1,128)} %reshape.4347), calls=%async_computation.1 | async-start | bytes 262144 | tf_op jit(solution)/shard_map/all_to_all | solution.py:123
  65.4 120.2 %all-reduce.3.cloned.1.call-start = ((), (), s32[]{:S(2)}) async-start(), calls=%async_computation.3 | async-start | bytes 688128
  183.7 0.7 copy-start.3
  189.7 11.3 %all-to-all-start.2 = ((f32[16,1,1344]{2,1,0:T(1,128)}), f32[16,1,1344]{2,1,0:T(1,128)S(1)}, u32[]{:S(2)}, u32[]{:S(2)}) async-start(f32[16,1,1344]{2,1,0:T(1,128)} %reshape.4361), calls=%async_computation.2 | async-start | bytes 180224 | tf_op jit(solution)/shard_map/all_to_all | solution.py:143
Sparse Core Ops, SparseCore 0:
  77.2 51.7 all-reduce.2
where the time goes:
time: 215 us; the launch traced here: 213 us
  loops' own time  82 us (38%)
  local copies, waits for them, and re-layouts  34.4 us (16%)
  other arithmetic  32.1 us (15%)
  waiting for transfers between devices  21 us (10%)
  starting transfers between devices  20 us (9%)
  between operations  15.2 us (7%)
  matrix products  8.19 us (4%)
    another operation x1, loops' own time, legendre_table(): lax.scan(march_forward, (empty, empty), jnp.arange(MMAX, dtype=jnp.int32)...  82 us
    while x112, other arithmetic  9.89 us
    slice x16, local copies, waits for them, and re-layouts, legendre_table(): lax.scan(march_forward, (empty, empty), jnp.arange(MMAX, dtype=jnp.int32)...  9.64 us
    all_to_all x1, starting transfers between devices, shards(): lax.all_to_all(outgoing, ('sec', 'lat'), split_axis=0, concat_axis=1, til...  9.38 us
    all_to_all x1, waiting for transfers between devices, shards(): lax.all_to_all(outgoing, ('sec', 'lat'), split_axis=0, concat_axis=1, til...  8.47 us
    unnamed x17, local copies, waits for them, and re-layouts  7.45 us
    all_to_all x1, waiting for transfers between devices, shards(): lax.all_to_all(homeward, ('sec', 'lat'), split_axis=0, concat_axis=1, til...  7.04 us
    reduce_sum x2, other arithmetic, cloud_model(): ground_precipitation = ground_precipitation + jnp.mean(condensed, axis=0)  6.33 us
  transfers between devices with their start and end apart: 4, of which 3 were waited for; matrix products, arithmetic and copies ran while one was open for 13% of the time, Pallas kernels for 0%

commit v1 on v0

v1 whole, which is shorter than its diff:
```python
import math

import jax
import jax.numpy as jnp
import numpy as np
from jax import lax
from jax.experimental import pallas as pl
from jax.experimental.pallas import tpu as pltpu
from jax.sharding import PartitionSpec as P

NLON = 384
NLAT = 192
MMAX = 128
NSUB = 4
NCRM = 32
LEVELS = 28
BAND = 12
LONS = 96
COLS = BAND * LONS
ROWS = LEVELS * BAND
TARGETS = 64
PER = 18
NL = 16
NS = 4
NC = 4
RUNS = NL * PER
LEV_OWN = LEVELS // NC
SLOTS_OWN = MMAX // NL

F32 = jnp.float32
BF16 = jnp.bfloat16
VMEM = pl.BlockSpec(memory_space=pltpu.VMEM)
SMEM = pl.BlockSpec(memory_space=pltpu.SMEM)


def split2(x):
    hi = x.astype(BF16)
    lo = (x - hi.astype(F32)).astype(BF16)
    return hi, lo


def params(mib=24):
    return pltpu.CompilerParams(vmem_limit_bytes=mib << 20)


def lanes_of(shape):
    return lax.broadcasted_iota(jnp.int32, shape, 1)


def fill_one_hot(order_ref, hot_ref):
    order = order_ref[...]
    step = 96
    for c in range(0, COLS, step):
        ids = lax.broadcasted_iota(jnp.int32, (step, COLS), 0) + c
        hot_ref[c : c + step, :] = jnp.where(ids == order, 1.0, 0.0).astype(BF16)


def pack_kernel(state_ref, force_ref, order_ref, out_ref, hot_ref, cols_ref):
    fill_one_hot(order_ref, hot_ref)
    for ref, base in ((state_ref, 0), (force_ref, LEVELS)):
        rows = ref[...].reshape(LEVELS, BAND, LONS)
        for b in range(BAND):
            cols_ref[base : base + LEVELS, b * LONS : (b + 1) * LONS] = rows[:, b, :]
    hi, lo = split2(cols_ref[...])
    both = jnp.concatenate((hi, lo), axis=0)
    got = jnp.dot(both, hot_ref[...], preferred_element_type=F32)
    got = got[: 2 * LEVELS] + got[2 * LEVELS :]
    lane = lanes_of((8, 128))
    groups = 2 * LEVELS // 8
    for t in range(TARGETS):
        v, off = divmod(t * PER, 128)
        tile = None
        for q in range(groups):
            src = got[q * 8 : q * 8 + 8, v * 128 : v * 128 + 128]
            if off + PER > 128:
                nxt = got[q * 8 : q * 8 + 8, v * 128 + 128 : v * 128 + 256]
                src = jnp.where(lane < off, nxt, src)
            shift = (q * PER - off) % 128
            if shift:
                src = pltpu.roll(src, shift, 1)
            tile = src if tile is None else jnp.where(lane >= q * PER, src, tile)
        out_ref[t] = tile


def gather_lanes(tile_of, q_list, first, count, width, store):
    lane = lanes_of((8, 128))
    for q in q_list:
        for v in range(pl.cdiv(width, 128)):
            acc = None
            for i in range(count):
                start = i * PER - v * 128
                if start >= 128 or start + PER <= 0:
                    continue
                src = tile_of(first + i)
                shift = (i * PER - q * PER) % 128
                if shift:
                    src = pltpu.roll(src, shift, 1)
                acc = src if acc is None else jnp.where(lane >= start, src, acc)
            store(q, v, acc)


def cloud_kernel(got_ref, moist_ref, out_ref, wind_ref, diff_ref, left_ref, right_ref, rain_ref):
    def store_wind(q, v, x):
        wind_ref[q * 8 : q * 8 + 8, v * 128 : v * 128 + 128] = x

    def store_diff(q, v, x):
        diff_ref[q * 8 : q * 8 + 8, v * 128 : v * 128 + 128] = x

    gather_lanes(lambda i: got_ref[i], range(4), 0, NL, RUNS, store_wind)
    cache = {}

    def diff(i):
        if i not in cache:
            cache[i] = got_ref[3 * NL + i] - got_ref[2 * NL + i]
        return cache[i]

    gather_lanes(diff, range(7), 0, NL, RUNS, store_diff)
    courant = 0.4 * jnp.tanh(wind_ref[...])
    mixing = 0.2 + 0.5 * jnp.abs(courant)
    left_ref[...] = mixing - 0.5 * courant
    right_ref[...] = mixing + 0.5 * courant
    rain_ref[...] = jnp.zeros_like(rain_ref)

    def level(k, carry):
        row = (pl.ds(k, 1), slice(0, RUNS))
        gap = diff_ref[row] + moist_ref[k].astype(F32)
        push = diff_ref[pl.ds(k + LEVELS, 1), 0:RUNS] * (1.0 / NSUB)
        ahead = left_ref[row]
        behind = right_ref[row]
        both = ahead + behind
        wet = jnp.maximum(gap, 0.0)
        for _ in range(NSUB - 1):
            up = pltpu.roll(gap, NCRM - 1, 0)
            down = pltpu.roll(gap, 1, 0)
            gap = (jnp.minimum(gap, 0.0) - both * gap) + (ahead * up + behind * down) + push
            wet = wet + jnp.maximum(gap, 0.0)
        rain_ref[pl.ds(k, 1), 0:RUNS] = jnp.sum(wet, axis=0, keepdims=True) * (0.5 / NCRM)
        return carry

    lax.fori_loop(0, LEVELS, level, 0)
    lane = lanes_of((8, 128))
    for i in range(NL):
        v, off = divmod(i * PER, 128)
        tile = None
        for q in range(4):
            src = rain_ref[q * 8 : q * 8 + 8, v * 128 : v * 128 + 128]
            if off + PER > 128:
                nxt = rain_ref[q * 8 : q * 8 + 8, v * 128 + 128 : v * 128 + 256]
                src = jnp.where(lane < off, nxt, src)
            shift = (q * PER - off) % 128
            if shift:
                src = pltpu.roll(src, shift, 1)
            tile = src if tile is None else jnp.where(lane >= q * PER, src, tile)
        for s in range(NS):
            out_ref[s * NL + i] = tile


def update_kernel(got_ref, order_ref, state_ref, force_ref, coef_ref, out_ref, hot_ref, slots_ref, rain_ref):
    fill_one_hot(order_ref, hot_ref)

    def store(q, v, x):
        slots_ref[q * 8 : q * 8 + 8, v * 128 : v * 128 + 128] = x

    gather_lanes(lambda i: got_ref[i], range(4), 0, TARGETS, COLS, store)
    hi, lo = split2(slots_ref[...])
    both = jnp.concatenate((hi, lo), axis=0)
    back = lax.dot_general(both, hot_ref[...], (((1,), (1,)), ((), ())), preferred_element_type=F32)
    back = back[:32] + back[32:]
    for b in range(BAND):
        rain_ref[:, b, :] = back[:LEVELS, b * LONS : (b + 1) * LONS]
    add = coef_ref[0]
    scale = coef_ref[1]
    rain = rain_ref[...].reshape(ROWS, 1, LONS)
    now = state_ref[...]
    out_ref[...] = now + (force_ref[...] + rain * (add + scale * now))


def trig_rows(wave_ref, hi_ref, lo_ref):
    orders = jnp.broadcast_to(wave_ref[...].astype(F32), (MMAX, MMAX)).T
    for v in range(NLON // 128):
        y = lax.broadcasted_iota(jnp.int32, (MMAX, 128), 1).astype(F32) + float(v * 128)
        product = y * orders
        phase = product - NLON * jnp.floor((product + 0.5) * (1.0 / NLON))
        turn = jnp.floor((phase + 48.5) * (1.0 / 96.0))
        x = (phase - 96.0 * turn) * (2.0 * math.pi / NLON)
        z = x * x
        sin = x * (1.0 + z * (-1.0 / 6 + z * (1.0 / 120 + z * (-1.0 / 5040 + z * (1.0 / 362880)))))
        cos = 1.0 + z * (-0.5 + z * (1.0 / 24 + z * (-1.0 / 720 + z * (1.0 / 40320))))
        odd = (turn == 1.0) | (turn == 3.0)
        cos_out = jnp.where(odd, sin, cos)
        sin_out = jnp.where(odd, cos, sin)
        cos_out = jnp.where((turn == 1.0) | (turn == 2.0), -cos_out, cos_out)
        sin_out = jnp.where((turn == 2.0) | (turn == 3.0), -sin_out, sin_out)
        norm = 1.0 / math.sqrt(NLON)
        both = jnp.concatenate(
            (cos_out.reshape(NL, 1, 8, 128), sin_out.reshape(NL, 1, 8, 128)), axis=1
        ).reshape(2 * MMAX, 128)
        hi, lo = split2(both * norm)
        hi_ref[:, v * 128 : v * 128 + 128] = hi
        lo_ref[:, v * 128 : v * 128 + 128] = lo


def table_kernel(wave_ref, own_ref, start_ref, geom_ref, hi_ref, lo_ref, poly_ref):
    trig_rows(wave_ref, hi_ref, lo_ref)
    sub = lax.broadcasted_iota(jnp.int32, (SLOTS_OWN, 128), 0)
    order = jnp.zeros((SLOTS_OWN, 128), F32)
    head = jnp.zeros((SLOTS_OWN, 128), F32)
    for s in range(SLOTS_OWN):
        m = own_ref[s]
        order = jnp.where(sub == s, m.astype(F32), order)
        head = jnp.where(sub == s, start_ref[m], head)
    degree = lax.broadcasted_iota(jnp.int32, (SLOTS_OWN, 128), 1).astype(F32)
    active = degree > order
    numer = jnp.where(active, 4.0 * degree * degree - 1.0, 0.0)
    denom = jnp.where(active, degree * degree - order * order, 1.0)
    grow = jnp.sqrt(numer / denom)
    lower = degree - 1.0
    retreat = jnp.sqrt(
        jnp.maximum(lower * lower - order * order, 0.0) / (4.0 * lower * lower - 1.0)
    )
    retreat = grow * retreat
    begin = jnp.where(degree == order, 1.0, 0.0)
    cosine = geom_ref[0:1, :]
    log_sine = geom_ref[1:2, :]
    weight = geom_ref[2:3, :]
    diagonal = jnp.exp(head[:, 0:1] + order[:, 0:1] * log_sine) * weight
    cosine = jnp.broadcast_to(cosine, (SLOTS_OWN, 256))
    previous = jnp.zeros((SLOTS_OWN, 256), F32)
    current = previous
    for n in range(MMAX):
        fresh = (grow[:, n : n + 1] * cosine) * current + (
            begin[:, n : n + 1] * diagonal - retreat[:, n : n + 1] * previous
        )
        poly_ref[0, n * 8 : n * 8 + 8, :] = fresh[:, :128]
        poly_ref[1, n * 8 : n * 8 + 8, :] = fresh[:, 128:]
        previous, current = current, fresh


def fourier_kernel(got_ref, hi_ref, lo_ref, out_ref, lon_ref):
    width = LEV_OWN * BAND
    rows = got_ref[...].reshape(NC, width, LONS)
    for j in range(NC):
        lon_ref[:, j * LONS : (j + 1) * LONS] = rows[j]
    hi, lo = split2(lon_ref[...])
    dims = (((1,), (1,)), ((), ()))
    out = lax.dot_general(hi_ref[...], hi, dims, preferred_element_type=F32)
    out = out + lax.dot_general(hi_ref[...], lo, dims, preferred_element_type=F32)
    out = out + lax.dot_general(lo_ref[...], hi, dims, preferred_element_type=F32)
    out_ref[...] = out.reshape(NL, 16, width)


def legendre_kernel(got_ref, poly_ref, out_ref, band_ref):
    band_ref[1] = jnp.zeros_like(band_ref[1])
    for k in range(LEV_OWN):
        for i in range(NL):
            h, at = divmod(i * BAND, 128)
            first = min(BAND, 128 - at)
            row = slice(k * 16, k * 16 + 16)
            piece = got_ref[i, :, k * BAND : (k + 1) * BAND]
            band_ref[h, row, at : at + first] = piece[:, :first]
            if first < BAND:
                band_ref[h + 1, row, 0 : BAND - first] = piece[:, first:]
    dims = (((1,), (1,)), ((), ()))
    for s in range(SLOTS_OWN):
        out = None
        for h in range(2):
            hi, lo = split2(band_ref[h, pl.ds(s, 2 * LEV_OWN, stride=8), :])
            whi, wlo = split2(poly_ref[h, pl.ds(s, MMAX, stride=8), :])
            part = lax.dot_general(hi, whi, dims, preferred_element_type=F32)
            part = part + lax.dot_general(hi, wlo, dims, preferred_element_type=F32)
            part = part + lax.dot_general(lo, whi, dims, preferred_element_type=F32)
            out = part if out is None else out + part
        out_ref[:, s, :, :] = out.reshape(LEV_OWN, 2, MMAX)


def diagonal_start():
    return np.array(
        [
            0.5 * (math.lgamma(m + 1.5) - math.lgamma(1.5) - math.lgamma(m + 1.0)) - 0.5 * math.log(2.0)
            for m in range(MMAX)
        ],
        np.float32,
    )


def geometry():
    theta = (np.arange(NLAT) + 0.5) * (math.pi / NLAT)
    sine = np.sin(theta)
    rows = np.stack((np.cos(theta), np.log(sine), sine / math.sqrt(NLAT))).astype(np.float32)
    return np.pad(rows, ((0, 0), (0, 256 - NLAT)))


def call(kernel, out, n_in, scratch=(), specs=None):
    return pl.pallas_call(
        kernel,
        out_shape=out,
        in_specs=specs or [VMEM] * n_in,
        out_specs=jax.tree.map(lambda _: VMEM, out),
        scratch_shapes=list(scratch),
        compiler_params=params(),
    )


def shards(state, forcing, crm_moisture, cloud_order, wave_table):
    shape = jax.ShapeDtypeStruct
    state = state.transpose(0, 2, 3, 1, 4).reshape(ROWS, 1, LONS)
    forcing = forcing.transpose(0, 2, 3, 1, 4).reshape(ROWS, 1, LONS)
    moist = crm_moisture.transpose(0, 2, 3, 4, 1, 5).reshape(LEVELS, NCRM, RUNS)
    order = cloud_order.reshape(1, COLS)
    waves = wave_table.reshape(1, MMAX)
    sec = lax.axis_index("sec")
    lat = lax.axis_index("lat")
    own = lax.dynamic_slice_in_dim(wave_table, lat * SLOTS_OWN, SLOTS_OWN)
    coef = jnp.stack(
        (
            jnp.where(sec == 2, 1.0, jnp.where(sec == 3, -1.0, 0.0)),
            jnp.where(sec < 2, -1.0 / NSUB, 0.0),
        )
    ).astype(F32)

    outgoing = call(
        pack_kernel,
        shape((TARGETS, 8, 128), F32),
        3,
        [pltpu.VMEM((COLS, COLS), BF16), pltpu.VMEM((2 * LEVELS, COLS), F32)],
    )(state, forcing, order)
    arrived = lax.all_to_all(outgoing, ("sec", "lat"), split_axis=0, concat_axis=0, tiled=True)
    trig_hi, trig_lo, poly = call(
        table_kernel,
        (
            shape((2 * MMAX, NLON), BF16),
            shape((2 * MMAX, NLON), BF16),
            shape((2, MMAX * SLOTS_OWN, 128), F32),
        ),
        4,
        specs=[VMEM, SMEM, SMEM, VMEM],
    )(waves, own, jnp.asarray(diagonal_start()), jnp.asarray(geometry()))
    rain = call(
        cloud_kernel,
        shape((TARGETS, 8, 128), F32),
        2,
        [
            pltpu.VMEM((32, 384), F32),
            pltpu.VMEM((56, 384), F32),
            pltpu.VMEM((32, 384), F32),
            pltpu.VMEM((32, 384), F32),
            pltpu.VMEM((32, 384), F32),
        ],
    )(arrived, moist)
    returned = lax.all_to_all(rain, ("sec", "lat"), split_axis=0, concat_axis=0, tiled=True)
    updated = call(
        update_kernel,
        shape((ROWS, 1, LONS), F32),
        5,
        [
            pltpu.VMEM((COLS, COLS), BF16),
            pltpu.VMEM((32, COLS), F32),
            pltpu.VMEM((LEVELS, BAND, LONS), F32),
        ],
        specs=[VMEM, VMEM, VMEM, VMEM, SMEM],
    )(returned, order, state, forcing, coef)
    all_lons = lax.all_to_all(updated, "col", split_axis=0, concat_axis=0, tiled=True)
    fourier = call(
        fourier_kernel,
        shape((NL, 16, LEV_OWN * BAND), F32),
        3,
        [pltpu.VMEM((LEV_OWN * BAND, NLON), F32)],
    )(all_lons, trig_hi, trig_lo)
    bands = lax.all_to_all(fourier, "lat", split_axis=0, concat_axis=0, tiled=True)
    spectral = call(
        legendre_kernel,
        shape((LEV_OWN, SLOTS_OWN, 2, MMAX), F32),
        2,
        [pltpu.VMEM((2, LEV_OWN * 16, 128), F32)],
    )(bands, poly)
    new_state = updated.reshape(1, LEVELS, BAND, 1, LONS).transpose(0, 3, 1, 2, 4)
    return new_state, spectral[None, None]


def solution(mesh):
    placed = (
        P(None, "sec", None, "lat", "col"),
        P(None, "sec", None, "lat", "col"),
        P(None, None, None, ("sec", "lat"), "col", None),
        P("col", "lat", None),
        P(),
    )
    return jax.shard_map(
        shards,
        mesh=mesh,
        in_specs=placed,
        out_specs=(P(None, "sec", None, "lat", "col"), P("sec", None, "col", "lat", None, None)),
        check_vma=False,
    )
```

time: 215 us -> 73.9 us (0.34)
  loops' own time: 82 us -> 0 us
  other arithmetic: 32.1 us -> 0.08 us
  local copies, waits for them, and re-layouts: 34.4 us -> 3.34 us
  blocking collectives: 0 us -> 28.7 us
  between operations: 15.2 us -> 0.71 us
  Pallas kernels: 0 us -> 11.1 us
  matrix products: 8.19 us -> 0 us
  starting transfers between devices: 20 us -> 13.4 us
  waiting for transfers between devices: 21 us -> 16.1 us
    another operation x1 -> x0, loops' own time: 82 us -> none  [legendre_table(): lax.scan(march_forward, (empty, empty), jnp.arange(MMAX, dtype=jnp.int32)...]
    all_to_all x0 -> x2, blocking collectives: none -> 28.7 us  [the longest x1 17.9 us: shards(): lax.all_to_all(outgoing, ('sec', 'lat'), split_axis=0, concat_axis=0, til...]
    slice x34 -> x0, local copies, waits for them, and re-layouts: 13.2 us -> none  [the longest x16 9.64 us: legendre_table(): lax.scan(march_forward, (empty, empty), jnp.arange(MMAX, dtype=jnp.int32)...]
    pallas_call x0 -> x6, Pallas kernels: none -> 11.1 us  [the longest x1 3.66 us: shards(): call(cloud_kernel, shape((TARGETS, 8, 128), F32), 2, [pltpu.VMEM((32, 384...]
    while x112 -> x0, other arithmetic: 9.89 us -> none
    reduce_sum x3 -> x0, other arithmetic: 9.39 us -> none  [the longest x2 6.33 us: cloud_model(): ground_precipitation = ground_precipitation + jnp.mean(condensed, axis=0)]
    dot_general x4 -> x0, matrix products: 8.19 us -> none  [the longest x1 4.34 us: shards(): jnp.einsum('xelc,tpc->txelp', stacked, selector, precision=lax.Precision....]
    all_to_all x3 -> x2, starting transfers between devices: 19.9 us -> 13.4 us  [the longest x1 7.69 us: shards(): lax.all_to_all(updated, 'col', split_axis=0, concat_axis=0, tiled=True)]
  transfers between devices with their start and end apart: 4 -> 2, of which waited for: 3 -> 2; matrix products, arithmetic and copies ran while one was open for 13% -> 0% of each run, Pallas kernels for 0% -> 2%
where the time goes in v1:
time: 73.9 us; the launch traced here: 73.5 us
  blocking collectives  28.7 us (39%)
  waiting for transfers between devices  16.1 us (22%)
  starting transfers between devices  13.4 us (18%)
  Pallas kernels  11.1 us (15%)
  local copies, waits for them, and re-layouts  3.34 us (5%)
    all_to_all x1, blocking collectives, shards(): lax.all_to_all(outgoing, ('sec', 'lat'), split_axis=0, concat_axis=0, til...  17.9 us
    all_to_all x1, blocking collectives, shards(): lax.all_to_all(fourier, 'lat', split_axis=0, concat_axis=0, tiled=True)  10.8 us
    all_to_all x1, waiting for transfers between devices, shards(): lax.all_to_all(rain, ('sec', 'lat'), split_axis=0, concat_axis=0, tiled=T...  8.71 us
    all_to_all x1, starting transfers between devices, shards(): lax.all_to_all(updated, 'col', split_axis=0, concat_axis=0, tiled=True)  7.69 us
    all_to_all x1, waiting for transfers between devices, shards(): lax.all_to_all(updated, 'col', split_axis=0, concat_axis=0, tiled=True)  7.36 us
    all_to_all x1, starting transfers between devices, shards(): lax.all_to_all(rain, ('sec', 'lat'), split_axis=0, concat_axis=0, tiled=T...  5.76 us
    pallas_call x1, Pallas kernels, shards(): call(cloud_kernel, shape((TARGETS, 8, 128), F32), 2, [pltpu.VMEM((32, 384...  3.66 us
    unnamed x20, local copies, waits for them, and re-layouts  3.26 us
  transfers between devices with their start and end apart: 2, of which 2 were waited for; matrix products, arithmetic and copies ran while one was open for 0% of the time, Pallas kernels for 2%

profile of v1, /device:TPU:2, one launch (start us, length us, event | category | flops | bytes accessed | tf_op | source)
XLA Modules:
  0.0 73.5 jit_solution(8191662742621669990)
XLA Ops:
  0.6 0.0 copy-start
  0.6 0.0 copy-start.1
  0.7 1.0 %copy-done.1 = f32[1,1,28,12,96]{4,1,3,2,0:T(1,128)S(1)} copy-done((f32[1,1,28,12,96]{4,1,3,2,0:T(1,128)S(1)}, f32[1,1,28,12,96]{4,1,3,2,0:T(1,128)}, u32[]{:S(2)}) %copy-start.1) | copy-done | bytes 129048
  1.6 0.0 copy-start.3
  1.6 0.9 %copy-done.3 = f32[1,1,28,12,96]{4,1,3,2,0:T(1,128)S(1)} copy-done((f32[1,1,28,12,96]{4,1,3,2,0:T(1,128)S(1)}, f32[1,1,28,12,96]{4,1,3,2,0:T(1,128)}, u32[]{:S(2)}) %copy-start.3) | copy-done | bytes 129048
  2.5 0.0 copy-start.5
  2.5 0.7 copy-done.5
  3.2 1.1 %shard_map.86 = f32[64,8,128]{2,1,0:T(8,128)S(1)} custom-call(f32[336,1,96]{2,1,0:T(1,128)S(1)} %bitcast.16, f32[336,1,96]{2,1,0:T(1,128)S(1)} %bitcast.18, s32[1,1152]{1,0:T(1,128)S(1)} %bitcast.20), custom_call_target="tpu_custom_call" | custom-call | tf_op jit(solution)/shard_map/pallas_call | solution.py:321
  4.3 17.9 %all_to_all.20.got_ref = f32[64,8,128]{2,1,0:T(8,128)S(1)} all-to-all(f32[64,8,128]{2,1,0:T(8,128)S(1)} %shard_map.86), channel_id=1, replica_groups=mesh['sec'=4,'lat'=16,'col'=4] {'sec','lat'}, dimensions={0} | all-to-all | bytes 524288 | tf_op jit(solution)/shard_map/all_to_all | solution.py:327
  22.2 0.0 copy-done
  22.2 3.7 %shard_map.87 = f32[64,8,128]{2,1,0:T(8,128)} custom-call(f32[64,8,128]{2,1,0:T(8,128)S(1)} %all_to_all.20.got_ref, bf16[28,32,288]{2,1,0:T(8,128)(2,1)S(1)} %bitcast.15), custom_call_target="tpu_custom_call" | custom-call | tf_op jit(solution)/shard_map/pallas_call | solution.py:338
  25.9 0.0 copy-start.2
  25.9 0.0 copy-start.4
  25.9 5.8 %all-to-all-start.1 = ((f32[64,8,128]{2,1,0:T(8,128)}), f32[64,8,128]{2,1,0:T(8,128)S(1)}, u32[]{:S(2)}, u32[]{:S(2)}) async-start(f32[64,8,128]{2,1,0:T(8,128)} %shard_map.87), calls=%async_computation.1 | async-start | bytes 524288 | tf_op jit(solution)/shard_map/all_to_all | solution.py:350
  31.7 0.0 copy-start.6
  31.7 0.1 pad_maximum_fusion.coef_ref
  31.8 8.7 %all-to-all-done.1.got_ref = f32[64,8,128]{2,1,0:T(8,128)S(1)} async-done(((f32[64,8,128]{2,1,0:T(8,128)}), f32[64,8,128]{2,1,0:T(8,128)S(1)}, u32[]{:S(2)}, u32[]{:S(2)}) %all-to-all-start.1) | async-done | bytes 262176 | tf_op jit(solution)/shard_map/all_to_all | solution.py:350
  40.5 0.0 copy-done.2
  40.5 0.0 copy-done.4
  40.5 0.0 copy-done.6
  40.5 2.7 %shard_map.88 = f32[336,1,96]{2,1,0:T(1,128)} custom-call(f32[64,8,128]{2,1,0:T(8,128)S(1)} %all-to-all-done.1.got_ref, s32[1,1152]{1,0:T(1,128)S(1)} %bitcast.21, f32[336,1,96]{2,1,0:T(1,128)S(1)} %bitcast.17, f32[336,1,96]{2,1,0:T(1,128)S(1)} %bitcast.19, f32[2]{0:T(128)S(1)} %pad_maximum_fusion.coef_ref), custom_call_target="tpu_custom_call" | custom-call | tf_op jit(solution)/shard_map/pallas_call | solution.py:351
  43.2 0.0 copy-start.8
  43.2 7.7 %all-to-all-start.2 = ((f32[336,1,96]{2,1,0:T(1,128)}), f32[336,1,96]{2,1,0:T(1,128)S(1)}, u32[]{:S(2)}, u32[]{:S(2)}) async-start(f32[336,1,96]{2,1,0:T(1,128)} %shard_map.88), calls=%async_computation.2 | async-start | bytes 344064 | tf_op jit(solution)/shard_map/all_to_all | solution.py:362
  50.9 0.0 copy-done.8
  50.9 0.1 dynamic_slice.3.own_ref
  50.9 0.6 copy-done.7
  51.5 0.0 copy-done.9
  51.6 1.5 %shard_map.89 = (bf16[256,384]{1,0:T(8,128)(2,1)S(1)}, bf16[256,384]{1,0:T(8,128)(2,1)S(1)}, f32[2,1024,128]{2,1,0:T(8,128)S(1)}) custom-call(s32[1,128]{1,0:T(1,128)S(1)} %bitcast.22, s32[8]{0:T(128)S(1)} %dynamic_slice.3.own_ref, f32[128]{0:T(128)S(1)} %copy-done.9, f32[3,256]{1,0:T(4,128)S(1)} %copy-done.7), custom_call_target="tpu_custom_call" | custom-call | tf_op jit(solution)/shard_map/pallas_call | solution.py:328
  53.1 7.4 %all-to-all-done.2.got_ref = f32[336,1,96]{2,1,0:T(1,128)S(1)} async-done(((f32[336,1,96]{2,1,0:T(1,128)}), f32[336,1,96]{2,1,0:T(1,128)S(1)}, u32[]{:S(2)}, u32[]{:S(2)}) %all-to-all-start.2) | async-done | bytes 129056 | tf_op jit(solution)/shard_map/all_to_all | solution.py:362
  60.5 0.5 shard_map.90
  60.9 10.8 %all_to_all.21.got_ref = f32[16,16,84]{2,1,0:T(8,128)S(1)} all-to-all(f32[16,16,84]{2,1,0:T(8,128)S(1)} %shard_map.90), channel_id=1, replica_groups=mesh['sec'=4,'lat'=16,'col'=4] {'lat'}, dimensions={0} | all-to-all | bytes 172032 | tf_op jit(solution)/shard_map/all_to_all | solution.py:369
  71.8 1.7 %shard_map.91 = f32[7,8,2,128]{3,2,1,0:T(2,128)} custom-call(f32[16,16,84]{2,1,0:T(8,128)S(1)} %all_to_all.21.got_ref, f32[2,1024,128]{2,1,0:T(8,128)S(1)} %get-tuple-element.7.poly_ref), custom_call_target="tpu_custom_call" | custom-call | tf_op jit(solution)/shard_map/pallas_call | solution.py:370
  (2 shorter events, 0.0 us)
Async XLA Ops:
  0.6 21.6 %copy-start = (bf16[1,32,28,1,1,288]{5,1,4,3,2,0:T(8,128)(2,1)S(1)}, bf16[1,32,28,1,1,288]{5,1,4,3,2,0:T(8,128)(2,1)}, u32[]{:S(2)}) copy-start(bf16[1,32,28,1,1,288]{5,1,4,3,2,0:T(8,128)(2,1)} %param.9) | copy-start | bytes 1548292
  0.6 1.0 %copy-start.1 = (f32[1,1,28,12,96]{4,1,3,2,0:T(1,128)S(1)}, f32[1,1,28,12,96]{4,1,3,2,0:T(1,128)}, u32[]{:S(2)}) copy-start(f32[1,1,28,12,96]{4,1,3,2,0:T(1,128)} %param.7) | copy-start | bytes 387076
  1.6 0.9 %copy-start.3 = (f32[1,1,28,12,96]{4,1,3,2,0:T(1,128)S(1)}, f32[1,1,28,12,96]{4,1,3,2,0:T(1,128)}, u32[]{:S(2)}) copy-start(f32[1,1,28,12,96]{4,1,3,2,0:T(1,128)} %param.8) | copy-start | bytes 387076
  2.5 0.7 copy-start.5
  25.9 14.6 %copy-start.2 = (f32[1,1,28,12,96]{4,1,3,2,0:T(1,128)S(1)}, f32[1,1,28,12,96]{4,1,3,2,0:T(1,128)}, u32[]{:S(2)}) copy-start(f32[1,1,28,12,96]{4,1,3,2,0:T(1,128)} %param.7) | copy-start | bytes 387076
  25.9 14.6 %copy-start.4 = (f32[1,1,28,12,96]{4,1,3,2,0:T(1,128)S(1)}, f32[1,1,28,12,96]{4,1,3,2,0:T(1,128)}, u32[]{:S(2)}) copy-start(f32[1,1,28,12,96]{4,1,3,2,0:T(1,128)} %param.8) | copy-start | bytes 387076
  25.9 14.6 %all-to-all-start.1 = ((f32[64,8,128]{2,1,0:T(8,128)}), f32[64,8,128]{2,1,0:T(8,128)S(1)}, u32[]{:S(2)}, u32[]{:S(2)}) async-start(f32[64,8,128]{2,1,0:T(8,128)} %shard_map.87), calls=%async_computation.1 | async-start | bytes 524288 | tf_op jit(solution)/shard_map/all_to_all | solution.py:350
  31.7 8.8 %copy-start.6 = (s32[1,1,1152]{2,1,0:T(1,128)S(1)}, s32[1,1,1152]{2,1,0:T(1,128)}, u32[]{:S(2)}) copy-start(s32[1,1,1152]{2,1,0:T(1,128)} %param.10) | copy-start | bytes 13828
  43.2 7.7 %copy-start.8 = (s32[128]{0:T(128)S(1)}, s32[128]{0:T(128)}, u32[]{:S(2)}) copy-start(s32[128]{0:T(128)} %param.11) | copy-start | bytes 1540
  43.2 17.3 %all-to-all-start.2 = ((f32[336,1,96]{2,1,0:T(1,128)}), f32[336,1,96]{2,1,0:T(1,128)S(1)}, u32[]{:S(2)}, u32[]{:S(2)}) async-start(f32[336,1,96]{2,1,0:T(1,128)} %shard_map.88), calls=%async_computation.2 | async-start | bytes 344064 | tf_op jit(solution)/shard_map/all_to_all | solution.py:362
  50.9 0.7 copy-start.7
  50.9 0.7 copy-start.9

commit v2 on v1

v2 whole, which is shorter than its diff:
```python
import math

import jax
import jax.numpy as jnp
import numpy as np
from jax import lax
from jax.experimental import pallas as pl
from jax.experimental.pallas import tpu as pltpu
from jax.sharding import PartitionSpec as P

NLON = 384
NLAT = 192
MMAX = 128
NSUB = 4
NCRM = 32
LEVELS = 28
BAND = 12
LONS = 96
COLS = BAND * LONS
ROWS = LEVELS * BAND
TARGETS = 64
PER = 18
NL = 16
NS = 4
NC = 4
RUNS = NL * PER
HALF = 4 * PER
LEV_OWN = LEVELS // NC
SLOTS_OWN = MMAX // NL

F32 = jnp.float32
BF16 = jnp.bfloat16
VMEM = pl.BlockSpec(memory_space=pltpu.VMEM)
HBM = pl.BlockSpec(memory_space=pltpu.HBM)


def split2(x):
    hi = x.astype(BF16)
    lo = (x - hi.astype(F32)).astype(BF16)
    return hi, lo


def params(mib=24):
    return pltpu.CompilerParams(vmem_limit_bytes=mib << 20)


def lanes_of(shape):
    return lax.broadcasted_iota(jnp.int32, shape, 1)


def fill_one_hot(order_ref, hot_ref):
    order = order_ref[...]
    step = 96
    for c in range(0, COLS, step):
        ids = lax.broadcasted_iota(jnp.int32, (step, COLS), 0) + c
        hot_ref[c : c + step, :] = jnp.where(ids == order, 1.0, 0.0).astype(BF16)


def trig_rows(orders, hi_ref, lo_ref):
    first = (lax.axis_index("col") * LONS).astype(F32)
    y = lax.broadcasted_iota(jnp.int32, (MMAX, 128), 1).astype(F32) + first
    product = y * orders
    phase = product - NLON * jnp.floor((product + 0.5) * (1.0 / NLON))
    turn = jnp.floor((phase + 48.5) * (1.0 / 96.0))
    x = (phase - 96.0 * turn) * (2.0 * math.pi / NLON)
    z = x * x
    sin = x * (1.0 + z * (-1.0 / 6 + z * (1.0 / 120 + z * (-1.0 / 5040 + z * (1.0 / 362880)))))
    cos = 1.0 + z * (-0.5 + z * (1.0 / 24 + z * (-1.0 / 720 + z * (1.0 / 40320))))
    odd = (turn == 1.0) | (turn == 3.0)
    cos_out = jnp.where(odd, sin, cos)
    sin_out = jnp.where(odd, cos, sin)
    cos_out = jnp.where((turn == 1.0) | (turn == 2.0), -cos_out, cos_out)
    sin_out = jnp.where((turn == 2.0) | (turn == 3.0), -sin_out, sin_out)
    norm = 1.0 / math.sqrt(NLON)
    both = jnp.concatenate(
        (cos_out.reshape(NL, 1, 8, 128), sin_out.reshape(NL, 1, 8, 128)), axis=1
    ).reshape(2 * MMAX, 128)
    hi, lo = split2(both * norm)
    hi_ref[...] = hi
    lo_ref[...] = lo


def legendre_rows(order, geom_ref, poly_ref):
    lane = lanes_of((SLOTS_OWN, 128)).astype(F32)
    head = jnp.sum(jnp.where(lane == order, geom_ref[3:4, 0:128], 0.0), axis=1, keepdims=True)
    degree = lax.broadcasted_iota(jnp.int32, (SLOTS_OWN, 128), 1).astype(F32)
    active = degree > order
    numer = jnp.where(active, 4.0 * degree * degree - 1.0, 0.0)
    denom = jnp.where(active, degree * degree - order * order, 1.0)
    grow = jnp.sqrt(numer / denom)
    lower = degree - 1.0
    retreat = jnp.sqrt(
        jnp.maximum(lower * lower - order * order, 0.0) / (4.0 * lower * lower - 1.0)
    )
    retreat = grow * retreat
    begin = jnp.where(degree == order, 1.0, 0.0)
    diagonal = jnp.exp(head + order[:, 0:1] * geom_ref[1:2, :]) * geom_ref[2:3, :]
    cosine = jnp.broadcast_to(geom_ref[0:1, :], (SLOTS_OWN, 256))
    previous = jnp.zeros((SLOTS_OWN, 256), F32)
    current = previous
    for n in range(MMAX):
        fresh = (grow[:, n : n + 1] * cosine) * current + (
            begin[:, n : n + 1] * diagonal - retreat[:, n : n + 1] * previous
        )
        poly_ref[0, n * 8 : n * 8 + 8, :] = fresh[:, :128]
        poly_ref[1, n * 8 : n * 8 + 8, :] = fresh[:, 128:]
        previous, current = current, fresh


def pack_kernel(
    state_hbm,
    force_hbm,
    order_hbm,
    wave_hbm,
    geom_hbm,
    moist_hbm,
    out_ref,
    hot_ref,
    cols_ref,
    hi_ref,
    lo_ref,
    poly_ref,
    moist_ref,
    state_ref,
    force_ref,
    order_ref,
    wave_ref,
    geom_ref,
    orders_ref,
    sems,
):
    loads = [
        pltpu.make_async_copy(src, dst, sems.at[n])
        for n, (src, dst) in enumerate(
            (
                (wave_hbm, wave_ref),
                (geom_hbm, geom_ref),
                (order_hbm, order_ref),
                (state_hbm, state_ref),
                (force_hbm, force_ref),
                (moist_hbm, moist_ref),
            )
        )
    ]
    for load in loads:
        load.start()
    loads[0].wait()
    orders = jnp.broadcast_to(wave_ref[...].astype(F32), (MMAX, MMAX)).T
    orders_ref[...] = orders
    trig_rows(orders, hi_ref, lo_ref)
    loads[1].wait()
    first = pl.multiple_of(lax.axis_index("lat") * SLOTS_OWN, SLOTS_OWN)
    legendre_rows(orders_ref[pl.ds(first, SLOTS_OWN), :], geom_ref, poly_ref)
    loads[2].wait()
    fill_one_hot(order_ref, hot_ref)
    loads[3].wait()
    loads[4].wait()
    for ref, base in ((state_ref, 0), (force_ref, LEVELS)):
        rows = ref[...].reshape(LEVELS, BAND, LONS)
        for b in range(BAND):
            cols_ref[base : base + LEVELS, b * LONS : (b + 1) * LONS] = rows[:, b, :]
    hi, lo = split2(cols_ref[...])
    both = jnp.concatenate((hi, lo), axis=0)
    got = jnp.dot(both, hot_ref[...], preferred_element_type=F32)
    got = got[: 2 * LEVELS] + got[2 * LEVELS :]
    lane = lanes_of((8, 128))
    groups = 2 * LEVELS // 8
    for t in range(TARGETS):
        v, off = divmod(t * PER, 128)
        tile = None
        for q in range(groups):
            src = got[q * 8 : q * 8 + 8, v * 128 : v * 128 + 128]
            if off + PER > 128:
                nxt = got[q * 8 : q * 8 + 8, v * 128 + 128 : v * 128 + 256]
                src = jnp.where(lane < off, nxt, src)
            shift = (q * PER - off) % 128
            if shift:
                src = pltpu.roll(src, shift, 1)
            tile = src if tile is None else jnp.where(lane >= q * PER, src, tile)
        out_ref[t] = tile
    loads[5].wait()


def gather_lanes(tile_of, q_list, first, count, width, store):
    lane = lanes_of((8, 128))
    for q in q_list:
        for v in range(pl.cdiv(width, 128)):
            acc = None
            for i in range(count):
                start = i * PER - v * 128
                if start >= 128 or start + PER <= 0:
                    continue
                src = tile_of(first + i)
                shift = (i * PER - q * PER) % 128
                if shift:
                    src = pltpu.roll(src, shift, 1)
                acc = src if acc is None else jnp.where(lane >= start, src, acc)
            store(q, v, acc)


def cloud_kernel(got_ref, moist_ref, out_ref, wind_ref, diff_ref, left_ref, right_ref, rain_ref):
    def store_wind(q, v, x):
        wind_ref[q * 8 : q * 8 + 8, v * 128 : v * 128 + 128] = x

    def store_diff(q, v, x):
        diff_ref[q * 8 : q * 8 + 8, v * 128 : v * 128 + 128] = x

    gather_lanes(lambda i: got_ref[i], range(4), 0, NL, RUNS, store_wind)
    cache = {}

    def diff(i):
        if i not in cache:
            cache[i] = got_ref[3 * NL + i] - got_ref[2 * NL + i]
        return cache[i]

    gather_lanes(diff, range(7), 0, NL, RUNS, store_diff)
    courant = 0.4 * jnp.tanh(wind_ref[...])
    mixing = 0.2 + 0.5 * jnp.abs(courant)
    left_ref[...] = mixing - 0.5 * courant
    right_ref[...] = mixing + 0.5 * courant
    rain_ref[...] = jnp.zeros_like(rain_ref)

    def level(k, carry):
        row = (pl.ds(k, 1), slice(0, RUNS))
        gap = diff_ref[row] + moist_ref[k].astype(F32)
        push = diff_ref[pl.ds(k + LEVELS, 1), 0:RUNS] * (1.0 / NSUB)
        ahead = left_ref[row]
        behind = right_ref[row]
        both = ahead + behind
        wet = jnp.maximum(gap, 0.0)
        for _ in range(NSUB - 1):
            up = pltpu.roll(gap, NCRM - 1, 0)
            down = pltpu.roll(gap, 1, 0)
            gap = (jnp.minimum(gap, 0.0) - both * gap) + (ahead * up + behind * down) + push
            wet = wet + jnp.maximum(gap, 0.0)
        rain_ref[pl.ds(k, 1), 0:RUNS] = jnp.sum(wet, axis=0, keepdims=True) * (0.5 / NCRM)
        return carry

    lax.fori_loop(0, LEVELS, level, 0)
    lane = lanes_of((8, 128))
    for i in range(NL):
        v, off = divmod(i * PER, 128)
        tile = None
        for q in range(4):
            src = rain_ref[q * 8 : q * 8 + 8, v * 128 : v * 128 + 128]
            if off + PER > 128:
                nxt = rain_ref[q * 8 : q * 8 + 8, v * 128 + 128 : v * 128 + 256]
                src = jnp.where(lane < off, nxt, src)
            shift = (q * PER - off) % 128
            if shift:
                src = pltpu.roll(src, shift, 1)
            tile = src if tile is None else jnp.where(lane >= q * PER, src, tile)
        low = tile[0:4]
        high = pltpu.roll(tile, HALF, 1)[4:8]
        tile = jnp.where(lane[0:4] < HALF, low, high)
        for s in range(NS):
            out_ref[s * NL + i] = tile


def update_kernel(got_ref, hot_ref, cols_ref, hi_ref, lo_ref, out_ref, four_ref, slots_ref, rows_ref):
    def store(q, v, x):
        slots_ref[q * 8 : q * 8 + 8, v * 128 : v * 128 + 128] = x

    cache = {}

    def tile_of(t):
        if t not in cache:
            tile = got_ref[t]
            cache[t] = jnp.concatenate((tile, pltpu.roll(tile, 128 - HALF, 1)), axis=0)
        return cache[t]

    gather_lanes(tile_of, range(4), 0, TARGETS, COLS, store)
    hi, lo = split2(slots_ref[...])
    both = jnp.concatenate((hi, lo), axis=0)
    back = lax.dot_general(both, hot_ref[...], (((1,), (1,)), ((), ())), preferred_element_type=F32)
    rain = back[:LEVELS] + back[32 : 32 + LEVELS]
    sec = lax.axis_index("sec")
    add = jnp.where(sec == 2, 1.0, jnp.where(sec == 3, -1.0, 0.0)).astype(F32)
    scale = jnp.where(sec < 2, -1.0 / NSUB, 0.0).astype(F32)
    now = cols_ref[0:LEVELS]
    now = now + (cols_ref[LEVELS : 2 * LEVELS] + rain * (add + scale * now))
    blank = jnp.zeros((LEVELS, 128 - LONS), F32)
    for b in range(BAND):
        piece = jnp.concatenate((now[:, b * LONS : (b + 1) * LONS], blank), axis=1)
        rows_ref[pl.ds(b, LEVELS, stride=BAND), :] = piece
    rows = rows_ref[...]
    out_ref[...] = rows[:, :LONS].reshape(ROWS, 1, LONS)
    xhi, xlo = split2(rows)
    dims = (((1,), (1,)), ((), ()))
    out = lax.dot_general(hi_ref[...], xhi, dims, preferred_element_type=F32)
    out = out + lax.dot_general(hi_ref[...], xlo, dims, preferred_element_type=F32)
    out = out + lax.dot_general(lo_ref[...], xhi, dims, preferred_element_type=F32)
    width = LEV_OWN * BAND
    for j in range(NC):
        part = out[:, j * width : (j + 1) * width].reshape(NL, 16, width)
        for i in range(NL):
            four_ref[i * NC + j] = part[i]


def legendre_kernel(got_ref, poly_ref, out_ref, band_ref):
    band_ref[1] = jnp.zeros_like(band_ref[1])
    bands = [
        (got_ref[i * NC] + got_ref[i * NC + 1]) + (got_ref[i * NC + 2] + got_ref[i * NC + 3])
        for i in range(NL)
    ]
    for k in range(LEV_OWN):
        for i in range(NL):
            h, at = divmod(i * BAND, 128)
            first = min(BAND, 128 - at)
            row = slice(k * 16, k * 16 + 16)
            piece = bands[i][:, k * BAND : (k + 1) * BAND]
            band_ref[h, row, at : at + first] = piece[:, :first]
            if first < BAND:
                band_ref[h + 1, row, 0 : BAND - first] = piece[:, first:]
    dims = (((1,), (1,)), ((), ()))
    for s in range(SLOTS_OWN):
        out = None
        for h in range(2):
            hi, lo = split2(band_ref[h, pl.ds(s, 2 * LEV_OWN, stride=8), :])
            whi, wlo = split2(poly_ref[h, pl.ds(s, MMAX, stride=8), :])
            part = lax.dot_general(hi, whi, dims, preferred_element_type=F32)
            part = part + lax.dot_general(hi, wlo, dims, preferred_element_type=F32)
            part = part + lax.dot_general(lo, whi, dims, preferred_element_type=F32)
            out = part if out is None else out + part
        out_ref[:, s, :, :] = out.reshape(LEV_OWN, 2, MMAX)


def geometry():
    theta = (np.arange(NLAT) + 0.5) * (math.pi / NLAT)
    sine = np.sin(theta)
    rows = np.zeros((4, 256))
    rows[0, :NLAT] = np.cos(theta)
    rows[1, :NLAT] = np.log(sine)
    rows[2, :NLAT] = sine / math.sqrt(NLAT)
    for m in range(MMAX):
        logs = math.lgamma(m + 1.5) - math.lgamma(1.5) - math.lgamma(m + 1.0)
        rows[3, m] = 0.5 * logs - 0.5 * math.log(2.0)
    return rows.astype(np.float32)


def call(kernel, out, specs, scratch=()):
    return pl.pallas_call(
        kernel,
        out_shape=out,
        in_specs=specs,
        out_specs=jax.tree.map(lambda _: VMEM, out),
        scratch_shapes=list(scratch),
        compiler_params=params(),
    )


def stay(x):
    return pltpu.with_memory_space_constraint(x, pltpu.HBM)


def shards(state, forcing, crm_moisture, cloud_order, wave_table):
    shape = jax.ShapeDtypeStruct
    state = state.transpose(0, 2, 3, 1, 4).reshape(ROWS, 1, LONS)
    forcing = forcing.transpose(0, 2, 3, 1, 4).reshape(ROWS, 1, LONS)
    moist = crm_moisture.transpose(0, 2, 3, 4, 1, 5).reshape(LEVELS, NCRM, RUNS)
    order = cloud_order.reshape(1, COLS)
    waves = wave_table.reshape(1, MMAX)
    outgoing, hot, cols, trig_hi, trig_lo, poly, moist = call(
        pack_kernel,
        (
            shape((TARGETS, 8, 128), F32),
            shape((COLS, COLS), BF16),
            shape((2 * LEVELS, COLS), F32),
            shape((2 * MMAX, 128), BF16),
            shape((2 * MMAX, 128), BF16),
            shape((2, MMAX * SLOTS_OWN, 128), F32),
            shape((LEVELS, NCRM, RUNS), BF16),
        ),
        [HBM] * 6,
        [
            pltpu.VMEM((ROWS, 1, LONS), F32),
            pltpu.VMEM((ROWS, 1, LONS), F32),
            pltpu.VMEM((1, COLS), jnp.int32),
            pltpu.VMEM((1, MMAX), jnp.int32),
            pltpu.VMEM((4, 256), F32),
            pltpu.VMEM((MMAX, 128), F32),
            pltpu.SemaphoreType.DMA((6,)),
        ],
    )(*(stay(x) for x in (state, forcing, order, waves, jnp.asarray(geometry()), moist)))
    arrived = lax.all_to_all(outgoing, ("sec", "lat"), split_axis=0, concat_axis=0, tiled=True)
    rain = call(
        cloud_kernel,
        shape((TARGETS, 4, 128), F32),
        [VMEM, VMEM],
        [
            pltpu.VMEM((32, 384), F32),
            pltpu.VMEM((56, 384), F32),
            pltpu.VMEM((32, 384), F32),
            pltpu.VMEM((32, 384), F32),
            pltpu.VMEM((32, 384), F32),
        ],
    )(arrived, moist)
    returned = lax.all_to_all(rain, ("sec", "lat"), split_axis=0, concat_axis=0, tiled=True)
    updated, fourier = call(
        update_kernel,
        (shape((ROWS, 1, LONS), F32), shape((NL * NC, 16, LEV_OWN * BAND), F32)),
        [VMEM] * 5,
        [pltpu.VMEM((32, COLS), F32), pltpu.VMEM((ROWS, 128), F32)],
    )(returned, hot, cols, trig_hi, trig_lo)
    bands = lax.all_to_all(fourier, ("lat", "col"), split_axis=0, concat_axis=0, tiled=True)
    spectral = call(
        legendre_kernel,
        shape((LEV_OWN, SLOTS_OWN, 2, MMAX), F32),
        [VMEM] * 2,
        [pltpu.VMEM((2, LEV_OWN * 16, 128), F32)],
    )(bands, poly)
    new_state = updated.reshape(1, LEVELS, BAND, 1, LONS).transpose(0, 3, 1, 2, 4)
    return new_state, spectral[None, None]


def solution(mesh):
    placed = (
        P(None, "sec", None, "lat", "col"),
        P(None, "sec", None, "lat", "col"),
        P(None, None, None, ("sec", "lat"), "col", None),
        P("col", "lat", None),
        P(),
    )
    return jax.shard_map(
        shards,
        mesh=mesh,
        in_specs=placed,
        out_specs=(P(None, "sec", None, "lat", "col"), P("sec", None, "col", "lat", None, None)),
        check_vma=False,
    )
```

time: 73.9 us -> 72.3 us (0.978)
  blocking collectives: 28.7 us -> 60.8 us
  waiting for transfers between devices: 16.1 us -> 0 us
  starting transfers between devices: 13.4 us -> 0 us
  local copies, waits for them, and re-layouts: 3.34 us -> 0 us
  Pallas kernels: 11.1 us -> 10.2 us
    all_to_all x1 -> x2, blocking collectives: 10.8 us -> 42.9 us  [the longest x1 30.3 us: shards(): lax.all_to_all(fourier, ('lat', 'col'), split_axis=0, concat_axis=0, tile...]
    all_to_all x2 -> x0, waiting for transfers between devices: 16.1 us -> none  [the longest x1 8.71 us: shards(): lax.all_to_all(rain, ('sec', 'lat'), split_axis=0, concat_axis=0, tiled=T...]
    all_to_all x2 -> x0, starting transfers between devices: 13.4 us -> none  [the longest x1 7.69 us: shards(): lax.all_to_all(updated, 'col', split_axis=0, concat_axis=0, tiled=True)]
    unnamed x20 -> x0, local copies, waits for them, and re-layouts: 3.26 us -> none
    pallas_call x6 -> x4, Pallas kernels: 11.1 us -> 10.2 us  [the longest x1 3.05 us: shards(): call(pack_kernel, (shape((TARGETS, 8, 128), F32), shape((COLS, COLS), BF1...]
  transfers between devices with their start and end apart: 2 -> 0, of which waited for: 2 -> 0; matrix products, arithmetic and copies ran while one was open for 0% -> 0% of each run, Pallas kernels for 2% -> 0%
where the time goes in v2:
time: 72.3 us; the launch traced here: 71.7 us
  blocking collectives  60.8 us (84%)
  Pallas kernels  10.2 us (14%)
    all_to_all x1, blocking collectives, shards(): lax.all_to_all(fourier, ('lat', 'col'), split_axis=0, concat_axis=0, tile...  30.3 us
    all_to_all x1, blocking collectives, shards(): lax.all_to_all(outgoing, ('sec', 'lat'), split_axis=0, concat_axis=0, til...  17.9 us
    all_to_all x1, blocking collectives, shards(): lax.all_to_all(rain, ('sec', 'lat'), split_axis=0, concat_axis=0, tiled=T...  12.6 us
    pallas_call x1, Pallas kernels, shards(): call(pack_kernel, (shape((TARGETS, 8, 128), F32), shape((COLS, COLS), BF1...  3.05 us
    pallas_call x1, Pallas kernels, shards(): call(cloud_kernel, shape((TARGETS, 4, 128), F32), [VMEM, VMEM], [pltpu.VM...  3.02 us
    pallas_call x1, Pallas kernels, shards(): call(update_kernel, (shape((ROWS, 1, LONS), F32), shape((NL * NC, 16, LEV...  2.39 us
    pallas_call x1, Pallas kernels, shards(): call(legendre_kernel, shape((LEV_OWN, SLOTS_OWN, 2, MMAX), F32), [VMEM] *...  1.75 us

profile of v2, /device:TPU:2, one launch (start us, length us, event | category | flops | bytes accessed | tf_op | source)
XLA Modules:
  0.0 71.7 jit_solution(11980940425546929986)
XLA Ops:
  0.6 3.1 %shard_map.77 = (f32[64,8,128]{2,1,0:T(8,128)S(1)}, bf16[1152,1152]{1,0:T(8,128)(2,1)S(1)}, f32[56,1152]{1,0:T(8,128)S(1)}, bf16[256,128]{1,0:T(8,128)(2,1)S(1)}...) custom-call(f32[336,1,96]{2,1,0:T(1,128)} %bitcast.14, ...), custom_call_target="tpu_custom_call" | custom-call | tf_op jit(solution)/shard_map/pallas_call | solution.py:363
  3.7 17.9 %all_to_all.15.got_ref = f32[64,8,128]{2,1,0:T(8,128)S(1)} all-to-all(f32[64,8,128]{2,1,0:T(8,128)S(1)} %get-tuple-element.11), channel_id=1, replica_groups=mesh['sec'=4,'lat'=16,'col'=4] {'sec','lat'}, dimensions={0} | all-to-all | bytes 524288 | tf_op jit(solution)/shard_map/all_to_all | solution.py:385
  21.6 3.0 %shard_map.78 = f32[64,4,128]{2,1,0:T(4,128)S(1)} custom-call(f32[64,8,128]{2,1,0:T(8,128)S(1)} %all_to_all.15.got_ref, bf16[28,32,288]{2,1,0:T(8,128)(2,1)S(1)} %get-tuple-element.12.moist_ref), custom_call_target="tpu_custom_call" | custom-call | tf_op jit(solution)/shard_map/pallas_call | solution.py:386
  24.6 12.6 %all_to_all.16.got_ref = f32[64,4,128]{2,1,0:T(4,128)S(1)} all-to-all(f32[64,4,128]{2,1,0:T(4,128)S(1)} %shard_map.78), channel_id=1, replica_groups=mesh['sec'=4,'lat'=16,'col'=4] {'sec','lat'}, dimensions={0} | all-to-all | bytes 262144 | tf_op jit(solution)/shard_map/all_to_all | solution.py:398
  37.2 2.4 %shard_map.79 = (f32[336,1,96]{2,1,0:T(1,128)}, f32[64,16,84]{2,1,0:T(8,128)S(1)}) custom-call(f32[64,4,128]{2,1,0:T(4,128)S(1)} %all_to_all.16.got_ref, bf16[1152,1152]{1,0:T(8,128)(2,1)S(1)} %get-tuple-element.13.hot_ref, f32[56,1152]{1,0:T(8,128)S(1)} %get-tuple-element.14.cols_ref, bf16[256,128]{1,0:T(8,128)(2,1)S(1)} %get-tuple-element.15.hi_ref, ...), custom_call_target="tpu_custom_call" | custom-call | tf_op jit(solution)/shard_map/pallas_call | solution.py:399
  39.6 30.3 %all_to_all.17.got_ref = f32[64,16,84]{2,1,0:T(8,128)S(1)} all-to-all(f32[64,16,84]{2,1,0:T(8,128)S(1)} %get-tuple-element.18), channel_id=1, replica_groups=mesh['sec'=4,'lat'=16,'col'=4] {'lat','col'}, dimensions={0} | all-to-all | bytes 688128 | tf_op jit(solution)/shard_map/all_to_all | solution.py:405
  69.9 1.8 %shard_map.80 = f32[7,8,2,128]{3,2,1,0:T(2,128)} custom-call(f32[64,16,84]{2,1,0:T(8,128)S(1)} %all_to_all.17.got_ref, f32[2,1024,128]{2,1,0:T(8,128)S(1)} %get-tuple-element.19.poly_ref), custom_call_target="tpu_custom_call" | custom-call | tf_op jit(solution)/shard_map/pallas_call | solution.py:406

commit v3 on v2

--- a/solution.py
+++ b/solution.py
@@ -40,7 +40,7 @@
     return hi, lo
 
 
-def params(mib=24):
+def params(mib=16):
     return pltpu.CompilerParams(vmem_limit_bytes=mib << 20)
 
 
@@ -56,7 +56,7 @@
         hot_ref[c : c + step, :] = jnp.where(ids == order, 1.0, 0.0).astype(BF16)
 
 
-def trig_rows(orders, hi_ref, lo_ref):
+def trig_rows(orders, trig_ref):
     first = (lax.axis_index("col") * LONS).astype(F32)
     y = lax.broadcasted_iota(jnp.int32, (MMAX, 128), 1).astype(F32) + first
     product = y * orders
@@ -72,15 +72,18 @@
     cos_out = jnp.where((turn == 1.0) | (turn == 2.0), -cos_out, cos_out)
     sin_out = jnp.where((turn == 2.0) | (turn == 3.0), -sin_out, sin_out)
     norm = 1.0 / math.sqrt(NLON)
-    both = jnp.concatenate(
-        (cos_out.reshape(NL, 1, 8, 128), sin_out.reshape(NL, 1, 8, 128)), axis=1
-    ).reshape(2 * MMAX, 128)
-    hi, lo = split2(both * norm)
-    hi_ref[...] = hi
-    lo_ref[...] = lo
-
-
-def legendre_rows(order, geom_ref, poly_ref):
+    halves = [
+        part.reshape(NL, 2, 4, 128)[:, h].reshape(NL * 4, 128)
+        for part in (cos_out * norm, sin_out * norm)
+        for h in range(2)
+    ]
+    hi, lo = split2(jnp.concatenate(halves, axis=0))
+    trig_ref[:, 0:128] = hi
+    trig_ref[:, 128:256] = hi
+    trig_ref[:, 256:384] = lo
+
+
+def legendre_rows(order, geom_ref, poly_ref, weight_ref):
     lane = lanes_of((SLOTS_OWN, 128)).astype(F32)
     head = jnp.sum(jnp.where(lane == order, geom_ref[3:4, 0:128], 0.0), axis=1, keepdims=True)
     degree = lax.broadcasted_iota(jnp.int32, (SLOTS_OWN, 128), 1).astype(F32)
@@ -105,56 +108,66 @@
         poly_ref[0, n * 8 : n * 8 + 8, :] = fresh[:, :128]
         poly_ref[1, n * 8 : n * 8 + 8, :] = fresh[:, 128:]
         previous, current = current, fresh
-
-
-def pack_kernel(
-    state_hbm,
-    force_hbm,
-    order_hbm,
+    for s in range(SLOTS_OWN):
+        for h in range(2):
+            hi, lo = split2(poly_ref[h, pl.ds(s, MMAX, stride=8), :])
+            for part, block in ((hi, 0), (lo, 2), (hi, 4)):
+                at = (block + h) * 128
+                weight_ref[s, :, at : at + 128] = part
+
+
+def table_kernel(
     wave_hbm,
     geom_hbm,
     moist_hbm,
-    out_ref,
-    hot_ref,
-    cols_ref,
-    hi_ref,
-    lo_ref,
-    poly_ref,
-    moist_ref,
-    state_ref,
-    force_ref,
-    order_ref,
+    trig_ref,
+    weight_ref,
+    water_hbm,
     wave_ref,
     geom_ref,
+    moist_ref,
+    poly_ref,
     orders_ref,
+    level_ref,
+    water_ref,
     sems,
 ):
-    loads = [
-        pltpu.make_async_copy(src, dst, sems.at[n])
-        for n, (src, dst) in enumerate(
-            (
-                (wave_hbm, wave_ref),
-                (geom_hbm, geom_ref),
-                (order_hbm, order_ref),
-                (state_hbm, state_ref),
-                (force_hbm, force_ref),
-                (moist_hbm, moist_ref),
-            )
-        )
-    ]
+    pairs = ((wave_hbm, wave_ref), (geom_hbm, geom_ref), (moist_hbm, moist_ref))
+    loads = [pltpu.make_async_copy(src, dst, sems.at[n]) for n, (src, dst) in enumerate(pairs)]
+    for load in loads:
+        load.start()
+    loads[2].wait()
+    blank = jnp.zeros((NCRM, 384 - RUNS), F32)
+    for k in range(LEVELS):
+        level = jnp.concatenate((moist_ref[k].astype(F32), blank), axis=1)
+        for v in range(3):
+            level_ref[k, v] = level[:, v * 128 : v * 128 + 128]
+        for v in range(3):
+            for n in range(4):
+                water_ref[k, v, n] = level_ref[k, v, pl.ds(n, 8, stride=4), :]
+    save = pltpu.make_async_copy(water_ref, water_hbm, sems.at[3])
+    save.start()
+    loads[0].wait()
+    loads[1].wait()
+    orders = jnp.broadcast_to(wave_ref[...].astype(F32), (MMAX, MMAX)).T
+    orders_ref[...] = orders
+    trig_rows(orders, trig_ref)
+    first = pl.multiple_of(lax.axis_index("lat") * SLOTS_OWN, SLOTS_OWN)
+    legendre_rows(orders_ref[pl.ds(first, SLOTS_OWN), :], geom_ref, poly_ref, weight_ref)
+    save.wait()
+
+
+def pack_kernel(
+    state_hbm, force_hbm, order_hbm, out_ref, hot_ref, cols_ref, state_ref, force_ref, order_ref, sems
+):
+    pairs = ((order_hbm, order_ref), (state_hbm, state_ref), (force_hbm, force_ref))
+    loads = [pltpu.make_async_copy(src, dst, sems.at[n]) for n, (src, dst) in enumerate(pairs)]
     for load in loads:
         load.start()
     loads[0].wait()
-    orders = jnp.broadcast_to(wave_ref[...].astype(F32), (MMAX, MMAX)).T
-    orders_ref[...] = orders
-    trig_rows(orders, hi_ref, lo_ref)
+    fill_one_hot(order_ref, hot_ref)
     loads[1].wait()
-    first = pl.multiple_of(lax.axis_index("lat") * SLOTS_OWN, SLOTS_OWN)
-    legendre_rows(orders_ref[pl.ds(first, SLOTS_OWN), :], geom_ref, poly_ref)
     loads[2].wait()
-    fill_one_hot(order_ref, hot_ref)
-    loads[3].wait()
-    loads[4].wait()
     for ref, base in ((state_ref, 0), (force_ref, LEVELS)):
         rows = ref[...].reshape(LEVELS, BAND, LONS)
         for b in range(BAND):
@@ -178,7 +191,6 @@
                 src = pltpu.roll(src, shift, 1)
             tile = src if tile is None else jnp.where(lane >= q * PER, src, tile)
         out_ref[t] = tile
-    loads[5].wait()
 
 
 def gather_lanes(tile_of, q_list, first, count, width, store):
@@ -198,12 +210,17 @@
             store(q, v, acc)
 
 
-def cloud_kernel(got_ref, moist_ref, out_ref, wind_ref, diff_ref, left_ref, right_ref, rain_ref):
+def cloud_kernel(
+    got_ref, water_hbm, out_ref, wind_ref, diff_ref, left_ref, right_ref, rain_ref, water_ref, sem
+):
+    load = pltpu.make_async_copy(water_hbm, water_ref, sem)
+    load.start()
+
     def store_wind(q, v, x):
-        wind_ref[q * 8 : q * 8 + 8, v * 128 : v * 128 + 128] = x
+        wind_ref[v, q * 8 : q * 8 + 8, :] = x
 
     def store_diff(q, v, x):
-        diff_ref[q * 8 : q * 8 + 8, v * 128 : v * 128 + 128] = x
+        diff_ref[v, q * 8 : q * 8 + 8, :] = x
 
     gather_lanes(lambda i: got_ref[i], range(4), 0, NL, RUNS, store_wind)
     cache = {}
@@ -221,30 +238,41 @@
     rain_ref[...] = jnp.zeros_like(rain_ref)
 
     def level(k, carry):
-        row = (pl.ds(k, 1), slice(0, RUNS))
-        gap = diff_ref[row] + moist_ref[k].astype(F32)
-        push = diff_ref[pl.ds(k + LEVELS, 1), 0:RUNS] * (1.0 / NSUB)
-        ahead = left_ref[row]
-        behind = right_ref[row]
-        both = ahead + behind
-        wet = jnp.maximum(gap, 0.0)
-        for _ in range(NSUB - 1):
-            up = pltpu.roll(gap, NCRM - 1, 0)
-            down = pltpu.roll(gap, 1, 0)
-            gap = (jnp.minimum(gap, 0.0) - both * gap) + (ahead * up + behind * down) + push
-            wet = wet + jnp.maximum(gap, 0.0)
-        rain_ref[pl.ds(k, 1), 0:RUNS] = jnp.sum(wet, axis=0, keepdims=True) * (0.5 / NCRM)
+        for v in range(3):
+
+            def row(ref, at):
+                return jnp.broadcast_to(ref[v, pl.ds(at, 1), :], (8, 128))
+
+            start = row(diff_ref, k)
+            push = row(diff_ref, k + LEVELS) * (1.0 / NSUB)
+            ahead = row(left_ref, k)
+            behind = row(right_ref, k)
+            keep = 1.0 - (ahead + behind)
+            gap = [start + water_ref[k, v, n] for n in range(4)]
+            wet = [jnp.maximum(g, 0.0) for g in gap]
+            total = (wet[0] + wet[1]) + (wet[2] + wet[3])
+            for _ in range(NSUB - 1):
+                up = gap[1:] + [pltpu.roll(gap[0], 7, 0)]
+                down = [pltpu.roll(gap[3], 1, 0)] + gap[:3]
+                gap = [
+                    ((keep * gap[n] - wet[n]) + push) + (ahead * up[n] + behind * down[n])
+                    for n in range(4)
+                ]
+                wet = [jnp.maximum(g, 0.0) for g in gap]
+                total = total + ((wet[0] + wet[1]) + (wet[2] + wet[3]))
+            rain_ref[v, pl.ds(k, 1), :] = jnp.sum(total, axis=0, keepdims=True) * (0.5 / NCRM)
         return carry
 
-    lax.fori_loop(0, LEVELS, level, 0)
+    load.wait()
+    lax.fori_loop(0, LEVELS, level, 0, unroll=2)
     lane = lanes_of((8, 128))
     for i in range(NL):
         v, off = divmod(i * PER, 128)
         tile = None
         for q in range(4):
-            src = rain_ref[q * 8 : q * 8 + 8, v * 128 : v * 128 + 128]
+            src = rain_ref[v, q * 8 : q * 8 + 8, :]
             if off + PER > 128:
-                nxt = rain_ref[q * 8 : q * 8 + 8, v * 128 + 128 : v * 128 + 256]
+                nxt = rain_ref[v + 1, q * 8 : q * 8 + 8, :]
                 src = jnp.where(lane < off, nxt, src)
             shift = (q * PER - off) % 128
             if shift:
@@ -257,7 +285,7 @@
             out_ref[s * NL + i] = tile
 
 
-def update_kernel(got_ref, hot_ref, cols_ref, hi_ref, lo_ref, out_ref, four_ref, slots_ref, rows_ref):
+def update_kernel(got_ref, hot_ref, cols_ref, trig_ref, out_ref, four_ref, slots_ref, rows_ref):
     def store(q, v, x):
         slots_ref[q * 8 : q * 8 + 8, v * 128 : v * 128 + 128] = x
 
@@ -285,43 +313,37 @@
         rows_ref[pl.ds(b, LEVELS, stride=BAND), :] = piece
     rows = rows_ref[...]
     out_ref[...] = rows[:, :LONS].reshape(ROWS, 1, LONS)
-    xhi, xlo = split2(rows)
+    hi, lo = split2(rows)
     dims = (((1,), (1,)), ((), ()))
-    out = lax.dot_general(hi_ref[...], xhi, dims, preferred_element_type=F32)
-    out = out + lax.dot_general(hi_ref[...], xlo, dims, preferred_element_type=F32)
-    out = out + lax.dot_general(lo_ref[...], xhi, dims, preferred_element_type=F32)
+    parts = jnp.concatenate((hi, lo, hi), axis=1)
+    out = lax.dot_general(trig_ref[...], parts, dims, preferred_element_type=F32)
     width = LEV_OWN * BAND
+    blank = jnp.zeros((NL * 4, 384 - 4 * width), F32)
     for j in range(NC):
-        part = out[:, j * width : (j + 1) * width].reshape(NL, 16, width)
-        for i in range(NL):
-            four_ref[i * NC + j] = part[i]
-
-
-def legendre_kernel(got_ref, poly_ref, out_ref, band_ref):
+        pieces = [out[g * 64 : g * 64 + 64, j * width : (j + 1) * width] for g in range(4)]
+        four_ref[:, j] = jnp.concatenate(pieces + [blank], axis=1).reshape(NL, 4, 384)
+
+
+def legendre_kernel(got_ref, weight_ref, out_ref, band_ref):
+    width = LEV_OWN * BAND
     band_ref[1] = jnp.zeros_like(band_ref[1])
-    bands = [
-        (got_ref[i * NC] + got_ref[i * NC + 1]) + (got_ref[i * NC + 2] + got_ref[i * NC + 3])
-        for i in range(NL)
-    ]
-    for k in range(LEV_OWN):
-        for i in range(NL):
-            h, at = divmod(i * BAND, 128)
-            first = min(BAND, 128 - at)
+    for i in range(NL):
+        part = (got_ref[i, 0] + got_ref[i, 1]) + (got_ref[i, 2] + got_ref[i, 3])
+        bands = jnp.concatenate([part[:, g * width : (g + 1) * width] for g in range(4)], axis=0)
+        h, at = divmod(i * BAND, 128)
+        first = min(BAND, 128 - at)
+        for k in range(LEV_OWN):
             row = slice(k * 16, k * 16 + 16)
-            piece = bands[i][:, k * BAND : (k + 1) * BAND]
+            piece = bands[:, k * BAND : (k + 1) * BAND]
             band_ref[h, row, at : at + first] = piece[:, :first]
             if first < BAND:
                 band_ref[h + 1, row, 0 : BAND - first] = piece[:, first:]
     dims = (((1,), (1,)), ((), ()))
     for s in range(SLOTS_OWN):
-        out = None
-        for h in range(2):
-            hi, lo = split2(band_ref[h, pl.ds(s, 2 * LEV_OWN, stride=8), :])
-            whi, wlo = split2(poly_ref[h, pl.ds(s, MMAX, stride=8), :])
-            part = lax.dot_general(hi, whi, dims, preferred_element_type=F32)
-            part = part + lax.dot_general(hi, wlo, dims, preferred_element_type=F32)
-            part = part + lax.dot_general(lo, whi, dims, preferred_element_type=F32)
-            out = part if out is None else out + part
+        rows = [band_ref[h, pl.ds(s, 2 * LEV_OWN, stride=8), :] for h in range(2)]
+        hi, lo = split2(jnp.concatenate(rows, axis=1))
+        parts = jnp.concatenate((hi, hi, lo), axis=1)
+        out = lax.dot_general(parts, weight_ref[s], dims, preferred_element_type=F32)
         out_ref[:, s, :, :] = out.reshape(LEV_OWN, 2, MMAX)
 
 
@@ -338,12 +360,12 @@
     return rows.astype(np.float32)
 
 
-def call(kernel, out, specs, scratch=()):
+def call(kernel, out, specs, scratch=(), out_specs=None):
     return pl.pallas_call(
         kernel,
         out_shape=out,
         in_specs=specs,
-        out_specs=jax.tree.map(lambda _: VMEM, out),
+        out_specs=out_specs or jax.tree.map(lambda _: VMEM, out),
         scratch_shapes=list(scratch),
         compiler_params=params(),
     )
@@ -360,55 +382,74 @@
     moist = crm_moisture.transpose(0, 2, 3, 4, 1, 5).reshape(LEVELS, NCRM, RUNS)
     order = cloud_order.reshape(1, COLS)
     waves = wave_table.reshape(1, MMAX)
-    outgoing, hot, cols, trig_hi, trig_lo, poly, moist = call(
+    outgoing, hot, cols = call(
         pack_kernel,
         (
             shape((TARGETS, 8, 128), F32),
             shape((COLS, COLS), BF16),
             shape((2 * LEVELS, COLS), F32),
-            shape((2 * MMAX, 128), BF16),
-            shape((2 * MMAX, 128), BF16),
-            shape((2, MMAX * SLOTS_OWN, 128), F32),
-            shape((LEVELS, NCRM, RUNS), BF16),
         ),
-        [HBM] * 6,
+        [HBM] * 3,
         [
             pltpu.VMEM((ROWS, 1, LONS), F32),
             pltpu.VMEM((ROWS, 1, LONS), F32),
             pltpu.VMEM((1, COLS), jnp.int32),
+            pltpu.SemaphoreType.DMA((3,)),
+        ],
+    )(*(stay(x) for x in (state, forcing, order)))
+    outgoing, waves = lax.optimization_barrier((outgoing, waves))
+    arrived = lax.all_to_all(outgoing, ("sec", "lat"), split_axis=0, concat_axis=0, tiled=True)
+    trig, weights, water = call(
+        table_kernel,
+        (
+            shape((2 * MMAX, 384), BF16),
+            shape((SLOTS_OWN, MMAX, 768), BF16),
+            shape((LEVELS, 3, 4, 8, 128), F32),
+        ),
+        [HBM] * 3,
+        [
             pltpu.VMEM((1, MMAX), jnp.int32),
             pltpu.VMEM((4, 256), F32),
+            pltpu.VMEM((LEVELS, NCRM, RUNS), BF16),
+            pltpu.VMEM((2, MMAX * SLOTS_OWN, 128), F32),
             pltpu.VMEM((MMAX, 128), F32),
-            pltpu.SemaphoreType.DMA((6,)),
+            pltpu.VMEM((LEVELS, 3, NCRM, 128), F32),
+            pltpu.VMEM((LEVELS, 3, 4, 8, 128), F32),
+            pltpu.SemaphoreType.DMA((4,)),
         ],
-    )(*(stay(x) for x in (state, forcing, order, waves, jnp.asarray(geometry()), moist)))
-    arrived = lax.all_to_all(outgoing, ("sec", "lat"), split_axis=0, concat_axis=0, tiled=True)
+        (VMEM, VMEM, HBM),
+    )(*(stay(x) for x in (waves, jnp.asarray(geometry()), moist)))
+    arrived, trig = lax.optimization_barrier((arrived, trig))
     rain = call(
         cloud_kernel,
         shape((TARGETS, 4, 128), F32),
-        [VMEM, VMEM],
+        [VMEM, HBM],
         [
-            pltpu.VMEM((32, 384), F32),
-            pltpu.VMEM((56, 384), F32),
-            pltpu.VMEM((32, 384), F32),
-            pltpu.VMEM((32, 384), F32),
-            pltpu.VMEM((32, 384), F32),
+            pltpu.VMEM((3, 32, 128), F32),
+            pltpu.VMEM((3, 56, 128), F32),
+            pltpu.VMEM((3, 32, 128), F32),
+            pltpu.VMEM((3, 32, 128), F32),
+            pltpu.VMEM((3, 32, 128), F32),
+            pltpu.VMEM((LEVELS, 3, 4, 8, 128), F32),
+            pltpu.SemaphoreType.DMA,
         ],
-    )(arrived, moist)
+    )(arrived, stay(water))
     returned = lax.all_to_all(rain, ("sec", "lat"), split_axis=0, concat_axis=0, tiled=True)
     updated, fourier = call(
         update_kernel,
-        (shape((ROWS, 1, LONS), F32), shape((NL * NC, 16, LEV_OWN * BAND), F32)),
-        [VMEM] * 5,
+        (shape((ROWS, 1, LONS), F32), shape((NL, NC, 4, 384), F32)),
+        [VMEM] * 4,
         [pltpu.VMEM((32, COLS), F32), pltpu.VMEM((ROWS, 128), F32)],
-    )(returned, hot, cols, trig_hi, trig_lo)
-    bands = lax.all_to_all(fourier, ("lat", "col"), split_axis=0, concat_axis=0, tiled=True)
+    )(returned, hot, cols, trig)
+    bands = lax.all_to_all(
+        fourier.reshape(NL * NC, 4, 384), ("lat", "col"), split_axis=0, concat_axis=0, tiled=True
+    )
     spectral = call(
         legendre_kernel,
         shape((LEV_OWN, SLOTS_OWN, 2, MMAX), F32),
         [VMEM] * 2,
         [pltpu.VMEM((2, LEV_OWN * 16, 128), F32)],
-    )(bands, poly)
+    )(bands.reshape(NL, NC, 4, 384), weights)
     new_state = updated.reshape(1, LEVELS, BAND, 1, LONS).transpose(0, 3, 1, 2, 4)
     return new_state, spectral[None, None]
 

time: 72.3 us -> 69.5 us (0.961)
  blocking collectives: 60.8 us -> 40.2 us
  starting transfers between devices: 0 us -> 9.39 us
  waiting for transfers between devices: 0 us -> 3.88 us
  local copies, waits for them, and re-layouts: 0 us -> 2.23 us
  Pallas kernels: 10.2 us -> 12.4 us
    all_to_all x2 -> x1, blocking collectives: 48.2 us -> 27.6 us  [shards(): lax.all_to_all(fourier.reshape(NL * NC, 4, 384), ('lat', 'col'), split_ax...]
    all_to_all x0 -> x1, starting transfers between devices: none -> 9.39 us  [shards(): lax.all_to_all(outgoing, ('sec', 'lat'), split_axis=0, concat_axis=0, til...]
    all_to_all x0 -> x1, waiting for transfers between devices: none -> 3.88 us  [shards(): lax.all_to_all(outgoing, ('sec', 'lat'), split_axis=0, concat_axis=0, til...]
    pallas_call x2 -> x3, Pallas kernels: 5.4 us -> 8.05 us  [the longest x1 3.43 us: shards(): call(cloud_kernel, shape((TARGETS, 4, 128), F32), [VMEM, HBM], [pltpu.VME...]
    unnamed x0 -> x6, local copies, waits for them, and re-layouts: none -> 2.23 us
  transfers between devices with their start and end apart: 0 -> 1, of which waited for: 0 -> 1; matrix products, arithmetic and copies ran while one was open for 0% -> 0% of each run, Pallas kernels for 0% -> 4%
where the time goes in v3:
time: 69.5 us; the launch traced here: 68.8 us
  blocking collectives  40.2 us (58%)
  Pallas kernels  12.4 us (18%)
  starting transfers between devices  9.39 us (14%)
  waiting for transfers between devices  3.88 us (6%)
  local copies, waits for them, and re-layouts  2.23 us (3%)
    all_to_all x1, blocking collectives, shards(): lax.all_to_all(fourier.reshape(NL * NC, 4, 384), ('lat', 'col'), split_ax...  27.6 us
    all_to_all x1, blocking collectives, shards(): lax.all_to_all(rain, ('sec', 'lat'), split_axis=0, concat_axis=0, tiled=T...  12.6 us
    all_to_all x1, starting transfers between devices, shards(): lax.all_to_all(outgoing, ('sec', 'lat'), split_axis=0, concat_axis=0, til...  9.39 us
    all_to_all x1, waiting for transfers between devices, shards(): lax.all_to_all(outgoing, ('sec', 'lat'), split_axis=0, concat_axis=0, til...  3.88 us
    pallas_call x1, Pallas kernels, shards(): call(cloud_kernel, shape((TARGETS, 4, 128), F32), [VMEM, HBM], [pltpu.VME...  3.43 us
    pallas_call x1, Pallas kernels, shards(): call(pack_kernel, (shape((TARGETS, 8, 128), F32), shape((COLS, COLS), BF1...  2.86 us
    pallas_call x1, Pallas kernels, shards(): call(table_kernel, (shape((2 * MMAX, 384), BF16), shape((SLOTS_OWN, MMAX,...  2.6 us
    unnamed x6, local copies, waits for them, and re-layouts  2.23 us
  transfers between devices with their start and end apart: 1, of which 1 were waited for; matrix products, arithmetic and copies ran while one was open for 0% of the time, Pallas kernels for 4%

profile of v3, /device:TPU:2, one launch (start us, length us, event | category | flops | bytes accessed | tf_op | source)
XLA Modules:
  0.0 68.8 jit_solution(13213753619152671966)
XLA Ops:
  0.6 2.9 %shard_map.77 = (f32[64,8,128]{2,1,0:T(8,128)}, bf16[1152,1152]{1,0:T(8,128)(2,1)S(1)}, f32[56,1152]{1,0:T(8,128)S(1)}) custom-call(f32[336,1,96]{2,1,0:T(1,128)} %bitcast.18, f32[336,1,96]{2,1,0:T(1,128)} %bitcast.19, s32[1,1152]{1,0:T(1,128)} %bitcast.21), custom_call_target="tpu_custom_call" | custom-call | tf_op jit(solution)/shard_map/pallas_call | solution.py:385
  3.5 9.4 %all-to-all-start = ((f32[64,8,128]{2,1,0:T(8,128)}), f32[64,8,128]{2,1,0:T(8,128)S(1)}, u32[]{:S(2)}, u32[]{:S(2)}) async-start(f32[64,8,128]{2,1,0:T(8,128)} %get-tuple-element.15), calls=%async_computation | async-start | bytes 524288 | tf_op jit(solution)/shard_map/all_to_all | solution.py:401
  12.9 2.6 %shard_map.78 = (bf16[256,384]{1,0:T(8,128)(2,1)S(1)}, bf16[8,128,768]{2,1,0:T(8,128)(2,1)S(1)}, f32[28,3,4,8,128]{4,3,2,1,0:T(8,128)S(1)}) custom-call(s32[1,128]{1,0:T(1,128)} %bitcast.22, f32[4,256]{1,0:T(4,128)} %constant.2.clone.geom_hbm, bf16[28,32,288]{2,1,0:T(8,128)(2,1)} %bitcast.17), custom_call_target="tpu_custom_call" | custom-call | tf_op jit(solution)/shard_map/pallas_call | solution.py:402
  15.5 0.0 copy-start
  15.5 1.1 %copy-done = bf16[8,128,768]{2,1,0:T(8,128)(2,1)} copy-done((bf16[8,128,768]{2,1,0:T(8,128)(2,1)}, bf16[8,128,768]{2,1,0:T(8,128)(2,1)S(1)}, u32[]{:S(2)}) %copy-start) | copy-done | bytes 1572888
  16.7 0.0 copy-start.2
  16.7 1.1 %copy-done.2 = f32[28,3,4,8,128]{4,3,2,1,0:T(8,128)} copy-done((f32[28,3,4,8,128]{4,3,2,1,0:T(8,128)}, f32[28,3,4,8,128]{4,3,2,1,0:T(8,128)S(1)}, u32[]{:S(2)}) %copy-start.2) | copy-done | bytes 1376280
  17.7 3.9 %all-to-all-done.got_ref = f32[64,8,128]{2,1,0:T(8,128)S(1)} async-done(((f32[64,8,128]{2,1,0:T(8,128)}), f32[64,8,128]{2,1,0:T(8,128)S(1)}, u32[]{:S(2)}, u32[]{:S(2)}) %all-to-all-start) | async-done | bytes 262176 | tf_op jit(solution)/shard_map/all_to_all | solution.py:401
  21.6 3.4 %shard_map.79 = f32[64,4,128]{2,1,0:T(4,128)S(1)} custom-call(f32[64,8,128]{2,1,0:T(8,128)S(1)} %all-to-all-done.got_ref, f32[28,3,4,8,128]{4,3,2,1,0:T(8,128)} %copy-done.2), custom_call_target="tpu_custom_call" | custom-call | tf_op jit(solution)/shard_map/pallas_call | solution.py:423
  25.1 12.6 %all_to_all.15.got_ref = f32[64,4,128]{2,1,0:T(4,128)S(1)} all-to-all(f32[64,4,128]{2,1,0:T(4,128)S(1)} %shard_map.79), channel_id=1, replica_groups=mesh['sec'=4,'lat'=16,'col'=4] {'sec','lat'}, dimensions={0} | all-to-all | bytes 262144 | tf_op jit(solution)/shard_map/all_to_all | solution.py:437
  37.7 0.0 copy-start.1
  37.7 2.0 %shard_map.80 = (f32[336,1,96]{2,1,0:T(1,128)}, f32[16,4,4,384]{3,2,1,0:T(4,128)S(1)}) custom-call(f32[64,4,128]{2,1,0:T(4,128)S(1)} %all_to_all.15.got_ref, bf16[1152,1152]{1,0:T(8,128)(2,1)S(1)} %get-tuple-element.20.hot_ref, f32[56,1152]{1,0:T(8,128)S(1)} %get-tuple-element.21.cols_ref, bf16[256,384]{1,0:T(8,128)(2,1)S(1)} %get-tuple-element.22.trig_ref), custom_call_target="tpu_custom_call" | custom-call | tf_op jit(solution)/shard_map/pallas_call | solution.py:438
  39.7 27.6 %all_to_all.16 = f32[64,4,384]{2,1,0:T(4,128)S(1)} all-to-all(f32[64,4,384]{2,1,0:T(4,128)S(1)} %bitcast.16), channel_id=1, replica_groups=mesh['sec'=4,'lat'=16,'col'=4] {'lat','col'}, dimensions={0} | all-to-all | bytes 786432 | tf_op jit(solution)/shard_map/all_to_all | solution.py:444
  67.3 0.0 copy-done.1
  67.3 1.5 %shard_map.81 = f32[7,8,2,128]{3,2,1,0:T(2,128)} custom-call(f32[16,4,4,384]{3,2,1,0:T(4,128)S(1)} %bitcast.15, bf16[8,128,768]{2,1,0:T(8,128)(2,1)S(1)} %copy-done.1), custom_call_target="tpu_custom_call" | custom-call | tf_op jit(solution)/shard_map/pallas_call | solution.py:447
Async XLA Ops:
  3.5 18.1 %all-to-all-start = ((f32[64,8,128]{2,1,0:T(8,128)}), f32[64,8,128]{2,1,0:T(8,128)S(1)}, u32[]{:S(2)}, u32[]{:S(2)}) async-start(f32[64,8,128]{2,1,0:T(8,128)} %get-tuple-element.15), calls=%async_computation | async-start | bytes 524288 | tf_op jit(solution)/shard_map/all_to_all | solution.py:401
  15.5 1.1 %copy-start = (bf16[8,128,768]{2,1,0:T(8,128)(2,1)}, bf16[8,128,768]{2,1,0:T(8,128)(2,1)S(1)}, u32[]{:S(2)}) copy-start(bf16[8,128,768]{2,1,0:T(8,128)(2,1)S(1)} %get-tuple-element.25.weight_ref) | copy-start | bytes 4718596
  16.7 1.1 %copy-start.2 = (f32[28,3,4,8,128]{4,3,2,1,0:T(8,128)}, f32[28,3,4,8,128]{4,3,2,1,0:T(8,128)S(1)}, u32[]{:S(2)}) copy-start(f32[28,3,4,8,128]{4,3,2,1,0:T(8,128)S(1)} %get-tuple-element.19.water_hbm) | copy-start | bytes 4128772
  37.7 29.6 %copy-start.1 = (bf16[8,128,768]{2,1,0:T(8,128)(2,1)S(1)}, bf16[8,128,768]{2,1,0:T(8,128)(2,1)}, u32[]{:S(2)}) copy-start(bf16[8,128,768]{2,1,0:T(8,128)(2,1)} %copy-done) | copy-start | bytes 4718596

commit v4 on v3

--- a/solution.py
+++ b/solution.py
@@ -25,6 +25,7 @@
 NC = 4
 RUNS = NL * PER
 HALF = 4 * PER
+TAIL = RUNS - 256
 LEV_OWN = LEVELS // NC
 SLOTS_OWN = MMAX // NL
 
@@ -116,58 +117,73 @@
                 weight_ref[s, :, at : at + 128] = part
 
 
-def table_kernel(
+def arrange_moisture(moist_ref, level_ref, water_ref, tail_ref):
+    lane = lanes_of((8, 128))
+    blank = jnp.zeros((NCRM, 384 - RUNS), F32)
+    for k in range(LEVELS):
+        level = jnp.concatenate((moist_ref[k].astype(F32), blank), axis=1)
+        for v in range(3):
+            level_ref[k, v] = level[:, v * 128 : v * 128 + 128]
+    for k in range(LEVELS):
+        for v in range(2):
+            for n in range(4):
+                water_ref[k, v, n] = level_ref[k, v, pl.ds(n, 8, stride=4), :]
+    for g in range(LEVELS // 4):
+        for n in range(4):
+            tile = level_ref[4 * g, 2, pl.ds(n, 8, stride=4), :]
+            for kk in range(1, 4):
+                more = pltpu.roll(level_ref[4 * g + kk, 2, pl.ds(n, 8, stride=4), :], kk * TAIL, 1)
+                tile = jnp.where(lane >= kk * TAIL, more, tile)
+            tail_ref[g, n] = tile
+
+
+def pack_kernel(
+    state_hbm,
+    force_hbm,
+    order_hbm,
     wave_hbm,
     geom_hbm,
     moist_hbm,
+    out_ref,
+    hot_ref,
+    cols_ref,
     trig_ref,
     weight_ref,
-    water_hbm,
+    water_ref,
+    tail_ref,
+    state_ref,
+    force_ref,
+    order_ref,
     wave_ref,
     geom_ref,
     moist_ref,
     poly_ref,
     orders_ref,
     level_ref,
-    water_ref,
     sems,
 ):
-    pairs = ((wave_hbm, wave_ref), (geom_hbm, geom_ref), (moist_hbm, moist_ref))
+    pairs = (
+        (wave_hbm, wave_ref),
+        (geom_hbm, geom_ref),
+        (order_hbm, order_ref),
+        (state_hbm, state_ref),
+        (force_hbm, force_ref),
+        (moist_hbm, moist_ref),
+    )
     loads = [pltpu.make_async_copy(src, dst, sems.at[n]) for n, (src, dst) in enumerate(pairs)]
     for load in loads:
         load.start()
-    loads[2].wait()
-    blank = jnp.zeros((NCRM, 384 - RUNS), F32)
-    for k in range(LEVELS):
-        level = jnp.concatenate((moist_ref[k].astype(F32), blank), axis=1)
-        for v in range(3):
-            level_ref[k, v] = level[:, v * 128 : v * 128 + 128]
-        for v in range(3):
-            for n in range(4):
-                water_ref[k, v, n] = level_ref[k, v, pl.ds(n, 8, stride=4), :]
-    save = pltpu.make_async_copy(water_ref, water_hbm, sems.at[3])
-    save.start()
-    loads[0].wait()
-    loads[1].wait()
+    for load in loads[:3]:
+        load.wait()
+    fill_one_hot(order_ref, hot_ref)
     orders = jnp.broadcast_to(wave_ref[...].astype(F32), (MMAX, MMAX)).T
     orders_ref[...] = orders
     trig_rows(orders, trig_ref)
     first = pl.multiple_of(lax.axis_index("lat") * SLOTS_OWN, SLOTS_OWN)
     legendre_rows(orders_ref[pl.ds(first, SLOTS_OWN), :], geom_ref, poly_ref, weight_ref)
-    save.wait()
-
-
-def pack_kernel(
-    state_hbm, force_hbm, order_hbm, out_ref, hot_ref, cols_ref, state_ref, force_ref, order_ref, sems
-):
-    pairs = ((order_hbm, order_ref), (state_hbm, state_ref), (force_hbm, force_ref))
-    loads = [pltpu.make_async_copy(src, dst, sems.at[n]) for n, (src, dst) in enumerate(pairs)]
-    for load in loads:
-        load.start()
-    loads[0].wait()
-    fill_one_hot(order_ref, hot_ref)
-    loads[1].wait()
-    loads[2].wait()
+    for load in loads[3:]:
+        load.wait()
+    arrange_moisture(moist_ref, level_ref, water_ref, tail_ref)
     for ref, base in ((state_ref, 0), (force_ref, LEVELS)):
         rows = ref[...].reshape(LEVELS, BAND, LONS)
         for b in range(BAND):
@@ -210,12 +226,41 @@
             store(q, v, acc)
 
 
+def coefficients(wind):
+    courant = 0.4 * jnp.tanh(wind)
+    mixing = 0.2 + 0.5 * jnp.abs(courant)
+    return mixing - 0.5 * courant, mixing + 0.5 * courant
+
+
+def cloud_tile(start, push, ahead, behind, water):
+    keep = 1.0 - (ahead + behind)
+    gap = [start + w for w in water]
+    wet = [jnp.maximum(g, 0.0) for g in gap]
+    total = (wet[0] + wet[1]) + (wet[2] + wet[3])
+    for _ in range(NSUB - 1):
+        up = gap[1:] + [pltpu.roll(gap[0], 7, 0)]
+        down = [pltpu.roll(gap[3], 1, 0)] + gap[:3]
+        gap = [
+            ((keep * gap[n] - wet[n]) + push) + (ahead * up[n] + behind * down[n]) for n in range(4)
+        ]
+        wet = [jnp.maximum(g, 0.0) for g in gap]
+        total = total + ((wet[0] + wet[1]) + (wet[2] + wet[3]))
+    return jnp.sum(total, axis=0, keepdims=True) * (0.5 / NCRM)
+
+
 def cloud_kernel(
-    got_ref, water_hbm, out_ref, wind_ref, diff_ref, left_ref, right_ref, rain_ref, water_ref, sem
+    got_ref,
+    water_ref,
+    tail_ref,
+    out_ref,
+    wind_ref,
+    diff_ref,
+    push_ref,
+    left_ref,
+    right_ref,
+    rain_ref,
+    last_ref,
 ):
-    load = pltpu.make_async_copy(water_hbm, water_ref, sem)
-    load.start()
-
     def store_wind(q, v, x):
         wind_ref[v, q * 8 : q * 8 + 8, :] = x
 
@@ -231,41 +276,52 @@
         return cache[i]
 
     gather_lanes(diff, range(7), 0, NL, RUNS, store_diff)
-    courant = 0.4 * jnp.tanh(wind_ref[...])
-    mixing = 0.2 + 0.5 * jnp.abs(courant)
-    left_ref[...] = mixing - 0.5 * courant
-    right_ref[...] = mixing + 0.5 * courant
+    lane = lanes_of((8, 128))
+    groups = LEVELS // 4
+
+    def tails(ref, base):
+        tile = ref[2, pl.ds(base, 8, stride=4), :]
+        for kk in range(1, 4):
+            more = pltpu.roll(ref[2, pl.ds(base + kk, 8, stride=4), :], kk * TAIL, 1)
+            tile = jnp.where(lane >= kk * TAIL, more, tile)
+        return tile
+
+    wind_tail = tails(wind_ref, 0)
+    diff_tail = tails(diff_ref, 0)
+    push_tail = tails(diff_ref, LEVELS) * (1.0 / NSUB)
+    for v in range(2):
+        left_ref[v], right_ref[v] = coefficients(wind_ref[v])
+        push_ref[v] = diff_ref[v, LEVELS : LEVELS + 32, :] * (1.0 / NSUB)
+    last_ref[4] = jnp.zeros_like(diff_tail)
+    last_ref[0] = diff_tail
+    last_ref[1] = push_tail
+    last_ref[2], last_ref[3] = coefficients(wind_tail)
     rain_ref[...] = jnp.zeros_like(rain_ref)
 
-    def level(k, carry):
-        for v in range(3):
-
-            def row(ref, at):
-                return jnp.broadcast_to(ref[v, pl.ds(at, 1), :], (8, 128))
-
-            start = row(diff_ref, k)
-            push = row(diff_ref, k + LEVELS) * (1.0 / NSUB)
-            ahead = row(left_ref, k)
-            behind = row(right_ref, k)
-            keep = 1.0 - (ahead + behind)
-            gap = [start + water_ref[k, v, n] for n in range(4)]
-            wet = [jnp.maximum(g, 0.0) for g in gap]
-            total = (wet[0] + wet[1]) + (wet[2] + wet[3])
-            for _ in range(NSUB - 1):
-                up = gap[1:] + [pltpu.roll(gap[0], 7, 0)]
-                down = [pltpu.roll(gap[3], 1, 0)] + gap[:3]
-                gap = [
-                    ((keep * gap[n] - wet[n]) + push) + (ahead * up[n] + behind * down[n])
-                    for n in range(4)
-                ]
-                wet = [jnp.maximum(g, 0.0) for g in gap]
-                total = total + ((wet[0] + wet[1]) + (wet[2] + wet[3]))
-            rain_ref[v, pl.ds(k, 1), :] = jnp.sum(total, axis=0, keepdims=True) * (0.5 / NCRM)
+    def level(g, carry):
+        for kk in range(4):
+            k = 4 * g + kk
+            for v in range(2):
+
+                def row(ref):
+                    return jnp.broadcast_to(ref[v, pl.ds(k, 1), :], (8, 128))
+
+                rain_ref[v, pl.ds(k, 1), :] = cloud_tile(
+                    row(diff_ref),
+                    row(push_ref),
+                    row(left_ref),
+                    row(right_ref),
+                    [water_ref[k, v, n] for n in range(4)],
+                )
+        rows = [jnp.broadcast_to(last_ref[c, pl.ds(g, 1), :], (8, 128)) for c in range(4)]
+        last_ref[4, pl.ds(g, 1), :] = cloud_tile(*rows, [tail_ref[g, n] for n in range(4)])
         return carry
 
-    load.wait()
-    lax.fori_loop(0, LEVELS, level, 0, unroll=2)
-    lane = lanes_of((8, 128))
+    lax.fori_loop(0, groups, level, 0)
+    rain_tail = last_ref[4]
+    for kk in range(4):
+        piece = rain_tail if kk == 0 else pltpu.roll(rain_tail, 128 - kk * TAIL, 1)
+        rain_ref[2, pl.ds(kk, 8, stride=4), :] = piece
     for i in range(NL):
         v, off = divmod(i * PER, 128)
         tile = None
@@ -285,7 +341,9 @@
             out_ref[s * NL + i] = tile
 
 
-def update_kernel(got_ref, hot_ref, cols_ref, trig_ref, out_ref, four_ref, slots_ref, rows_ref):
+def update_kernel(
+    got_ref, hot_ref, cols_ref, trig_ref, out_hbm, four_ref, slots_ref, rows_ref, out_ref, sem
+):
     def store(q, v, x):
         slots_ref[q * 8 : q * 8 + 8, v * 128 : v * 128 + 128] = x
 
@@ -313,6 +371,8 @@
         rows_ref[pl.ds(b, LEVELS, stride=BAND), :] = piece
     rows = rows_ref[...]
     out_ref[...] = rows[:, :LONS].reshape(ROWS, 1, LONS)
+    save = pltpu.make_async_copy(out_ref, out_hbm, sem)
+    save.start()
     hi, lo = split2(rows)
     dims = (((1,), (1,)), ((), ()))
     parts = jnp.concatenate((hi, lo, hi), axis=1)
@@ -322,9 +382,10 @@
     for j in range(NC):
         pieces = [out[g * 64 : g * 64 + 64, j * width : (j + 1) * width] for g in range(4)]
         four_ref[:, j] = jnp.concatenate(pieces + [blank], axis=1).reshape(NL, 4, 384)
-
-
-def legendre_kernel(got_ref, weight_ref, out_ref, band_ref):
+    save.wait()
+
+
+def legendre_kernel(got_ref, weight_ref, out_hbm, band_ref, out_ref, sems):
     width = LEV_OWN * BAND
     band_ref[1] = jnp.zeros_like(band_ref[1])
     for i in range(NL):
@@ -339,12 +400,20 @@
             if first < BAND:
                 band_ref[h + 1, row, 0 : BAND - first] = piece[:, first:]
     dims = (((1,), (1,)), ((), ()))
+    saves = []
     for s in range(SLOTS_OWN):
         rows = [band_ref[h, pl.ds(s, 2 * LEV_OWN, stride=8), :] for h in range(2)]
         hi, lo = split2(jnp.concatenate(rows, axis=1))
         parts = jnp.concatenate((hi, hi, lo), axis=1)
         out = lax.dot_general(parts, weight_ref[s], dims, preferred_element_type=F32)
         out_ref[:, s, :, :] = out.reshape(LEV_OWN, 2, MMAX)
+        if s % 4 == 3:
+            part = pl.ds(s - 3, 4)
+            save = pltpu.make_async_copy(out_ref.at[:, part], out_hbm.at[:, part], sems.at[s // 4])
+            save.start()
+            saves.append(save)
+    for save in saves:
+        save.wait()
 
 
 def geometry():
@@ -382,64 +451,58 @@
     moist = crm_moisture.transpose(0, 2, 3, 4, 1, 5).reshape(LEVELS, NCRM, RUNS)
     order = cloud_order.reshape(1, COLS)
     waves = wave_table.reshape(1, MMAX)
-    outgoing, hot, cols = call(
+    outgoing, hot, cols, trig, weights, water, tail = call(
         pack_kernel,
         (
             shape((TARGETS, 8, 128), F32),
             shape((COLS, COLS), BF16),
             shape((2 * LEVELS, COLS), F32),
+            shape((2 * MMAX, 384), BF16),
+            shape((SLOTS_OWN, MMAX, 768), BF16),
+            shape((LEVELS, 2, 4, 8, 128), F32),
+            shape((LEVELS // 4, 4, 8, 128), F32),
         ),
-        [HBM] * 3,
+        [HBM] * 6,
         [
             pltpu.VMEM((ROWS, 1, LONS), F32),
             pltpu.VMEM((ROWS, 1, LONS), F32),
             pltpu.VMEM((1, COLS), jnp.int32),
-            pltpu.SemaphoreType.DMA((3,)),
-        ],
-    )(*(stay(x) for x in (state, forcing, order)))
-    outgoing, waves = lax.optimization_barrier((outgoing, waves))
-    arrived = lax.all_to_all(outgoing, ("sec", "lat"), split_axis=0, concat_axis=0, tiled=True)
-    trig, weights, water = call(
-        table_kernel,
-        (
-            shape((2 * MMAX, 384), BF16),
-            shape((SLOTS_OWN, MMAX, 768), BF16),
-            shape((LEVELS, 3, 4, 8, 128), F32),
-        ),
-        [HBM] * 3,
-        [
             pltpu.VMEM((1, MMAX), jnp.int32),
             pltpu.VMEM((4, 256), F32),
             pltpu.VMEM((LEVELS, NCRM, RUNS), BF16),
             pltpu.VMEM((2, MMAX * SLOTS_OWN, 128), F32),
             pltpu.VMEM((MMAX, 128), F32),
             pltpu.VMEM((LEVELS, 3, NCRM, 128), F32),
-            pltpu.VMEM((LEVELS, 3, 4, 8, 128), F32),
-            pltpu.SemaphoreType.DMA((4,)),
+            pltpu.SemaphoreType.DMA((6,)),
         ],
-        (VMEM, VMEM, HBM),
-    )(*(stay(x) for x in (waves, jnp.asarray(geometry()), moist)))
-    arrived, trig = lax.optimization_barrier((arrived, trig))
+    )(*(stay(x) for x in (state, forcing, order, waves, jnp.asarray(geometry()), moist)))
+    arrived = lax.all_to_all(outgoing, ("sec", "lat"), split_axis=0, concat_axis=0, tiled=True)
     rain = call(
         cloud_kernel,
         shape((TARGETS, 4, 128), F32),
-        [VMEM, HBM],
+        [VMEM] * 3,
         [
             pltpu.VMEM((3, 32, 128), F32),
-            pltpu.VMEM((3, 56, 128), F32),
+            pltpu.VMEM((3, 64, 128), F32),
+            pltpu.VMEM((2, 32, 128), F32),
+            pltpu.VMEM((2, 32, 128), F32),
+            pltpu.VMEM((2, 32, 128), F32),
             pltpu.VMEM((3, 32, 128), F32),
-            pltpu.VMEM((3, 32, 128), F32),
-            pltpu.VMEM((3, 32, 128), F32),
-            pltpu.VMEM((LEVELS, 3, 4, 8, 128), F32),
-            pltpu.SemaphoreType.DMA,
+            pltpu.VMEM((5, 8, 128), F32),
         ],
-    )(arrived, stay(water))
+    )(arrived, water, tail)
     returned = lax.all_to_all(rain, ("sec", "lat"), split_axis=0, concat_axis=0, tiled=True)
     updated, fourier = call(
         update_kernel,
         (shape((ROWS, 1, LONS), F32), shape((NL, NC, 4, 384), F32)),
         [VMEM] * 4,
-        [pltpu.VMEM((32, COLS), F32), pltpu.VMEM((ROWS, 128), F32)],
+        [
+            pltpu.VMEM((32, COLS), F32),
+            pltpu.VMEM((ROWS, 128), F32),
+            pltpu.VMEM((ROWS, 1, LONS), F32),
+            pltpu.SemaphoreType.DMA,
+        ],
+        (HBM, VMEM),
     )(returned, hot, cols, trig)
     bands = lax.all_to_all(
         fourier.reshape(NL * NC, 4, 384), ("lat", "col"), split_axis=0, concat_axis=0, tiled=True
@@ -448,7 +511,12 @@
         legendre_kernel,
         shape((LEV_OWN, SLOTS_OWN, 2, MMAX), F32),
         [VMEM] * 2,
-        [pltpu.VMEM((2, LEV_OWN * 16, 128), F32)],
+        [
+            pltpu.VMEM((2, LEV_OWN * 16, 128), F32),
+            pltpu.VMEM((LEV_OWN, SLOTS_OWN, 2, MMAX), F32),
+            pltpu.SemaphoreType.DMA((2,)),
+        ],
+        HBM,
     )(bands.reshape(NL, NC, 4, 384), weights)
     new_state = updated.reshape(1, LEVELS, BAND, 1, LONS).transpose(0, 3, 1, 2, 4)
     return new_state, spectral[None, None]

time: 69.5 us -> 68.1 us (0.980)
  blocking collectives: 40.2 us -> 58.1 us
  starting transfers between devices: 9.39 us -> 0 us
  waiting for transfers between devices: 3.88 us -> 0 us
  Pallas kernels: 12.4 us -> 8.76 us
  local copies, waits for them, and re-layouts: 2.23 us -> 0 us
    all_to_all x0 -> x1, blocking collectives: none -> 17.9 us  [shards(): lax.all_to_all(outgoing, ('sec', 'lat'), split_axis=0, concat_axis=0, til...]
    all_to_all x1 -> x0, starting transfers between devices: 9.39 us -> none  [shards(): lax.all_to_all(outgoing, ('sec', 'lat'), split_axis=0, concat_axis=0, til...]
    pallas_call x2 -> x1, Pallas kernels: 6.03 us -> 1.71 us  [shards(): call(cloud_kernel, shape((TARGETS, 4, 128), F32), [VMEM] * 3, [pltpu.VMEM...]
    all_to_all x1 -> x0, waiting for transfers between devices: 3.88 us -> none  [shards(): lax.all_to_all(outgoing, ('sec', 'lat'), split_axis=0, concat_axis=0, til...]
    unnamed x6 -> x0, local copies, waits for them, and re-layouts: 2.23 us -> none
  transfers between devices with their start and end apart: 1 -> 0, of which waited for: 1 -> 0; matrix products, arithmetic and copies ran while one was open for 0% -> 0% of each run, Pallas kernels for 4% -> 0%
where the time goes in v4:
time: 68.1 us; the launch traced here: 67.5 us
  blocking collectives  58.1 us (85%)
  Pallas kernels  8.76 us (13%)
    all_to_all x1, blocking collectives, shards(): lax.all_to_all(fourier.reshape(NL * NC, 4, 384), ('lat', 'col'), split_ax...  27.6 us
    all_to_all x1, blocking collectives, shards(): lax.all_to_all(outgoing, ('sec', 'lat'), split_axis=0, concat_axis=0, til...  17.9 us
    all_to_all x1, blocking collectives, shards(): lax.all_to_all(rain, ('sec', 'lat'), split_axis=0, concat_axis=0, tiled=T...  12.6 us
    pallas_call x1, Pallas kernels, shards(): call(pack_kernel, (shape((TARGETS, 8, 128), F32), shape((COLS, COLS), BF1...  3.51 us
    pallas_call x1, Pallas kernels, shards(): call(update_kernel, (shape((ROWS, 1, LONS), F32), shape((NL, NC, 4, 384),...  2.03 us
    pallas_call x1, Pallas kernels, shards(): call(cloud_kernel, shape((TARGETS, 4, 128), F32), [VMEM] * 3, [pltpu.VMEM...  1.71 us
    pallas_call x1, Pallas kernels, shards(): call(legendre_kernel, shape((LEV_OWN, SLOTS_OWN, 2, MMAX), F32), [VMEM] *...  1.51 us

profile of v4, /device:TPU:2, one launch (start us, length us, event | category | flops | bytes accessed | tf_op | source)
XLA Modules:
  0.0 67.5 jit_solution(14904143013215587068)
XLA Ops:
  0.6 3.5 %shard_map.77 = (f32[64,8,128]{2,1,0:T(8,128)S(1)}, bf16[1152,1152]{1,0:T(8,128)(2,1)S(1)}, f32[56,1152]{1,0:T(8,128)S(1)}, bf16[256,384]{1,0:T(8,128)(2,1)S(1)}...) custom-call(f32[336,1,96]{2,1,0:T(1,128)} %bitcast.18, ...), custom_call_target="tpu_custom_call" | custom-call | tf_op jit(solution)/shard_map/pallas_call | solution.py:454
  4.2 17.9 %all_to_all.15.got_ref = f32[64,8,128]{2,1,0:T(8,128)S(1)} all-to-all(f32[64,8,128]{2,1,0:T(8,128)S(1)} %get-tuple-element.11), channel_id=1, replica_groups=mesh['sec'=4,'lat'=16,'col'=4] {'sec','lat'}, dimensions={0} | all-to-all | bytes 524288 | tf_op jit(solution)/shard_map/all_to_all | solution.py:479
  22.1 1.7 %shard_map.78 = f32[64,4,128]{2,1,0:T(4,128)S(1)} custom-call(f32[64,8,128]{2,1,0:T(8,128)S(1)} %all_to_all.15.got_ref, f32[28,2,4,8,128]{4,3,2,1,0:T(8,128)S(1)} %get-tuple-element.12.water_ref, f32[7,4,8,128]{3,2,1,0:T(8,128)S(1)} %get-tuple-element.13.tail_ref), custom_call_target="tpu_custom_call" | custom-call | tf_op jit(solution)/shard_map/pallas_call | solution.py:480
  23.8 12.6 %all_to_all.16.got_ref = f32[64,4,128]{2,1,0:T(4,128)S(1)} all-to-all(f32[64,4,128]{2,1,0:T(4,128)S(1)} %shard_map.78), channel_id=1, replica_groups=mesh['sec'=4,'lat'=16,'col'=4] {'sec','lat'}, dimensions={0} | all-to-all | bytes 262144 | tf_op jit(solution)/shard_map/all_to_all | solution.py:494
  36.4 2.0 %shard_map.79 = (f32[336,1,96]{2,1,0:T(1,128)}, f32[16,4,4,384]{3,2,1,0:T(4,128)S(1)}) custom-call(f32[64,4,128]{2,1,0:T(4,128)S(1)} %all_to_all.16.got_ref, bf16[1152,1152]{1,0:T(8,128)(2,1)S(1)} %get-tuple-element.14.hot_ref, f32[56,1152]{1,0:T(8,128)S(1)} %get-tuple-element.15.cols_ref, bf16[256,384]{1,0:T(8,128)(2,1)S(1)} %get-tuple-element.16.trig_ref), custom_call_target="tpu_custom_call" | custom-call | tf_op jit(solution)/shard_map/pallas_call | solution.py:495
  38.4 27.6 %all_to_all.17 = f32[64,4,384]{2,1,0:T(4,128)S(1)} all-to-all(f32[64,4,384]{2,1,0:T(4,128)S(1)} %bitcast.16), channel_id=1, replica_groups=mesh['sec'=4,'lat'=16,'col'=4] {'lat','col'}, dimensions={0} | all-to-all | bytes 786432 | tf_op jit(solution)/shard_map/all_to_all | solution.py:507
  66.0 1.5 %shard_map.80 = f32[7,8,2,128]{3,2,1,0:T(2,128)} custom-call(f32[16,4,4,384]{3,2,1,0:T(4,128)S(1)} %bitcast.15, bf16[8,128,768]{2,1,0:T(8,128)(2,1)S(1)} %get-tuple-element.19.weight_ref), custom_call_target="tpu_custom_call" | custom-call | tf_op jit(solution)/shard_map/pallas_call | solution.py:510

commit v5 on v4

--- a/solution.py
+++ b/solution.py
@@ -112,7 +112,7 @@
     for s in range(SLOTS_OWN):
         for h in range(2):
             hi, lo = split2(poly_ref[h, pl.ds(s, MMAX, stride=8), :])
-            for part, block in ((hi, 0), (lo, 2), (hi, 4)):
+            for part, block in ((hi, 0), (lo, 2)):
                 at = (block + h) * 128
                 weight_ref[s, :, at : at + 128] = part
 
@@ -137,25 +137,19 @@
             tail_ref[g, n] = tile
 
 
-def pack_kernel(
-    state_hbm,
-    force_hbm,
-    order_hbm,
+def table_kernel(
     wave_hbm,
     geom_hbm,
+    order_hbm,
     moist_hbm,
-    out_ref,
-    hot_ref,
-    cols_ref,
     trig_ref,
     weight_ref,
     water_ref,
     tail_ref,
-    state_ref,
-    force_ref,
-    order_ref,
+    column_ref,
     wave_ref,
     geom_ref,
+    order_ref,
     moist_ref,
     poly_ref,
     orders_ref,
@@ -166,8 +160,6 @@
         (wave_hbm, wave_ref),
         (geom_hbm, geom_ref),
         (order_hbm, order_ref),
-        (state_hbm, state_ref),
-        (force_hbm, force_ref),
         (moist_hbm, moist_ref),
     )
     loads = [pltpu.make_async_copy(src, dst, sems.at[n]) for n, (src, dst) in enumerate(pairs)]
@@ -175,15 +167,44 @@
         load.start()
     for load in loads[:3]:
         load.wait()
-    fill_one_hot(order_ref, hot_ref)
     orders = jnp.broadcast_to(wave_ref[...].astype(F32), (MMAX, MMAX)).T
     orders_ref[...] = orders
     trig_rows(orders, trig_ref)
     first = pl.multiple_of(lax.axis_index("lat") * SLOTS_OWN, SLOTS_OWN)
     legendre_rows(orders_ref[pl.ds(first, SLOTS_OWN), :], geom_ref, poly_ref, weight_ref)
-    for load in loads[3:]:
+    order = order_ref[...].astype(F32)
+    for v in range(COLS // 128):
+        at = slice(v * 128, v * 128 + 128)
+        column_ref[at, :] = jnp.broadcast_to(order[:, at], (128, 128)).T
+    loads[3].wait()
+    arrange_moisture(moist_ref, level_ref, water_ref, tail_ref)
+
+
+def pack_kernel(
+    state_hbm,
+    force_hbm,
+    order_hbm,
+    out_hbm,
+    cols_ref,
+    state_ref,
+    force_ref,
+    order_ref,
+    hot_ref,
+    out_ref,
+    sems,
+):
+    half = ROWS // 2
+    pairs = [(order_hbm, order_ref)]
+    for part in (pl.ds(0, half), pl.ds(half, half)):
+        pairs.append((state_hbm.at[part], state_ref.at[part]))
+        pairs.append((force_hbm.at[part], force_ref.at[part]))
+    loads = [pltpu.make_async_copy(src, dst, sems.at[n]) for n, (src, dst) in enumerate(pairs)]
+    for load in loads:
+        load.start()
+    loads[0].wait()
+    fill_one_hot(order_ref, hot_ref)
+    for load in loads[1:]:
         load.wait()
-    arrange_moisture(moist_ref, level_ref, water_ref, tail_ref)
     for ref, base in ((state_ref, 0), (force_ref, LEVELS)):
         rows = ref[...].reshape(LEVELS, BAND, LONS)
         for b in range(BAND):
@@ -194,6 +215,7 @@
     got = got[: 2 * LEVELS] + got[2 * LEVELS :]
     lane = lanes_of((8, 128))
     groups = 2 * LEVELS // 8
+    saves = []
     for t in range(TARGETS):
         v, off = divmod(t * PER, 128)
         tile = None
@@ -207,6 +229,13 @@
                 src = pltpu.roll(src, shift, 1)
             tile = src if tile is None else jnp.where(lane >= q * PER, src, tile)
         out_ref[t] = tile
+        if t % 16 == 15:
+            part = pl.ds(t - 15, 16)
+            save = pltpu.make_async_copy(out_ref.at[part], out_hbm.at[part], sems.at[5 + t // 16])
+            save.start()
+            saves.append(save)
+    for save in saves:
+        save.wait()
 
 
 def gather_lanes(tile_of, q_list, first, count, width, store):
@@ -342,8 +371,26 @@
 
 
 def update_kernel(
-    got_ref, hot_ref, cols_ref, trig_ref, out_hbm, four_ref, slots_ref, rows_ref, out_ref, sem
+    got_ref,
+    column_ref,
+    cols_ref,
+    trig_ref,
+    out_hbm,
+    four_ref,
+    slots_ref,
+    rows_ref,
+    out_ref,
+    hot_ref,
+    sem,
 ):
+    lane = lanes_of((128, 128)).astype(F32)
+    for v in range(COLS // 128):
+        rows = slice(v * 128, v * 128 + 128)
+        column = column_ref[rows, :]
+        for c in range(COLS // 128):
+            hot = jnp.where(lane + float(c * 128) == column, 1.0, 0.0)
+            hot_ref[rows, c * 128 : c * 128 + 128] = hot.astype(BF16)
+
     def store(q, v, x):
         slots_ref[q * 8 : q * 8 + 8, v * 128 : v * 128 + 128] = x
 
@@ -358,7 +405,7 @@
     gather_lanes(tile_of, range(4), 0, TARGETS, COLS, store)
     hi, lo = split2(slots_ref[...])
     both = jnp.concatenate((hi, lo), axis=0)
-    back = lax.dot_general(both, hot_ref[...], (((1,), (1,)), ((), ())), preferred_element_type=F32)
+    back = jnp.dot(both, hot_ref[...], preferred_element_type=F32)
     rain = back[:LEVELS] + back[32 : 32 + LEVELS]
     sec = lax.axis_index("sec")
     add = jnp.where(sec == 2, 1.0, jnp.where(sec == 3, -1.0, 0.0)).astype(F32)
@@ -404,8 +451,9 @@
     for s in range(SLOTS_OWN):
         rows = [band_ref[h, pl.ds(s, 2 * LEV_OWN, stride=8), :] for h in range(2)]
         hi, lo = split2(jnp.concatenate(rows, axis=1))
-        parts = jnp.concatenate((hi, hi, lo), axis=1)
+        parts = jnp.concatenate((hi, hi), axis=1)
         out = lax.dot_general(parts, weight_ref[s], dims, preferred_element_type=F32)
+        out = out + lax.dot_general(lo, weight_ref[s, :, 0:256], dims, preferred_element_type=F32)
         out_ref[:, s, :, :] = out.reshape(LEV_OWN, 2, MMAX)
         if s % 4 == 3:
             part = pl.ds(s - 3, 4)
@@ -451,32 +499,44 @@
     moist = crm_moisture.transpose(0, 2, 3, 4, 1, 5).reshape(LEVELS, NCRM, RUNS)
     order = cloud_order.reshape(1, COLS)
     waves = wave_table.reshape(1, MMAX)
-    outgoing, hot, cols, trig, weights, water, tail = call(
+    outgoing, cols = call(
         pack_kernel,
-        (
-            shape((TARGETS, 8, 128), F32),
-            shape((COLS, COLS), BF16),
-            shape((2 * LEVELS, COLS), F32),
-            shape((2 * MMAX, 384), BF16),
-            shape((SLOTS_OWN, MMAX, 768), BF16),
-            shape((LEVELS, 2, 4, 8, 128), F32),
-            shape((LEVELS // 4, 4, 8, 128), F32),
-        ),
-        [HBM] * 6,
+        (shape((TARGETS, 8, 128), F32), shape((2 * LEVELS, COLS), F32)),
+        [HBM] * 3,
         [
             pltpu.VMEM((ROWS, 1, LONS), F32),
             pltpu.VMEM((ROWS, 1, LONS), F32),
             pltpu.VMEM((1, COLS), jnp.int32),
+            pltpu.VMEM((COLS, COLS), BF16),
+            pltpu.VMEM((TARGETS, 8, 128), F32),
+            pltpu.SemaphoreType.DMA((9,)),
+        ],
+        (HBM, VMEM),
+    )(*(stay(x) for x in (state, forcing, order)))
+    outgoing, waves = lax.optimization_barrier((outgoing, waves))
+    arrived = lax.all_to_all(outgoing, ("sec", "lat"), split_axis=0, concat_axis=0, tiled=True)
+    trig, weights, water, tail, column = call(
+        table_kernel,
+        (
+            shape((2 * MMAX, 384), BF16),
+            shape((SLOTS_OWN, MMAX, 512), BF16),
+            shape((LEVELS, 2, 4, 8, 128), F32),
+            shape((LEVELS // 4, 4, 8, 128), F32),
+            shape((COLS, 128), F32),
+        ),
+        [HBM] * 4,
+        [
             pltpu.VMEM((1, MMAX), jnp.int32),
             pltpu.VMEM((4, 256), F32),
+            pltpu.VMEM((1, COLS), jnp.int32),
             pltpu.VMEM((LEVELS, NCRM, RUNS), BF16),
             pltpu.VMEM((2, MMAX * SLOTS_OWN, 128), F32),
             pltpu.VMEM((MMAX, 128), F32),
             pltpu.VMEM((LEVELS, 3, NCRM, 128), F32),
-            pltpu.SemaphoreType.DMA((6,)),
+            pltpu.SemaphoreType.DMA((4,)),
         ],
-    )(*(stay(x) for x in (state, forcing, order, waves, jnp.asarray(geometry()), moist)))
-    arrived = lax.all_to_all(outgoing, ("sec", "lat"), split_axis=0, concat_axis=0, tiled=True)
+    )(*(stay(x) for x in (waves, jnp.asarray(geometry()), order, moist)))
+    arrived, trig = lax.optimization_barrier((arrived, trig))
     rain = call(
         cloud_kernel,
         shape((TARGETS, 4, 128), F32),
@@ -500,10 +560,11 @@
             pltpu.VMEM((32, COLS), F32),
             pltpu.VMEM((ROWS, 128), F32),
             pltpu.VMEM((ROWS, 1, LONS), F32),
+            pltpu.VMEM((COLS, COLS), BF16),
             pltpu.SemaphoreType.DMA,
         ],
         (HBM, VMEM),
-    )(returned, hot, cols, trig)
+    )(returned, column, cols, trig)
     bands = lax.all_to_all(
         fourier.reshape(NL * NC, 4, 384), ("lat", "col"), split_axis=0, concat_axis=0, tiled=True
     )

time: 68.1 us -> 67.7 us (level)
  blocking collectives: 58.1 us -> 40.2 us
  starting transfers between devices: 0 us -> 9.39 us
  waiting for transfers between devices: 0 us -> 6.55 us
  Pallas kernels: 8.76 us -> 10.2 us
    all_to_all x1 -> x0, blocking collectives: 17.9 us -> none  [shards(): lax.all_to_all(outgoing, ('sec', 'lat'), split_axis=0, concat_axis=0, til...]
    all_to_all x0 -> x1, starting transfers between devices: none -> 9.39 us  [shards(): lax.all_to_all(outgoing, ('sec', 'lat'), split_axis=0, concat_axis=0, til...]
    all_to_all x0 -> x1, waiting for transfers between devices: none -> 6.55 us  [shards(): lax.all_to_all(outgoing, ('sec', 'lat'), split_axis=0, concat_axis=0, til...]
    pallas_call x1 -> x2, Pallas kernels: 3.51 us -> 4.98 us  [the longest x1 2.82 us: shards(): call(pack_kernel, (shape((TARGETS, 8, 128), F32), shape((2 * LEVELS, COLS...]
  transfers between devices with their start and end apart: 0 -> 1, of which waited for: 0 -> 1; matrix products, arithmetic and copies ran while one was open for 0% -> 0% of each run, Pallas kernels for 0% -> 3%
where the time goes in v5:
time: 67.7 us; the launch traced here: 67.1 us
  blocking collectives  40.2 us (59%)
  Pallas kernels  10.2 us (15%)
  starting transfers between devices  9.39 us (14%)
  waiting for transfers between devices  6.55 us (10%)
    all_to_all x1, blocking collectives, shards(): lax.all_to_all(fourier.reshape(NL * NC, 4, 384), ('lat', 'col'), split_ax...  27.6 us
    all_to_all x1, blocking collectives, shards(): lax.all_to_all(rain, ('sec', 'lat'), split_axis=0, concat_axis=0, tiled=T...  12.6 us
    all_to_all x1, starting transfers between devices, shards(): lax.all_to_all(outgoing, ('sec', 'lat'), split_axis=0, concat_axis=0, til...  9.39 us
    all_to_all x1, waiting for transfers between devices, shards(): lax.all_to_all(outgoing, ('sec', 'lat'), split_axis=0, concat_axis=0, til...  6.55 us
    pallas_call x1, Pallas kernels, shards(): call(pack_kernel, (shape((TARGETS, 8, 128), F32), shape((2 * LEVELS, COLS...  2.82 us
    pallas_call x1, Pallas kernels, shards(): call(table_kernel, (shape((2 * MMAX, 384), BF16), shape((SLOTS_OWN, MMAX,...  2.17 us
    pallas_call x1, Pallas kernels, shards(): call(update_kernel, (shape((ROWS, 1, LONS), F32), shape((NL, NC, 4, 384),...  2.05 us
    pallas_call x1, Pallas kernels, shards(): call(cloud_kernel, shape((TARGETS, 4, 128), F32), [VMEM] * 3, [pltpu.VMEM...  1.71 us
  transfers between devices with their start and end apart: 1, of which 1 were waited for; matrix products, arithmetic and copies ran while one was open for 0% of the time, Pallas kernels for 3%

profile of v5, /device:TPU:2, one launch (start us, length us, event | category | flops | bytes accessed | tf_op | source)
XLA Modules:
  0.0 67.1 jit_solution(14448213166619049966)
XLA Ops:
  0.6 2.8 %shard_map.77 = (f32[64,8,128]{2,1,0:T(8,128)}, f32[56,1152]{1,0:T(8,128)S(1)}) custom-call(f32[336,1,96]{2,1,0:T(1,128)} %bitcast.18, f32[336,1,96]{2,1,0:T(1,128)} %bitcast.19, s32[1,1152]{1,0:T(1,128)} %bitcast.21), custom_call_target="tpu_custom_call" | custom-call | tf_op jit(solution)/shard_map/pallas_call | solution.py:502
  3.5 9.4 %all-to-all-start = ((f32[64,8,128]{2,1,0:T(8,128)}), f32[64,8,128]{2,1,0:T(8,128)S(1)}, u32[]{:S(2)}, u32[]{:S(2)}) async-start(f32[64,8,128]{2,1,0:T(8,128)} %get-tuple-element.16), calls=%async_computation | async-start | bytes 524288 | tf_op jit(solution)/shard_map/all_to_all | solution.py:517
  12.8 2.2 %shard_map.78 = (bf16[256,384]{1,0:T(8,128)(2,1)S(1)}, bf16[8,128,512]{2,1,0:T(8,128)(2,1)S(1)}, f32[28,2,4,8,128]{4,3,2,1,0:T(8,128)S(1)}, f32[7,4,8,128]{3,2,1,0:T(8,128)S(1)}, f32[1152,128]{1,0:T(8,128)S(1)}) custom-call(s32[1,128]{1,0:T(1,128)} %bitcast.23, f32[4,256]{1,0:T(4,128)} %constant.2.clone.geom_hbm, s32[1,1152]{1,0:T(1,128)} %bitcast.22, ...), custom_call_target="tpu_custom_call" | custom-call | tf_op jit(solution)/shard_map/pallas_call | solution.py:518
  15.0 6.5 %all-to-all-done.got_ref = f32[64,8,128]{2,1,0:T(8,128)S(1)} async-done(((f32[64,8,128]{2,1,0:T(8,128)}), f32[64,8,128]{2,1,0:T(8,128)S(1)}, u32[]{:S(2)}, u32[]{:S(2)}) %all-to-all-start) | async-done | bytes 262176 | tf_op jit(solution)/shard_map/all_to_all | solution.py:517
  21.6 1.7 %shard_map.79 = f32[64,4,128]{2,1,0:T(4,128)S(1)} custom-call(f32[64,8,128]{2,1,0:T(8,128)S(1)} %all-to-all-done.got_ref, f32[28,2,4,8,128]{4,3,2,1,0:T(8,128)S(1)} %get-tuple-element.20.water_ref, f32[7,4,8,128]{3,2,1,0:T(8,128)S(1)} %get-tuple-element.21.tail_ref), custom_call_target="tpu_custom_call" | custom-call | tf_op jit(solution)/shard_map/pallas_call | solution.py:540
  23.3 12.6 %all_to_all.15.got_ref = f32[64,4,128]{2,1,0:T(4,128)S(1)} all-to-all(f32[64,4,128]{2,1,0:T(4,128)S(1)} %shard_map.79), channel_id=1, replica_groups=mesh['sec'=4,'lat'=16,'col'=4] {'sec','lat'}, dimensions={0} | all-to-all | bytes 262144 | tf_op jit(solution)/shard_map/all_to_all | solution.py:554
  35.9 2.0 %shard_map.80 = (f32[336,1,96]{2,1,0:T(1,128)}, f32[16,4,4,384]{3,2,1,0:T(4,128)S(1)}) custom-call(f32[64,4,128]{2,1,0:T(4,128)S(1)} %all_to_all.15.got_ref, f32[1152,128]{1,0:T(8,128)S(1)} %get-tuple-element.22.column_ref, f32[56,1152]{1,0:T(8,128)S(1)} %get-tuple-element.23.cols_ref, bf16[256,384]{1,0:T(8,128)(2,1)S(1)} %get-tuple-element.24.trig_ref), custom_call_target="tpu_custom_call" | custom-call | tf_op jit(solution)/shard_map/pallas_call | solution.py:555
  37.9 27.6 %all_to_all.16 = f32[64,4,384]{2,1,0:T(4,128)S(1)} all-to-all(f32[64,4,384]{2,1,0:T(4,128)S(1)} %bitcast.16), channel_id=1, replica_groups=mesh['sec'=4,'lat'=16,'col'=4] {'lat','col'}, dimensions={0} | all-to-all | bytes 786432 | tf_op jit(solution)/shard_map/all_to_all | solution.py:568
  65.6 1.5 %shard_map.81 = f32[7,8,2,128]{3,2,1,0:T(2,128)} custom-call(f32[16,4,4,384]{3,2,1,0:T(4,128)S(1)} %bitcast.15, bf16[8,128,512]{2,1,0:T(8,128)(2,1)S(1)} %get-tuple-element.27.weight_ref), custom_call_target="tpu_custom_call" | custom-call | tf_op jit(solution)/shard_map/pallas_call | solution.py:571
Async XLA Ops:
  3.5 18.1 %all-to-all-start = ((f32[64,8,128]{2,1,0:T(8,128)}), f32[64,8,128]{2,1,0:T(8,128)S(1)}, u32[]{:S(2)}, u32[]{:S(2)}) async-start(f32[64,8,128]{2,1,0:T(8,128)} %get-tuple-element.16), calls=%async_computation | async-start | bytes 524288 | tf_op jit(solution)/shard_map/all_to_all | solution.py:517

commit v6 on v5

--- a/solution.py
+++ b/solution.py
@@ -17,6 +17,7 @@
 BAND = 12
 LONS = 96
 COLS = BAND * LONS
+WIDE = BAND * 128
 ROWS = LEVELS * BAND
 TARGETS = 64
 PER = 18
@@ -49,10 +50,15 @@
     return lax.broadcasted_iota(jnp.int32, shape, 1)
 
 
+def widened(order):
+    order = order.astype(F32)
+    return order + 32.0 * jnp.floor((order + 0.5) * (1.0 / LONS))
+
+
 def fill_one_hot(order_ref, hot_ref):
-    order = order_ref[...]
-    step = 96
-    for c in range(0, COLS, step):
+    order = widened(order_ref[...]).astype(jnp.int32)
+    step = 128
+    for c in range(0, WIDE, step):
         ids = lax.broadcasted_iota(jnp.int32, (step, COLS), 0) + c
         hot_ref[c : c + step, :] = jnp.where(ids == order, 1.0, 0.0).astype(BF16)
 
@@ -112,9 +118,10 @@
     for s in range(SLOTS_OWN):
         for h in range(2):
             hi, lo = split2(poly_ref[h, pl.ds(s, MMAX, stride=8), :])
-            for part, block in ((hi, 0), (lo, 2)):
-                at = (block + h) * 128
-                weight_ref[s, :, at : at + 128] = part
+            size = min(128, NLAT - h * 128)
+            for part, base in ((hi, 0), (lo, NLAT)):
+                at = base + h * 128
+                weight_ref[s, :, at : at + size] = part[:, :size]
 
 
 def arrange_moisture(moist_ref, level_ref, water_ref, tail_ref):
@@ -172,7 +179,7 @@
     trig_rows(orders, trig_ref)
     first = pl.multiple_of(lax.axis_index("lat") * SLOTS_OWN, SLOTS_OWN)
     legendre_rows(orders_ref[pl.ds(first, SLOTS_OWN), :], geom_ref, poly_ref, weight_ref)
-    order = order_ref[...].astype(F32)
+    order = widened(order_ref[...])
     for v in range(COLS // 128):
         at = slice(v * 128, v * 128 + 128)
         column_ref[at, :] = jnp.broadcast_to(order[:, at], (128, 128)).T
@@ -193,29 +200,26 @@
     out_ref,
     sems,
 ):
-    half = ROWS // 2
-    pairs = [(order_hbm, order_ref)]
-    for part in (pl.ds(0, half), pl.ds(half, half)):
-        pairs.append((state_hbm.at[part], state_ref.at[part]))
-        pairs.append((force_hbm.at[part], force_ref.at[part]))
+    pairs = ((order_hbm, order_ref), (state_hbm, state_ref), (force_hbm, force_ref))
     loads = [pltpu.make_async_copy(src, dst, sems.at[n]) for n, (src, dst) in enumerate(pairs)]
     for load in loads:
         load.start()
     loads[0].wait()
     fill_one_hot(order_ref, hot_ref)
-    for load in loads[1:]:
-        load.wait()
+    loads[1].wait()
+    loads[2].wait()
+    blank = jnp.zeros((LEVELS, 128 - LONS), F32)
     for ref, base in ((state_ref, 0), (force_ref, LEVELS)):
         rows = ref[...].reshape(LEVELS, BAND, LONS)
         for b in range(BAND):
-            cols_ref[base : base + LEVELS, b * LONS : (b + 1) * LONS] = rows[:, b, :]
+            piece = jnp.concatenate((rows[:, b, :], blank), axis=1)
+            cols_ref[base : base + LEVELS, b * 128 : (b + 1) * 128] = piece
     hi, lo = split2(cols_ref[...])
     both = jnp.concatenate((hi, lo), axis=0)
     got = jnp.dot(both, hot_ref[...], preferred_element_type=F32)
     got = got[: 2 * LEVELS] + got[2 * LEVELS :]
     lane = lanes_of((8, 128))
     groups = 2 * LEVELS // 8
-    saves = []
     for t in range(TARGETS):
         v, off = divmod(t * PER, 128)
         tile = None
@@ -229,13 +233,9 @@
                 src = pltpu.roll(src, shift, 1)
             tile = src if tile is None else jnp.where(lane >= q * PER, src, tile)
         out_ref[t] = tile
-        if t % 16 == 15:
-            part = pl.ds(t - 15, 16)
-            save = pltpu.make_async_copy(out_ref.at[part], out_hbm.at[part], sems.at[5 + t // 16])
-            save.start()
-            saves.append(save)
-    for save in saves:
-        save.wait()
+    save = pltpu.make_async_copy(out_ref, out_hbm, sems.at[3])
+    save.start()
+    save.wait()
 
 
 def gather_lanes(tile_of, q_list, first, count, width, store):
@@ -375,19 +375,17 @@
     column_ref,
     cols_ref,
     trig_ref,
-    out_hbm,
+    out_ref,
     four_ref,
     slots_ref,
     rows_ref,
-    out_ref,
     hot_ref,
-    sem,
 ):
     lane = lanes_of((128, 128)).astype(F32)
     for v in range(COLS // 128):
         rows = slice(v * 128, v * 128 + 128)
         column = column_ref[rows, :]
-        for c in range(COLS // 128):
+        for c in range(WIDE // 128):
             hot = jnp.where(lane + float(c * 128) == column, 1.0, 0.0)
             hot_ref[rows, c * 128 : c * 128 + 128] = hot.astype(BF16)
 
@@ -412,14 +410,10 @@
     scale = jnp.where(sec < 2, -1.0 / NSUB, 0.0).astype(F32)
     now = cols_ref[0:LEVELS]
     now = now + (cols_ref[LEVELS : 2 * LEVELS] + rain * (add + scale * now))
-    blank = jnp.zeros((LEVELS, 128 - LONS), F32)
     for b in range(BAND):
-        piece = jnp.concatenate((now[:, b * LONS : (b + 1) * LONS], blank), axis=1)
-        rows_ref[pl.ds(b, LEVELS, stride=BAND), :] = piece
+        rows_ref[pl.ds(b, LEVELS, stride=BAND), :] = now[:, b * 128 : (b + 1) * 128]
     rows = rows_ref[...]
     out_ref[...] = rows[:, :LONS].reshape(ROWS, 1, LONS)
-    save = pltpu.make_async_copy(out_ref, out_hbm, sem)
-    save.start()
     hi, lo = split2(rows)
     dims = (((1,), (1,)), ((), ()))
     parts = jnp.concatenate((hi, lo, hi), axis=1)
@@ -429,10 +423,13 @@
     for j in range(NC):
         pieces = [out[g * 64 : g * 64 + 64, j * width : (j + 1) * width] for g in range(4)]
         four_ref[:, j] = jnp.concatenate(pieces + [blank], axis=1).reshape(NL, 4, 384)
-    save.wait()
-
-
-def legendre_kernel(got_ref, weight_ref, out_hbm, band_ref, out_ref, sems):
+
+
+def legendre_kernel(
+    got_ref, weight_ref, state_ref, out_hbm, state_hbm, band_ref, out_ref, sems
+):
+    saves = [pltpu.make_async_copy(state_ref, state_hbm, sems.at[2])]
+    saves[0].start()
     width = LEV_OWN * BAND
     band_ref[1] = jnp.zeros_like(band_ref[1])
     for i in range(NL):
@@ -447,13 +444,12 @@
             if first < BAND:
                 band_ref[h + 1, row, 0 : BAND - first] = piece[:, first:]
     dims = (((1,), (1,)), ((), ()))
-    saves = []
     for s in range(SLOTS_OWN):
         rows = [band_ref[h, pl.ds(s, 2 * LEV_OWN, stride=8), :] for h in range(2)]
-        hi, lo = split2(jnp.concatenate(rows, axis=1))
+        hi, lo = split2(jnp.concatenate(rows, axis=1)[:, :NLAT])
         parts = jnp.concatenate((hi, hi), axis=1)
         out = lax.dot_general(parts, weight_ref[s], dims, preferred_element_type=F32)
-        out = out + lax.dot_general(lo, weight_ref[s, :, 0:256], dims, preferred_element_type=F32)
+        out = out + lax.dot_general(lo, weight_ref[s, :, 0:NLAT], dims, preferred_element_type=F32)
         out_ref[:, s, :, :] = out.reshape(LEV_OWN, 2, MMAX)
         if s % 4 == 3:
             part = pl.ds(s - 3, 4)
@@ -501,15 +497,15 @@
     waves = wave_table.reshape(1, MMAX)
     outgoing, cols = call(
         pack_kernel,
-        (shape((TARGETS, 8, 128), F32), shape((2 * LEVELS, COLS), F32)),
+        (shape((TARGETS, 8, 128), F32), shape((2 * LEVELS, WIDE), F32)),
         [HBM] * 3,
         [
             pltpu.VMEM((ROWS, 1, LONS), F32),
             pltpu.VMEM((ROWS, 1, LONS), F32),
             pltpu.VMEM((1, COLS), jnp.int32),
-            pltpu.VMEM((COLS, COLS), BF16),
+            pltpu.VMEM((WIDE, COLS), BF16),
             pltpu.VMEM((TARGETS, 8, 128), F32),
-            pltpu.SemaphoreType.DMA((9,)),
+            pltpu.SemaphoreType.DMA((4,)),
         ],
         (HBM, VMEM),
     )(*(stay(x) for x in (state, forcing, order)))
@@ -519,7 +515,7 @@
         table_kernel,
         (
             shape((2 * MMAX, 384), BF16),
-            shape((SLOTS_OWN, MMAX, 512), BF16),
+            shape((SLOTS_OWN, MMAX, 2 * NLAT), BF16),
             shape((LEVELS, 2, 4, 8, 128), F32),
             shape((LEVELS // 4, 4, 8, 128), F32),
             shape((COLS, 128), F32),
@@ -559,26 +555,23 @@
         [
             pltpu.VMEM((32, COLS), F32),
             pltpu.VMEM((ROWS, 128), F32),
-            pltpu.VMEM((ROWS, 1, LONS), F32),
-            pltpu.VMEM((COLS, COLS), BF16),
-            pltpu.SemaphoreType.DMA,
+            pltpu.VMEM((COLS, WIDE), BF16),
         ],
-        (HBM, VMEM),
     )(returned, column, cols, trig)
     bands = lax.all_to_all(
         fourier.reshape(NL * NC, 4, 384), ("lat", "col"), split_axis=0, concat_axis=0, tiled=True
     )
-    spectral = call(
+    spectral, updated = call(
         legendre_kernel,
-        shape((LEV_OWN, SLOTS_OWN, 2, MMAX), F32),
-        [VMEM] * 2,
+        (shape((LEV_OWN, SLOTS_OWN, 2, MMAX), F32), shape((ROWS, 1, LONS), F32)),
+        [VMEM] * 3,
         [
             pltpu.VMEM((2, LEV_OWN * 16, 128), F32),
             pltpu.VMEM((LEV_OWN, SLOTS_OWN, 2, MMAX), F32),
-            pltpu.SemaphoreType.DMA((2,)),
+            pltpu.SemaphoreType.DMA((3,)),
         ],
-        HBM,
-    )(bands.reshape(NL, NC, 4, 384), weights)
+        (HBM, HBM),
+    )(bands.reshape(NL, NC, 4, 384), weights, updated)
     new_state = updated.reshape(1, LEVELS, BAND, 1, LONS).transpose(0, 3, 1, 2, 4)
     return new_state, spectral[None, None]
 

time: 67.7 us -> 68 us (level)
  transfers between devices with their start and end apart: 1 -> 1, of which waited for: 1 -> 1; matrix products, arithmetic and copies ran while one was open for 0% -> 0% of each run, Pallas kernels for 3% -> 4%
where the time goes in v6:
time: 68 us; the launch traced here: 67.3 us
  blocking collectives  40.2 us (59%)
  Pallas kernels  10.8 us (16%)
  starting transfers between devices  9.37 us (14%)
  waiting for transfers between devices  6.23 us (9%)
    all_to_all x1, blocking collectives, shards(): lax.all_to_all(fourier.reshape(NL * NC, 4, 384), ('lat', 'col'), split_ax...  27.6 us
    all_to_all x1, blocking collectives, shards(): lax.all_to_all(rain, ('sec', 'lat'), split_axis=0, concat_axis=0, tiled=T...  12.6 us
    all_to_all x1, starting transfers between devices, shards(): lax.all_to_all(outgoing, ('sec', 'lat'), split_axis=0, concat_axis=0, til...  9.37 us
    all_to_all x1, waiting for transfers between devices, shards(): lax.all_to_all(outgoing, ('sec', 'lat'), split_axis=0, concat_axis=0, til...  6.23 us
    pallas_call x1, Pallas kernels, shards(): call(pack_kernel, (shape((TARGETS, 8, 128), F32), shape((2 * LEVELS, WIDE...  3.12 us
    pallas_call x1, Pallas kernels, shards(): call(table_kernel, (shape((2 * MMAX, 384), BF16), shape((SLOTS_OWN, MMAX,...  2.48 us
    pallas_call x1, Pallas kernels, shards(): call(update_kernel, (shape((ROWS, 1, LONS), F32), shape((NL, NC, 4, 384),...  1.97 us
    pallas_call x1, Pallas kernels, shards(): call(cloud_kernel, shape((TARGETS, 4, 128), F32), [VMEM] * 3, [pltpu.VMEM...  1.71 us
  transfers between devices with their start and end apart: 1, of which 1 were waited for; matrix products, arithmetic and copies ran while one was open for 0% of the time, Pallas kernels for 4%

profile of v6, /device:TPU:2, one launch (start us, length us, event | category | flops | bytes accessed | tf_op | source)
XLA Modules:
  0.0 67.3 jit_solution(5242474348221809196)
XLA Ops:
  0.6 3.1 %shard_map.77 = (f32[64,8,128]{2,1,0:T(8,128)}, f32[56,1536]{1,0:T(8,128)S(1)}) custom-call(f32[336,1,96]{2,1,0:T(1,128)} %bitcast.18, f32[336,1,96]{2,1,0:T(1,128)} %bitcast.19, s32[1,1152]{1,0:T(1,128)} %bitcast.20), custom_call_target="tpu_custom_call" | custom-call | tf_op jit(solution)/shard_map/pallas_call | solution.py:498
  3.8 9.4 %all-to-all-start = ((f32[64,8,128]{2,1,0:T(8,128)}), f32[64,8,128]{2,1,0:T(8,128)S(1)}, u32[]{:S(2)}, u32[]{:S(2)}) async-start(f32[64,8,128]{2,1,0:T(8,128)} %get-tuple-element.18), calls=%async_computation | async-start | bytes 524288 | tf_op jit(solution)/shard_map/all_to_all | solution.py:513
  13.1 2.5 %shard_map.78 = (bf16[256,384]{1,0:T(8,128)(2,1)S(1)}, bf16[8,128,384]{2,1,0:T(8,128)(2,1)S(1)}, f32[28,2,4,8,128]{4,3,2,1,0:T(8,128)S(1)}, f32[7,4,8,128]{3,2,1,0:T(8,128)S(1)}, f32[1152,128]{1,0:T(8,128)S(1)}) custom-call(s32[1,128]{1,0:T(1,128)} %bitcast.22, f32[4,256]{1,0:T(4,128)} %constant.2.clone.geom_hbm, s32[1,1152]{1,0:T(1,128)} %bitcast.21, ...), custom_call_target="tpu_custom_call" | custom-call | tf_op jit(solution)/shard_map/pallas_call | solution.py:514
  15.6 6.2 %all-to-all-done.got_ref = f32[64,8,128]{2,1,0:T(8,128)S(1)} async-done(((f32[64,8,128]{2,1,0:T(8,128)}), f32[64,8,128]{2,1,0:T(8,128)S(1)}, u32[]{:S(2)}, u32[]{:S(2)}) %all-to-all-start) | async-done | bytes 262176 | tf_op jit(solution)/shard_map/all_to_all | solution.py:513
  21.9 1.7 %shard_map.79 = f32[64,4,128]{2,1,0:T(4,128)S(1)} custom-call(f32[64,8,128]{2,1,0:T(8,128)S(1)} %all-to-all-done.got_ref, f32[28,2,4,8,128]{4,3,2,1,0:T(8,128)S(1)} %get-tuple-element.22.water_ref, f32[7,4,8,128]{3,2,1,0:T(8,128)S(1)} %get-tuple-element.23.tail_ref), custom_call_target="tpu_custom_call" | custom-call | tf_op jit(solution)/shard_map/pallas_call | solution.py:536
  23.6 12.6 %all_to_all.15.got_ref = f32[64,4,128]{2,1,0:T(4,128)S(1)} all-to-all(f32[64,4,128]{2,1,0:T(4,128)S(1)} %shard_map.79), channel_id=1, replica_groups=mesh['sec'=4,'lat'=16,'col'=4] {'sec','lat'}, dimensions={0} | all-to-all | bytes 262144 | tf_op jit(solution)/shard_map/all_to_all | solution.py:550
  36.2 2.0 %shard_map.80 = (f32[336,1,96]{2,1,0:T(1,128)S(1)}, f32[16,4,4,384]{3,2,1,0:T(4,128)S(1)}) custom-call(f32[64,4,128]{2,1,0:T(4,128)S(1)} %all_to_all.15.got_ref, f32[1152,128]{1,0:T(8,128)S(1)} %get-tuple-element.24.column_ref, f32[56,1536]{1,0:T(8,128)S(1)} %get-tuple-element.25.cols_ref, bf16[256,384]{1,0:T(8,128)(2,1)S(1)} %get-tuple-element.26.trig_ref), custom_call_target="tpu_custom_call" | custom-call | tf_op jit(solution)/shard_map/pallas_call | solution.py:551
  38.2 27.6 %all_to_all.16 = f32[64,4,384]{2,1,0:T(4,128)S(1)} all-to-all(f32[64,4,384]{2,1,0:T(4,128)S(1)} %bitcast.16), channel_id=1, replica_groups=mesh['sec'=4,'lat'=16,'col'=4] {'lat','col'}, dimensions={0} | all-to-all | bytes 786432 | tf_op jit(solution)/shard_map/all_to_all | solution.py:561
  65.8 1.5 %shard_map.81 = (f32[7,8,2,128]{3,2,1,0:T(2,128)}, f32[336,1,96]{2,1,0:T(1,128)}) custom-call(f32[16,4,4,384]{3,2,1,0:T(4,128)S(1)} %bitcast.15, bf16[8,128,384]{2,1,0:T(8,128)(2,1)S(1)} %get-tuple-element.28.weight_ref, f32[336,1,96]{2,1,0:T(1,128)S(1)} %get-tuple-element.29.state_ref), custom_call_target="tpu_custom_call" | custom-call | tf_op jit(solution)/shard_map/pallas_call | solution.py:564
Async XLA Ops:
  3.8 18.1 %all-to-all-start = ((f32[64,8,128]{2,1,0:T(8,128)}), f32[64,8,128]{2,1,0:T(8,128)S(1)}, u32[]{:S(2)}, u32[]{:S(2)}) async-start(f32[64,8,128]{2,1,0:T(8,128)} %get-tuple-element.18), calls=%async_computation | async-start | bytes 524288 | tf_op jit(solution)/shard_map/all_to_all | solution.py:513

commit v7 on v6

--- a/solution.py
+++ b/solution.py
@@ -17,7 +17,6 @@
 BAND = 12
 LONS = 96
 COLS = BAND * LONS
-WIDE = BAND * 128
 ROWS = LEVELS * BAND
 TARGETS = 64
 PER = 18
@@ -50,15 +49,10 @@
     return lax.broadcasted_iota(jnp.int32, shape, 1)
 
 
-def widened(order):
-    order = order.astype(F32)
-    return order + 32.0 * jnp.floor((order + 0.5) * (1.0 / LONS))
-
-
 def fill_one_hot(order_ref, hot_ref):
-    order = widened(order_ref[...]).astype(jnp.int32)
-    step = 128
-    for c in range(0, WIDE, step):
+    order = order_ref[...]
+    step = 96
+    for c in range(0, COLS, step):
         ids = lax.broadcasted_iota(jnp.int32, (step, COLS), 0) + c
         hot_ref[c : c + step, :] = jnp.where(ids == order, 1.0, 0.0).astype(BF16)
 
@@ -179,7 +173,7 @@
     trig_rows(orders, trig_ref)
     first = pl.multiple_of(lax.axis_index("lat") * SLOTS_OWN, SLOTS_OWN)
     legendre_rows(orders_ref[pl.ds(first, SLOTS_OWN), :], geom_ref, poly_ref, weight_ref)
-    order = widened(order_ref[...])
+    order = order_ref[...].astype(F32)
     for v in range(COLS // 128):
         at = slice(v * 128, v * 128 + 128)
         column_ref[at, :] = jnp.broadcast_to(order[:, at], (128, 128)).T
@@ -208,12 +202,10 @@
     fill_one_hot(order_ref, hot_ref)
     loads[1].wait()
     loads[2].wait()
-    blank = jnp.zeros((LEVELS, 128 - LONS), F32)
     for ref, base in ((state_ref, 0), (force_ref, LEVELS)):
         rows = ref[...].reshape(LEVELS, BAND, LONS)
         for b in range(BAND):
-            piece = jnp.concatenate((rows[:, b, :], blank), axis=1)
-            cols_ref[base : base + LEVELS, b * 128 : (b + 1) * 128] = piece
+            cols_ref[base : base + LEVELS, b * LONS : (b + 1) * LONS] = rows[:, b, :]
     hi, lo = split2(cols_ref[...])
     both = jnp.concatenate((hi, lo), axis=0)
     got = jnp.dot(both, hot_ref[...], preferred_element_type=F32)
@@ -385,7 +377,7 @@
     for v in range(COLS // 128):
         rows = slice(v * 128, v * 128 + 128)
         column = column_ref[rows, :]
-        for c in range(WIDE // 128):
+        for c in range(COLS // 128):
             hot = jnp.where(lane + float(c * 128) == column, 1.0, 0.0)
             hot_ref[rows, c * 128 : c * 128 + 128] = hot.astype(BF16)
 
@@ -410,8 +402,10 @@
     scale = jnp.where(sec < 2, -1.0 / NSUB, 0.0).astype(F32)
     now = cols_ref[0:LEVELS]
     now = now + (cols_ref[LEVELS : 2 * LEVELS] + rain * (add + scale * now))
+    blank = jnp.zeros((LEVELS, 128 - LONS), F32)
     for b in range(BAND):
-        rows_ref[pl.ds(b, LEVELS, stride=BAND), :] = now[:, b * 128 : (b + 1) * 128]
+        piece = jnp.concatenate((now[:, b * LONS : (b + 1) * LONS], blank), axis=1)
+        rows_ref[pl.ds(b, LEVELS, stride=BAND), :] = piece
     rows = rows_ref[...]
     out_ref[...] = rows[:, :LONS].reshape(ROWS, 1, LONS)
     hi, lo = split2(rows)
@@ -497,13 +491,13 @@
     waves = wave_table.reshape(1, MMAX)
     outgoing, cols = call(
         pack_kernel,
-        (shape((TARGETS, 8, 128), F32), shape((2 * LEVELS, WIDE), F32)),
+        (shape((TARGETS, 8, 128), F32), shape((2 * LEVELS, COLS), F32)),
         [HBM] * 3,
         [
             pltpu.VMEM((ROWS, 1, LONS), F32),
             pltpu.VMEM((ROWS, 1, LONS), F32),
             pltpu.VMEM((1, COLS), jnp.int32),
-            pltpu.VMEM((WIDE, COLS), BF16),
+            pltpu.VMEM((COLS, COLS), BF16),
             pltpu.VMEM((TARGETS, 8, 128), F32),
             pltpu.SemaphoreType.DMA((4,)),
         ],
@@ -555,7 +549,7 @@
         [
             pltpu.VMEM((32, COLS), F32),
             pltpu.VMEM((ROWS, 128), F32),
-            pltpu.VMEM((COLS, WIDE), BF16),
+            pltpu.VMEM((COLS, COLS), BF16),
         ],
     )(returned, column, cols, trig)
     bands = lax.all_to_all(

time: 68 us -> 67.5 us (level)
  no operation moved by 1% of the time
where the time goes in v7:
time: 67.5 us; the launch traced here: 67 us
  blocking collectives  40.3 us (60%)
  Pallas kernels  10.4 us (15%)
  starting transfers between devices  9.39 us (14%)
  waiting for transfers between devices  6.23 us (9%)
    all_to_all x1, blocking collectives, shards(): lax.all_to_all(fourier.reshape(NL * NC, 4, 384), ('lat', 'col'), split_ax...  27.7 us
    all_to_all x1, blocking collectives, shards(): lax.all_to_all(rain, ('sec', 'lat'), split_axis=0, concat_axis=0, tiled=T...  12.6 us
    all_to_all x1, starting transfers between devices, shards(): lax.all_to_all(outgoing, ('sec', 'lat'), split_axis=0, concat_axis=0, til...  9.39 us
    all_to_all x1, waiting for transfers between devices, shards(): lax.all_to_all(outgoing, ('sec', 'lat'), split_axis=0, concat_axis=0, til...  6.23 us
    pallas_call x1, Pallas kernels, shards(): call(pack_kernel, (shape((TARGETS, 8, 128), F32), shape((2 * LEVELS, COLS...  2.85 us
    pallas_call x1, Pallas kernels, shards(): call(table_kernel, (shape((2 * MMAX, 384), BF16), shape((SLOTS_OWN, MMAX,...  2.48 us
    pallas_call x1, Pallas kernels, shards(): call(update_kernel, (shape((ROWS, 1, LONS), F32), shape((NL, NC, 4, 384),...  1.8 us
    pallas_call x1, Pallas kernels, shards(): call(cloud_kernel, shape((TARGETS, 4, 128), F32), [VMEM] * 3, [pltpu.VMEM...  1.71 us
  transfers between devices with their start and end apart: 1, of which 1 were waited for; matrix products, arithmetic and copies ran while one was open for 0% of the time, Pallas kernels for 4%

profile of v7, /device:TPU:2, one launch (start us, length us, event | category | flops | bytes accessed | tf_op | source)
XLA Modules:
  0.0 67.0 jit_solution(15662075672868323615)
XLA Ops:
  0.6 2.8 %shard_map.77 = (f32[64,8,128]{2,1,0:T(8,128)}, f32[56,1152]{1,0:T(8,128)S(1)}) custom-call(f32[336,1,96]{2,1,0:T(1,128)} %bitcast.18, f32[336,1,96]{2,1,0:T(1,128)} %bitcast.19, s32[1,1152]{1,0:T(1,128)} %bitcast.20), custom_call_target="tpu_custom_call" | custom-call | tf_op jit(solution)/shard_map/pallas_call | solution.py:492
  3.5 9.4 %all-to-all-start = ((f32[64,8,128]{2,1,0:T(8,128)}), f32[64,8,128]{2,1,0:T(8,128)S(1)}, u32[]{:S(2)}, u32[]{:S(2)}) async-start(f32[64,8,128]{2,1,0:T(8,128)} %get-tuple-element.18), calls=%async_computation | async-start | bytes 524288 | tf_op jit(solution)/shard_map/all_to_all | solution.py:507
  12.9 2.5 %shard_map.78 = (bf16[256,384]{1,0:T(8,128)(2,1)S(1)}, bf16[8,128,384]{2,1,0:T(8,128)(2,1)S(1)}, f32[28,2,4,8,128]{4,3,2,1,0:T(8,128)S(1)}, f32[7,4,8,128]{3,2,1,0:T(8,128)S(1)}, f32[1152,128]{1,0:T(8,128)S(1)}) custom-call(s32[1,128]{1,0:T(1,128)} %bitcast.22, f32[4,256]{1,0:T(4,128)} %constant.2.clone.geom_hbm, s32[1,1152]{1,0:T(1,128)} %bitcast.21, ...), custom_call_target="tpu_custom_call" | custom-call | tf_op jit(solution)/shard_map/pallas_call | solution.py:508
  15.4 6.2 %all-to-all-done.got_ref = f32[64,8,128]{2,1,0:T(8,128)S(1)} async-done(((f32[64,8,128]{2,1,0:T(8,128)}), f32[64,8,128]{2,1,0:T(8,128)S(1)}, u32[]{:S(2)}, u32[]{:S(2)}) %all-to-all-start) | async-done | bytes 262176 | tf_op jit(solution)/shard_map/all_to_all | solution.py:507
  21.6 1.7 %shard_map.79 = f32[64,4,128]{2,1,0:T(4,128)S(1)} custom-call(f32[64,8,128]{2,1,0:T(8,128)S(1)} %all-to-all-done.got_ref, f32[28,2,4,8,128]{4,3,2,1,0:T(8,128)S(1)} %get-tuple-element.22.water_ref, f32[7,4,8,128]{3,2,1,0:T(8,128)S(1)} %get-tuple-element.23.tail_ref), custom_call_target="tpu_custom_call" | custom-call | tf_op jit(solution)/shard_map/pallas_call | solution.py:530
  23.3 12.6 %all_to_all.15.got_ref = f32[64,4,128]{2,1,0:T(4,128)S(1)} all-to-all(f32[64,4,128]{2,1,0:T(4,128)S(1)} %shard_map.79), channel_id=1, replica_groups=mesh['sec'=4,'lat'=16,'col'=4] {'sec','lat'}, dimensions={0} | all-to-all | bytes 262144 | tf_op jit(solution)/shard_map/all_to_all | solution.py:544
  35.9 1.8 %shard_map.80 = (f32[336,1,96]{2,1,0:T(1,128)S(1)}, f32[16,4,4,384]{3,2,1,0:T(4,128)S(1)}) custom-call(f32[64,4,128]{2,1,0:T(4,128)S(1)} %all_to_all.15.got_ref, f32[1152,128]{1,0:T(8,128)S(1)} %get-tuple-element.24.column_ref, f32[56,1152]{1,0:T(8,128)S(1)} %get-tuple-element.25.cols_ref, bf16[256,384]{1,0:T(8,128)(2,1)S(1)} %get-tuple-element.26.trig_ref), custom_call_target="tpu_custom_call" | custom-call | tf_op jit(solution)/shard_map/pallas_call | solution.py:545
  37.7 27.7 %all_to_all.16 = f32[64,4,384]{2,1,0:T(4,128)S(1)} all-to-all(f32[64,4,384]{2,1,0:T(4,128)S(1)} %bitcast.16), channel_id=1, replica_groups=mesh['sec'=4,'lat'=16,'col'=4] {'lat','col'}, dimensions={0} | all-to-all | bytes 786432 | tf_op jit(solution)/shard_map/all_to_all | solution.py:555
  65.5 1.5 %shard_map.81 = (f32[7,8,2,128]{3,2,1,0:T(2,128)}, f32[336,1,96]{2,1,0:T(1,128)}) custom-call(f32[16,4,4,384]{3,2,1,0:T(4,128)S(1)} %bitcast.15, bf16[8,128,384]{2,1,0:T(8,128)(2,1)S(1)} %get-tuple-element.28.weight_ref, f32[336,1,96]{2,1,0:T(1,128)S(1)} %get-tuple-element.29.state_ref), custom_call_target="tpu_custom_call" | custom-call | tf_op jit(solution)/shard_map/pallas_call | solution.py:558
Async XLA Ops:
  3.5 18.1 %all-to-all-start = ((f32[64,8,128]{2,1,0:T(8,128)}), f32[64,8,128]{2,1,0:T(8,128)S(1)}, u32[]{:S(2)}, u32[]{:S(2)}) async-start(f32[64,8,128]{2,1,0:T(8,128)} %get-tuple-element.18), calls=%async_computation | async-start | bytes 524288 | tf_op jit(solution)/shard_map/all_to_all | solution.py:507

commit v8 on v7

--- a/solution.py
+++ b/solution.py
@@ -416,7 +416,7 @@
     blank = jnp.zeros((NL * 4, 384 - 4 * width), F32)
     for j in range(NC):
         pieces = [out[g * 64 : g * 64 + 64, j * width : (j + 1) * width] for g in range(4)]
-        four_ref[:, j] = jnp.concatenate(pieces + [blank], axis=1).reshape(NL, 4, 384)
+        four_ref[j] = jnp.concatenate(pieces + [blank], axis=1).reshape(NL, 4, 384)
 
 
 def legendre_kernel(
@@ -427,7 +427,7 @@
     width = LEV_OWN * BAND
     band_ref[1] = jnp.zeros_like(band_ref[1])
     for i in range(NL):
-        part = (got_ref[i, 0] + got_ref[i, 1]) + (got_ref[i, 2] + got_ref[i, 3])
+        part = (got_ref[0, i] + got_ref[1, i]) + (got_ref[2, i] + got_ref[3, i])
         bands = jnp.concatenate([part[:, g * width : (g + 1) * width] for g in range(4)], axis=0)
         h, at = divmod(i * BAND, 128)
         first = min(BAND, 128 - at)
@@ -544,7 +544,7 @@
     returned = lax.all_to_all(rain, ("sec", "lat"), split_axis=0, concat_axis=0, tiled=True)
     updated, fourier = call(
         update_kernel,
-        (shape((ROWS, 1, LONS), F32), shape((NL, NC, 4, 384), F32)),
+        (shape((ROWS, 1, LONS), F32), shape((NC, NL, 4, 384), F32)),
         [VMEM] * 4,
         [
             pltpu.VMEM((32, COLS), F32),
@@ -553,7 +553,7 @@
         ],
     )(returned, column, cols, trig)
     bands = lax.all_to_all(
-        fourier.reshape(NL * NC, 4, 384), ("lat", "col"), split_axis=0, concat_axis=0, tiled=True
+        fourier.reshape(NL * NC, 4, 384), ("col", "lat"), split_axis=0, concat_axis=0, tiled=True
     )
     spectral, updated = call(
         legendre_kernel,
@@ -565,7 +565,7 @@
             pltpu.SemaphoreType.DMA((3,)),
         ],
         (HBM, HBM),
-    )(bands.reshape(NL, NC, 4, 384), weights, updated)
+    )(bands.reshape(NC, NL, 4, 384), weights, updated)
     new_state = updated.reshape(1, LEVELS, BAND, 1, LONS).transpose(0, 3, 1, 2, 4)
     return new_state, spectral[None, None]
 

time: 67.5 us -> 66.5 us (0.985)
  blocking collectives: 40.3 us -> 39.2 us
    all_to_all x1, blocking collectives: 27.7 us -> 26.6 us  [shards(): lax.all_to_all(fourier.reshape(NL * NC, 4, 384), ('col', 'lat'), split_ax...]
where the time goes in v8:
time: 66.5 us; the launch traced here: 65.9 us
  blocking collectives  39.2 us (59%)
  Pallas kernels  10.4 us (16%)
  starting transfers between devices  9.39 us (14%)
  waiting for transfers between devices  6.23 us (9%)
    all_to_all x1, blocking collectives, shards(): lax.all_to_all(fourier.reshape(NL * NC, 4, 384), ('col', 'lat'), split_ax...  26.6 us
    all_to_all x1, blocking collectives, shards(): lax.all_to_all(rain, ('sec', 'lat'), split_axis=0, concat_axis=0, tiled=T...  12.6 us
    all_to_all x1, starting transfers between devices, shards(): lax.all_to_all(outgoing, ('sec', 'lat'), split_axis=0, concat_axis=0, til...  9.39 us
    all_to_all x1, waiting for transfers between devices, shards(): lax.all_to_all(outgoing, ('sec', 'lat'), split_axis=0, concat_axis=0, til...  6.23 us
    pallas_call x1, Pallas kernels, shards(): call(pack_kernel, (shape((TARGETS, 8, 128), F32), shape((2 * LEVELS, COLS...  2.85 us
    pallas_call x1, Pallas kernels, shards(): call(table_kernel, (shape((2 * MMAX, 384), BF16), shape((SLOTS_OWN, MMAX,...  2.48 us
    pallas_call x1, Pallas kernels, shards(): call(update_kernel, (shape((ROWS, 1, LONS), F32), shape((NC, NL, 4, 384),...  1.8 us
    pallas_call x1, Pallas kernels, shards(): call(cloud_kernel, shape((TARGETS, 4, 128), F32), [VMEM] * 3, [pltpu.VMEM...  1.71 us
  transfers between devices with their start and end apart: 1, of which 1 were waited for; matrix products, arithmetic and copies ran while one was open for 0% of the time, Pallas kernels for 4%

profile of v8, /device:TPU:2, one launch (start us, length us, event | category | flops | bytes accessed | tf_op | source)
XLA Modules:
  0.0 65.9 jit_solution(15805955967752875232)
XLA Ops:
  0.6 2.8 %shard_map.77 = (f32[64,8,128]{2,1,0:T(8,128)}, f32[56,1152]{1,0:T(8,128)S(1)}) custom-call(f32[336,1,96]{2,1,0:T(1,128)} %bitcast.18, f32[336,1,96]{2,1,0:T(1,128)} %bitcast.19, s32[1,1152]{1,0:T(1,128)} %bitcast.20), custom_call_target="tpu_custom_call" | custom-call | tf_op jit(solution)/shard_map/pallas_call | solution.py:492
  3.5 9.4 %all-to-all-start = ((f32[64,8,128]{2,1,0:T(8,128)}), f32[64,8,128]{2,1,0:T(8,128)S(1)}, u32[]{:S(2)}, u32[]{:S(2)}) async-start(f32[64,8,128]{2,1,0:T(8,128)} %get-tuple-element.18), calls=%async_computation | async-start | bytes 524288 | tf_op jit(solution)/shard_map/all_to_all | solution.py:507
  12.9 2.5 %shard_map.78 = (bf16[256,384]{1,0:T(8,128)(2,1)S(1)}, bf16[8,128,384]{2,1,0:T(8,128)(2,1)S(1)}, f32[28,2,4,8,128]{4,3,2,1,0:T(8,128)S(1)}, f32[7,4,8,128]{3,2,1,0:T(8,128)S(1)}, f32[1152,128]{1,0:T(8,128)S(1)}) custom-call(s32[1,128]{1,0:T(1,128)} %bitcast.22, f32[4,256]{1,0:T(4,128)} %constant.2.clone.geom_hbm, s32[1,1152]{1,0:T(1,128)} %bitcast.21, ...), custom_call_target="tpu_custom_call" | custom-call | tf_op jit(solution)/shard_map/pallas_call | solution.py:508
  15.4 6.2 %all-to-all-done.got_ref = f32[64,8,128]{2,1,0:T(8,128)S(1)} async-done(((f32[64,8,128]{2,1,0:T(8,128)}), f32[64,8,128]{2,1,0:T(8,128)S(1)}, u32[]{:S(2)}, u32[]{:S(2)}) %all-to-all-start) | async-done | bytes 262176 | tf_op jit(solution)/shard_map/all_to_all | solution.py:507
  21.6 1.7 %shard_map.79 = f32[64,4,128]{2,1,0:T(4,128)S(1)} custom-call(f32[64,8,128]{2,1,0:T(8,128)S(1)} %all-to-all-done.got_ref, f32[28,2,4,8,128]{4,3,2,1,0:T(8,128)S(1)} %get-tuple-element.22.water_ref, f32[7,4,8,128]{3,2,1,0:T(8,128)S(1)} %get-tuple-element.23.tail_ref), custom_call_target="tpu_custom_call" | custom-call | tf_op jit(solution)/shard_map/pallas_call | solution.py:530
  23.3 12.6 %all_to_all.15.got_ref = f32[64,4,128]{2,1,0:T(4,128)S(1)} all-to-all(f32[64,4,128]{2,1,0:T(4,128)S(1)} %shard_map.79), channel_id=1, replica_groups=mesh['sec'=4,'lat'=16,'col'=4] {'sec','lat'}, dimensions={0} | all-to-all | bytes 262144 | tf_op jit(solution)/shard_map/all_to_all | solution.py:544
  35.9 1.8 %shard_map.80 = (f32[336,1,96]{2,1,0:T(1,128)S(1)}, f32[4,16,4,384]{3,2,1,0:T(4,128)S(1)}) custom-call(f32[64,4,128]{2,1,0:T(4,128)S(1)} %all_to_all.15.got_ref, f32[1152,128]{1,0:T(8,128)S(1)} %get-tuple-element.24.column_ref, f32[56,1152]{1,0:T(8,128)S(1)} %get-tuple-element.25.cols_ref, bf16[256,384]{1,0:T(8,128)(2,1)S(1)} %get-tuple-element.26.trig_ref), custom_call_target="tpu_custom_call" | custom-call | tf_op jit(solution)/shard_map/pallas_call | solution.py:545
  37.7 26.6 %all_to_all.16 = f32[64,4,384]{2,1,0:T(4,128)S(1)} all-to-all(f32[64,4,384]{2,1,0:T(4,128)S(1)} %bitcast.16), channel_id=1, replica_groups=mesh['sec'=4,'lat'=16,'col'=4] {'col','lat'}, dimensions={0} | all-to-all | bytes 786432 | tf_op jit(solution)/shard_map/all_to_all | solution.py:555
  64.3 1.5 %shard_map.81 = (f32[7,8,2,128]{3,2,1,0:T(2,128)}, f32[336,1,96]{2,1,0:T(1,128)}) custom-call(f32[4,16,4,384]{3,2,1,0:T(4,128)S(1)} %bitcast.15, bf16[8,128,384]{2,1,0:T(8,128)(2,1)S(1)} %get-tuple-element.28.weight_ref, f32[336,1,96]{2,1,0:T(1,128)S(1)} %get-tuple-element.29.state_ref), custom_call_target="tpu_custom_call" | custom-call | tf_op jit(solution)/shard_map/pallas_call | solution.py:558
Async XLA Ops:
  3.5 18.1 %all-to-all-start = ((f32[64,8,128]{2,1,0:T(8,128)}), f32[64,8,128]{2,1,0:T(8,128)S(1)}, u32[]{:S(2)}, u32[]{:S(2)}) async-start(f32[64,8,128]{2,1,0:T(8,128)} %get-tuple-element.18), calls=%async_computation | async-start | bytes 524288 | tf_op jit(solution)/shard_map/all_to_all | solution.py:507

commit v9 on v8

--- a/solution.py
+++ b/solution.py
@@ -47,6 +47,10 @@
 
 def lanes_of(shape):
     return lax.broadcasted_iota(jnp.int32, shape, 1)
+
+
+def place(t):
+    return t % NL * NS + t // NL
 
 
 def fill_one_hot(order_ref, hot_ref):
@@ -224,7 +228,7 @@
             if shift:
                 src = pltpu.roll(src, shift, 1)
             tile = src if tile is None else jnp.where(lane >= q * PER, src, tile)
-        out_ref[t] = tile
+        out_ref[place(t)] = tile
     save = pltpu.make_async_copy(out_ref, out_hbm, sems.at[3])
     save.start()
     save.wait()
@@ -288,12 +292,12 @@
     def store_diff(q, v, x):
         diff_ref[v, q * 8 : q * 8 + 8, :] = x
 
-    gather_lanes(lambda i: got_ref[i], range(4), 0, NL, RUNS, store_wind)
+    gather_lanes(lambda i: got_ref[place(i)], range(4), 0, NL, RUNS, store_wind)
     cache = {}
 
     def diff(i):
         if i not in cache:
-            cache[i] = got_ref[3 * NL + i] - got_ref[2 * NL + i]
+            cache[i] = got_ref[place(3 * NL + i)] - got_ref[place(2 * NL + i)]
         return cache[i]
 
     gather_lanes(diff, range(7), 0, NL, RUNS, store_diff)
@@ -359,7 +363,7 @@
         high = pltpu.roll(tile, HALF, 1)[4:8]
         tile = jnp.where(lane[0:4] < HALF, low, high)
         for s in range(NS):
-            out_ref[s * NL + i] = tile
+            out_ref[place(s * NL + i)] = tile
 
 
 def update_kernel(
@@ -388,7 +392,7 @@
 
     def tile_of(t):
         if t not in cache:
-            tile = got_ref[t]
+            tile = got_ref[place(t)]
             cache[t] = jnp.concatenate((tile, pltpu.roll(tile, 128 - HALF, 1)), axis=0)
         return cache[t]
 
@@ -504,7 +508,7 @@
         (HBM, VMEM),
     )(*(stay(x) for x in (state, forcing, order)))
     outgoing, waves = lax.optimization_barrier((outgoing, waves))
-    arrived = lax.all_to_all(outgoing, ("sec", "lat"), split_axis=0, concat_axis=0, tiled=True)
+    arrived = lax.all_to_all(outgoing, ("lat", "sec"), split_axis=0, concat_axis=0, tiled=True)
     trig, weights, water, tail, column = call(
         table_kernel,
         (
@@ -541,7 +545,7 @@
             pltpu.VMEM((5, 8, 128), F32),
         ],
     )(arrived, water, tail)
-    returned = lax.all_to_all(rain, ("sec", "lat"), split_axis=0, concat_axis=0, tiled=True)
+    returned = lax.all_to_all(rain, ("lat", "sec"), split_axis=0, concat_axis=0, tiled=True)
     updated, fourier = call(
         update_kernel,
         (shape((ROWS, 1, LONS), F32), shape((NC, NL, 4, 384), F32)),

time: 66.5 us -> 67.2 us (1.011)
  no operation moved by 1% of the time
where the time goes in v9:
time: 67.2 us; the launch traced here: 66.3 us
  blocking collectives  39.5 us (59%)
  Pallas kernels  10.4 us (15%)
  starting transfers between devices  9.39 us (14%)
  waiting for transfers between devices  6.4 us (10%)
    all_to_all x1, blocking collectives, shards(): lax.all_to_all(fourier.reshape(NL * NC, 4, 384), ('col', 'lat'), split_ax...  26.7 us
    all_to_all x1, blocking collectives, shards(): lax.all_to_all(rain, ('lat', 'sec'), split_axis=0, concat_axis=0, tiled=T...  12.8 us
    all_to_all x1, starting transfers between devices, shards(): lax.all_to_all(outgoing, ('lat', 'sec'), split_axis=0, concat_axis=0, til...  9.39 us
    all_to_all x1, waiting for transfers between devices, shards(): lax.all_to_all(outgoing, ('lat', 'sec'), split_axis=0, concat_axis=0, til...  6.4 us
    pallas_call x1, Pallas kernels, shards(): call(pack_kernel, (shape((TARGETS, 8, 128), F32), shape((2 * LEVELS, COLS...  2.85 us
    pallas_call x1, Pallas kernels, shards(): call(table_kernel, (shape((2 * MMAX, 384), BF16), shape((SLOTS_OWN, MMAX,...  2.48 us
    pallas_call x1, Pallas kernels, shards(): call(update_kernel, (shape((ROWS, 1, LONS), F32), shape((NC, NL, 4, 384),...  1.8 us
    pallas_call x1, Pallas kernels, shards(): call(cloud_kernel, shape((TARGETS, 4, 128), F32), [VMEM] * 3, [pltpu.VMEM...  1.71 us
  transfers between devices with their start and end apart: 1, of which 1 were waited for; matrix products, arithmetic and copies ran while one was open for 0% of the time, Pallas kernels for 4%

profile of v9, /device:TPU:2, one launch (start us, length us, event | category | flops | bytes accessed | tf_op | source)
XLA Modules:
  0.0 66.3 jit_solution(17604869958020642159)
XLA Ops:
  0.6 2.8 %shard_map.77 = (f32[64,8,128]{2,1,0:T(8,128)}, f32[56,1152]{1,0:T(8,128)S(1)}) custom-call(f32[336,1,96]{2,1,0:T(1,128)} %bitcast.18, f32[336,1,96]{2,1,0:T(1,128)} %bitcast.19, s32[1,1152]{1,0:T(1,128)} %bitcast.20), custom_call_target="tpu_custom_call" | custom-call | tf_op jit(solution)/shard_map/pallas_call | solution.py:496
  3.5 9.4 %all-to-all-start = ((f32[64,8,128]{2,1,0:T(8,128)}), f32[64,8,128]{2,1,0:T(8,128)S(1)}, u32[]{:S(2)}, u32[]{:S(2)}) async-start(f32[64,8,128]{2,1,0:T(8,128)} %get-tuple-element.18), calls=%async_computation | async-start | bytes 524288 | tf_op jit(solution)/shard_map/all_to_all | solution.py:511
  12.9 2.5 %shard_map.78 = (bf16[256,384]{1,0:T(8,128)(2,1)S(1)}, bf16[8,128,384]{2,1,0:T(8,128)(2,1)S(1)}, f32[28,2,4,8,128]{4,3,2,1,0:T(8,128)S(1)}, f32[7,4,8,128]{3,2,1,0:T(8,128)S(1)}, f32[1152,128]{1,0:T(8,128)S(1)}) custom-call(s32[1,128]{1,0:T(1,128)} %bitcast.22, f32[4,256]{1,0:T(4,128)} %constant.2.clone.geom_hbm, s32[1,1152]{1,0:T(1,128)} %bitcast.21, ...), custom_call_target="tpu_custom_call" | custom-call | tf_op jit(solution)/shard_map/pallas_call | solution.py:512
  15.4 6.4 %all-to-all-done.got_ref = f32[64,8,128]{2,1,0:T(8,128)S(1)} async-done(((f32[64,8,128]{2,1,0:T(8,128)}), f32[64,8,128]{2,1,0:T(8,128)S(1)}, u32[]{:S(2)}, u32[]{:S(2)}) %all-to-all-start) | async-done | bytes 262176 | tf_op jit(solution)/shard_map/all_to_all | solution.py:511
  21.8 1.7 %shard_map.79 = f32[64,4,128]{2,1,0:T(4,128)S(1)} custom-call(f32[64,8,128]{2,1,0:T(8,128)S(1)} %all-to-all-done.got_ref, f32[28,2,4,8,128]{4,3,2,1,0:T(8,128)S(1)} %get-tuple-element.22.water_ref, f32[7,4,8,128]{3,2,1,0:T(8,128)S(1)} %get-tuple-element.23.tail_ref), custom_call_target="tpu_custom_call" | custom-call | tf_op jit(solution)/shard_map/pallas_call | solution.py:534
  23.5 12.8 %all_to_all.15.got_ref = f32[64,4,128]{2,1,0:T(4,128)S(1)} all-to-all(f32[64,4,128]{2,1,0:T(4,128)S(1)} %shard_map.79), channel_id=1, replica_groups=mesh['sec'=4,'lat'=16,'col'=4] {'lat','sec'}, dimensions={0} | all-to-all | bytes 262144 | tf_op jit(solution)/shard_map/all_to_all | solution.py:548
  36.3 1.8 %shard_map.80 = (f32[336,1,96]{2,1,0:T(1,128)S(1)}, f32[4,16,4,384]{3,2,1,0:T(4,128)S(1)}) custom-call(f32[64,4,128]{2,1,0:T(4,128)S(1)} %all_to_all.15.got_ref, f32[1152,128]{1,0:T(8,128)S(1)} %get-tuple-element.24.column_ref, f32[56,1152]{1,0:T(8,128)S(1)} %get-tuple-element.25.cols_ref, bf16[256,384]{1,0:T(8,128)(2,1)S(1)} %get-tuple-element.26.trig_ref), custom_call_target="tpu_custom_call" | custom-call | tf_op jit(solution)/shard_map/pallas_call | solution.py:549
  38.1 26.7 %all_to_all.16 = f32[64,4,384]{2,1,0:T(4,128)S(1)} all-to-all(f32[64,4,384]{2,1,0:T(4,128)S(1)} %bitcast.16), channel_id=1, replica_groups=mesh['sec'=4,'lat'=16,'col'=4] {'col','lat'}, dimensions={0} | all-to-all | bytes 786432 | tf_op jit(solution)/shard_map/all_to_all | solution.py:559
  64.8 1.5 %shard_map.81 = (f32[7,8,2,128]{3,2,1,0:T(2,128)}, f32[336,1,96]{2,1,0:T(1,128)}) custom-call(f32[4,16,4,384]{3,2,1,0:T(4,128)S(1)} %bitcast.15, bf16[8,128,384]{2,1,0:T(8,128)(2,1)S(1)} %get-tuple-element.28.weight_ref, f32[336,1,96]{2,1,0:T(1,128)S(1)} %get-tuple-element.29.state_ref), custom_call_target="tpu_custom_call" | custom-call | tf_op jit(solution)/shard_map/pallas_call | solution.py:562
Async XLA Ops:
  3.5 18.3 %all-to-all-start = ((f32[64,8,128]{2,1,0:T(8,128)}), f32[64,8,128]{2,1,0:T(8,128)S(1)}, u32[]{:S(2)}, u32[]{:S(2)}) async-start(f32[64,8,128]{2,1,0:T(8,128)} %get-tuple-element.18), calls=%async_computation | async-start | bytes 524288 | tf_op jit(solution)/shard_map/all_to_all | solution.py:511

commit v10 on v8

--- a/solution.py
+++ b/solution.py
@@ -98,7 +98,8 @@
     )
     retreat = grow * retreat
     begin = jnp.where(degree == order, 1.0, 0.0)
-    diagonal = jnp.exp(head + order[:, 0:1] * geom_ref[1:2, :]) * geom_ref[2:3, :]
+    diagonal = jnp.exp(head + order[:, 0:1] * geom_ref[1:2, :])
+    weight = geom_ref[2:3, :]
     cosine = jnp.broadcast_to(geom_ref[0:1, :], (SLOTS_OWN, 256))
     previous = jnp.zeros((SLOTS_OWN, 256), F32)
     current = previous
@@ -106,8 +107,8 @@
         fresh = (grow[:, n : n + 1] * cosine) * current + (
             begin[:, n : n + 1] * diagonal - retreat[:, n : n + 1] * previous
         )
-        poly_ref[0, n * 8 : n * 8 + 8, :] = fresh[:, :128]
-        poly_ref[1, n * 8 : n * 8 + 8, :] = fresh[:, 128:]
+        poly_ref[0, n * 8 : n * 8 + 8, :] = fresh[:, :128] * weight[:, :128]
+        poly_ref[1, n * 8 : n * 8 + 8, :] = fresh[:, 128:] * weight[:, 128:]
         previous, current = current, fresh
     for s in range(SLOTS_OWN):
         for h in range(2):
@@ -406,7 +407,7 @@
     for b in range(BAND):
         piece = jnp.concatenate((now[:, b * LONS : (b + 1) * LONS], blank), axis=1)
         rows_ref[pl.ds(b, LEVELS, stride=BAND), :] = piece
-    rows = rows_ref[...]
+    rows = rows_ref[0:ROWS, :]
     out_ref[...] = rows[:, :LONS].reshape(ROWS, 1, LONS)
     hi, lo = split2(rows)
     dims = (((1,), (1,)), ((), ()))
@@ -548,7 +549,7 @@
         [VMEM] * 4,
         [
             pltpu.VMEM((32, COLS), F32),
-            pltpu.VMEM((ROWS, 128), F32),
+            pltpu.VMEM((32 * BAND, 128), F32),
             pltpu.VMEM((COLS, COLS), BF16),
         ],
     )(returned, column, cols, trig)
@@ -560,7 +561,7 @@
         (shape((LEV_OWN, SLOTS_OWN, 2, MMAX), F32), shape((ROWS, 1, LONS), F32)),
         [VMEM] * 3,
         [
-            pltpu.VMEM((2, LEV_OWN * 16, 128), F32),
+            pltpu.VMEM((2, 128, 128), F32),
             pltpu.VMEM((LEV_OWN, SLOTS_OWN, 2, MMAX), F32),
             pltpu.SemaphoreType.DMA((3,)),
         ],

time: 66.5 us -> 66.5 us (level)
  no operation moved by 1% of the time
where the time goes in v10:
time: 66.5 us; the launch traced here: 65.9 us
  blocking collectives  39.2 us (59%)
  Pallas kernels  10.4 us (16%)
  starting transfers between devices  9.39 us (14%)
  waiting for transfers between devices  6.23 us (9%)
    all_to_all x1, blocking collectives, shards(): lax.all_to_all(fourier.reshape(NL * NC, 4, 384), ('col', 'lat'), split_ax...  26.6 us
    all_to_all x1, blocking collectives, shards(): lax.all_to_all(rain, ('sec', 'lat'), split_axis=0, concat_axis=0, tiled=T...  12.6 us
    all_to_all x1, starting transfers between devices, shards(): lax.all_to_all(outgoing, ('sec', 'lat'), split_axis=0, concat_axis=0, til...  9.39 us
    all_to_all x1, waiting for transfers between devices, shards(): lax.all_to_all(outgoing, ('sec', 'lat'), split_axis=0, concat_axis=0, til...  6.23 us
    pallas_call x1, Pallas kernels, shards(): call(pack_kernel, (shape((TARGETS, 8, 128), F32), shape((2 * LEVELS, COLS...  2.85 us
    pallas_call x1, Pallas kernels, shards(): call(table_kernel, (shape((2 * MMAX, 384), BF16), shape((SLOTS_OWN, MMAX,...  2.48 us
    pallas_call x1, Pallas kernels, shards(): call(update_kernel, (shape((ROWS, 1, LONS), F32), shape((NC, NL, 4, 384),...  1.8 us
    pallas_call x1, Pallas kernels, shards(): call(cloud_kernel, shape((TARGETS, 4, 128), F32), [VMEM] * 3, [pltpu.VMEM...  1.71 us
  transfers between devices with their start and end apart: 1, of which 1 were waited for; matrix products, arithmetic and copies ran while one was open for 0% of the time, Pallas kernels for 4%

profile of v10, /device:TPU:2, one launch (start us, length us, event | category | flops | bytes accessed | tf_op | source)
XLA Modules:
  0.0 65.9 jit_solution(11863323101876687643)
XLA Ops:
  0.6 2.8 %shard_map.77 = (f32[64,8,128]{2,1,0:T(8,128)}, f32[56,1152]{1,0:T(8,128)S(1)}) custom-call(f32[336,1,96]{2,1,0:T(1,128)} %bitcast.18, f32[336,1,96]{2,1,0:T(1,128)} %bitcast.19, s32[1,1152]{1,0:T(1,128)} %bitcast.20), custom_call_target="tpu_custom_call" | custom-call | tf_op jit(solution)/shard_map/pallas_call | solution.py:493
  3.5 9.4 %all-to-all-start = ((f32[64,8,128]{2,1,0:T(8,128)}), f32[64,8,128]{2,1,0:T(8,128)S(1)}, u32[]{:S(2)}, u32[]{:S(2)}) async-start(f32[64,8,128]{2,1,0:T(8,128)} %get-tuple-element.18), calls=%async_computation | async-start | bytes 524288 | tf_op jit(solution)/shard_map/all_to_all | solution.py:508
  12.9 2.5 %shard_map.78 = (bf16[256,384]{1,0:T(8,128)(2,1)S(1)}, bf16[8,128,384]{2,1,0:T(8,128)(2,1)S(1)}, f32[28,2,4,8,128]{4,3,2,1,0:T(8,128)S(1)}, f32[7,4,8,128]{3,2,1,0:T(8,128)S(1)}, f32[1152,128]{1,0:T(8,128)S(1)}) custom-call(s32[1,128]{1,0:T(1,128)} %bitcast.22, f32[4,256]{1,0:T(4,128)} %constant.2.clone.geom_hbm, s32[1,1152]{1,0:T(1,128)} %bitcast.21, ...), custom_call_target="tpu_custom_call" | custom-call | tf_op jit(solution)/shard_map/pallas_call | solution.py:509
  15.4 6.2 %all-to-all-done.got_ref = f32[64,8,128]{2,1,0:T(8,128)S(1)} async-done(((f32[64,8,128]{2,1,0:T(8,128)}), f32[64,8,128]{2,1,0:T(8,128)S(1)}, u32[]{:S(2)}, u32[]{:S(2)}) %all-to-all-start) | async-done | bytes 262176 | tf_op jit(solution)/shard_map/all_to_all | solution.py:508
  21.6 1.7 %shard_map.79 = f32[64,4,128]{2,1,0:T(4,128)S(1)} custom-call(f32[64,8,128]{2,1,0:T(8,128)S(1)} %all-to-all-done.got_ref, f32[28,2,4,8,128]{4,3,2,1,0:T(8,128)S(1)} %get-tuple-element.22.water_ref, f32[7,4,8,128]{3,2,1,0:T(8,128)S(1)} %get-tuple-element.23.tail_ref), custom_call_target="tpu_custom_call" | custom-call | tf_op jit(solution)/shard_map/pallas_call | solution.py:531
  23.3 12.6 %all_to_all.15.got_ref = f32[64,4,128]{2,1,0:T(4,128)S(1)} all-to-all(f32[64,4,128]{2,1,0:T(4,128)S(1)} %shard_map.79), channel_id=1, replica_groups=mesh['sec'=4,'lat'=16,'col'=4] {'sec','lat'}, dimensions={0} | all-to-all | bytes 262144 | tf_op jit(solution)/shard_map/all_to_all | solution.py:545
  35.9 1.8 %shard_map.80 = (f32[336,1,96]{2,1,0:T(1,128)S(1)}, f32[4,16,4,384]{3,2,1,0:T(4,128)S(1)}) custom-call(f32[64,4,128]{2,1,0:T(4,128)S(1)} %all_to_all.15.got_ref, f32[1152,128]{1,0:T(8,128)S(1)} %get-tuple-element.24.column_ref, f32[56,1152]{1,0:T(8,128)S(1)} %get-tuple-element.25.cols_ref, bf16[256,384]{1,0:T(8,128)(2,1)S(1)} %get-tuple-element.26.trig_ref), custom_call_target="tpu_custom_call" | custom-call | tf_op jit(solution)/shard_map/pallas_call | solution.py:546
  37.7 26.6 %all_to_all.16 = f32[64,4,384]{2,1,0:T(4,128)S(1)} all-to-all(f32[64,4,384]{2,1,0:T(4,128)S(1)} %bitcast.16), channel_id=1, replica_groups=mesh['sec'=4,'lat'=16,'col'=4] {'col','lat'}, dimensions={0} | all-to-all | bytes 786432 | tf_op jit(solution)/shard_map/all_to_all | solution.py:556
  64.3 1.5 %shard_map.81 = (f32[7,8,2,128]{3,2,1,0:T(2,128)}, f32[336,1,96]{2,1,0:T(1,128)}) custom-call(f32[4,16,4,384]{3,2,1,0:T(4,128)S(1)} %bitcast.15, bf16[8,128,384]{2,1,0:T(8,128)(2,1)S(1)} %get-tuple-element.28.weight_ref, f32[336,1,96]{2,1,0:T(1,128)S(1)} %get-tuple-element.29.state_ref), custom_call_target="tpu_custom_call" | custom-call | tf_op jit(solution)/shard_map/pallas_call | solution.py:559
Async XLA Ops:
  3.5 18.1 %all-to-all-start = ((f32[64,8,128]{2,1,0:T(8,128)}), f32[64,8,128]{2,1,0:T(8,128)S(1)}, u32[]{:S(2)}, u32[]{:S(2)}) async-start(f32[64,8,128]{2,1,0:T(8,128)} %get-tuple-element.18), calls=%async_computation | async-start | bytes 524288 | tf_op jit(solution)/shard_map/all_to_all | solution.py:508

commit v11 on v10

--- a/solution.py
+++ b/solution.py
@@ -212,19 +212,30 @@
     got = jnp.dot(both, hot_ref[...], preferred_element_type=F32)
     got = got[: 2 * LEVELS] + got[2 * LEVELS :]
     lane = lanes_of((8, 128))
-    groups = 2 * LEVELS // 8
+    wide = lanes_of((8, COLS)).astype(F32)
+    window = jnp.floor((wide + 0.5) * (1.0 / PER))
+    even = window - 2.0 * jnp.floor(window * 0.5) == 0.0
+    groups = [got[q * 8 : q * 8 + 8] for q in range(2 * LEVELS // 8)]
+    paired = []
+    for parity in range(2):
+        here = even if parity == 0 else ~even
+        rows = [
+            jnp.where(here, groups[q], pltpu.roll(groups[q + 1], PER, 1)) for q in range(0, 6, 2)
+        ]
+        paired.append(rows + [groups[6]])
     for t in range(TARGETS):
         v, off = divmod(t * PER, 128)
         tile = None
-        for q in range(groups):
-            src = got[q * 8 : q * 8 + 8, v * 128 : v * 128 + 128]
-            if off + PER > 128:
-                nxt = got[q * 8 : q * 8 + 8, v * 128 + 128 : v * 128 + 256]
-                src = jnp.where(lane < off, nxt, src)
-            shift = (q * PER - off) % 128
+        for p, row in enumerate(paired[t % 2]):
+            span = PER if p == 3 else 2 * PER
+            src = row[:, v * 128 : v * 128 + 128]
+            if off + span > 128:
+                w = (v + 1) % (COLS // 128)
+                src = jnp.where(lane < off, row[:, w * 128 : w * 128 + 128], src)
+            shift = (2 * p * PER - off) % 128
             if shift:
                 src = pltpu.roll(src, shift, 1)
-            tile = src if tile is None else jnp.where(lane >= q * PER, src, tile)
+            tile = src if tile is None else jnp.where(lane >= 2 * p * PER, src, tile)
         out_ref[t] = tile
     save = pltpu.make_async_copy(out_ref, out_hbm, sems.at[3])
     save.start()
@@ -378,9 +389,11 @@
     for v in range(COLS // 128):
         rows = slice(v * 128, v * 128 + 128)
         column = column_ref[rows, :]
+        block = jnp.floor((column + 0.5) * (1.0 / 128.0))
+        same = jnp.where(column - 128.0 * block == lane, 1.0, 0.0).astype(BF16)
+        block = block.astype(BF16)
         for c in range(COLS // 128):
-            hot = jnp.where(lane + float(c * 128) == column, 1.0, 0.0)
-            hot_ref[rows, c * 128 : c * 128 + 128] = hot.astype(BF16)
+            hot_ref[rows, c * 128 : c * 128 + 128] = jnp.where(block == c, same, jnp.zeros_like(same))
 
     def store(q, v, x):
         slots_ref[q * 8 : q * 8 + 8, v * 128 : v * 128 + 128] = x
@@ -446,11 +459,8 @@
         out = lax.dot_general(parts, weight_ref[s], dims, preferred_element_type=F32)
         out = out + lax.dot_general(lo, weight_ref[s, :, 0:NLAT], dims, preferred_element_type=F32)
         out_ref[:, s, :, :] = out.reshape(LEV_OWN, 2, MMAX)
-        if s % 4 == 3:
-            part = pl.ds(s - 3, 4)
-            save = pltpu.make_async_copy(out_ref.at[:, part], out_hbm.at[:, part], sems.at[s // 4])
-            save.start()
-            saves.append(save)
+    saves.append(pltpu.make_async_copy(out_ref, out_hbm, sems.at[0]))
+    saves[1].start()
     for save in saves:
         save.wait()
 

time: 66.5 us -> 66.5 us (level)
  no operation moved by 1% of the time
where the time goes in v11:
time: 66.5 us; the launch traced here: 65.9 us
  blocking collectives  39.2 us (59%)
  Pallas kernels  10.4 us (16%)
  starting transfers between devices  9.39 us (14%)
  waiting for transfers between devices  6.23 us (9%)
    all_to_all x1, blocking collectives, shards(): lax.all_to_all(fourier.reshape(NL * NC, 4, 384), ('col', 'lat'), split_ax...  26.6 us
    all_to_all x1, blocking collectives, shards(): lax.all_to_all(rain, ('sec', 'lat'), split_axis=0, concat_axis=0, tiled=T...  12.6 us
    all_to_all x1, starting transfers between devices, shards(): lax.all_to_all(outgoing, ('sec', 'lat'), split_axis=0, concat_axis=0, til...  9.39 us
    all_to_all x1, waiting for transfers between devices, shards(): lax.all_to_all(outgoing, ('sec', 'lat'), split_axis=0, concat_axis=0, til...  6.23 us
    pallas_call x1, Pallas kernels, shards(): call(pack_kernel, (shape((TARGETS, 8, 128), F32), shape((2 * LEVELS, COLS...  2.8 us
    pallas_call x1, Pallas kernels, shards(): call(table_kernel, (shape((2 * MMAX, 384), BF16), shape((SLOTS_OWN, MMAX,...  2.48 us
    pallas_call x1, Pallas kernels, shards(): call(update_kernel, (shape((ROWS, 1, LONS), F32), shape((NC, NL, 4, 384),...  1.83 us
    pallas_call x1, Pallas kernels, shards(): call(cloud_kernel, shape((TARGETS, 4, 128), F32), [VMEM] * 3, [pltpu.VMEM...  1.71 us
  transfers between devices with their start and end apart: 1, of which 1 were waited for; matrix products, arithmetic and copies ran while one was open for 0% of the time, Pallas kernels for 4%

profile of v11, /device:TPU:2, one launch (start us, length us, event | category | flops | bytes accessed | tf_op | source)
XLA Modules:
  0.0 65.9 jit_solution(4423507713968180343)
XLA Ops:
  0.6 2.8 %shard_map.77 = (f32[64,8,128]{2,1,0:T(8,128)}, f32[56,1152]{1,0:T(8,128)S(1)}) custom-call(f32[336,1,96]{2,1,0:T(1,128)} %bitcast.18, f32[336,1,96]{2,1,0:T(1,128)} %bitcast.19, s32[1,1152]{1,0:T(1,128)} %bitcast.20), custom_call_target="tpu_custom_call" | custom-call | tf_op jit(solution)/shard_map/pallas_call | solution.py:503
  3.4 9.4 %all-to-all-start = ((f32[64,8,128]{2,1,0:T(8,128)}), f32[64,8,128]{2,1,0:T(8,128)S(1)}, u32[]{:S(2)}, u32[]{:S(2)}) async-start(f32[64,8,128]{2,1,0:T(8,128)} %get-tuple-element.18), calls=%async_computation | async-start | bytes 524288 | tf_op jit(solution)/shard_map/all_to_all | solution.py:518
  12.8 2.5 %shard_map.78 = (bf16[256,384]{1,0:T(8,128)(2,1)S(1)}, bf16[8,128,384]{2,1,0:T(8,128)(2,1)S(1)}, f32[28,2,4,8,128]{4,3,2,1,0:T(8,128)S(1)}, f32[7,4,8,128]{3,2,1,0:T(8,128)S(1)}, f32[1152,128]{1,0:T(8,128)S(1)}) custom-call(s32[1,128]{1,0:T(1,128)} %bitcast.22, f32[4,256]{1,0:T(4,128)} %constant.2.clone.geom_hbm, s32[1,1152]{1,0:T(1,128)} %bitcast.21, ...), custom_call_target="tpu_custom_call" | custom-call | tf_op jit(solution)/shard_map/pallas_call | solution.py:519
  15.3 6.2 %all-to-all-done.got_ref = f32[64,8,128]{2,1,0:T(8,128)S(1)} async-done(((f32[64,8,128]{2,1,0:T(8,128)}), f32[64,8,128]{2,1,0:T(8,128)S(1)}, u32[]{:S(2)}, u32[]{:S(2)}) %all-to-all-start) | async-done | bytes 262176 | tf_op jit(solution)/shard_map/all_to_all | solution.py:518
  21.6 1.7 %shard_map.79 = f32[64,4,128]{2,1,0:T(4,128)S(1)} custom-call(f32[64,8,128]{2,1,0:T(8,128)S(1)} %all-to-all-done.got_ref, f32[28,2,4,8,128]{4,3,2,1,0:T(8,128)S(1)} %get-tuple-element.22.water_ref, f32[7,4,8,128]{3,2,1,0:T(8,128)S(1)} %get-tuple-element.23.tail_ref), custom_call_target="tpu_custom_call" | custom-call | tf_op jit(solution)/shard_map/pallas_call | solution.py:541
  23.3 12.6 %all_to_all.15.got_ref = f32[64,4,128]{2,1,0:T(4,128)S(1)} all-to-all(f32[64,4,128]{2,1,0:T(4,128)S(1)} %shard_map.79), channel_id=1, replica_groups=mesh['sec'=4,'lat'=16,'col'=4] {'sec','lat'}, dimensions={0} | all-to-all | bytes 262144 | tf_op jit(solution)/shard_map/all_to_all | solution.py:555
  35.9 1.8 %shard_map.80 = (f32[336,1,96]{2,1,0:T(1,128)S(1)}, f32[4,16,4,384]{3,2,1,0:T(4,128)S(1)}) custom-call(f32[64,4,128]{2,1,0:T(4,128)S(1)} %all_to_all.15.got_ref, f32[1152,128]{1,0:T(8,128)S(1)} %get-tuple-element.24.column_ref, f32[56,1152]{1,0:T(8,128)S(1)} %get-tuple-element.25.cols_ref, bf16[256,384]{1,0:T(8,128)(2,1)S(1)} %get-tuple-element.26.trig_ref), custom_call_target="tpu_custom_call" | custom-call | tf_op jit(solution)/shard_map/pallas_call | solution.py:556
  37.7 26.6 %all_to_all.16 = f32[64,4,384]{2,1,0:T(4,128)S(1)} all-to-all(f32[64,4,384]{2,1,0:T(4,128)S(1)} %bitcast.16), channel_id=1, replica_groups=mesh['sec'=4,'lat'=16,'col'=4] {'col','lat'}, dimensions={0} | all-to-all | bytes 786432 | tf_op jit(solution)/shard_map/all_to_all | solution.py:566
  64.3 1.5 %shard_map.81 = (f32[7,8,2,128]{3,2,1,0:T(2,128)}, f32[336,1,96]{2,1,0:T(1,128)}) custom-call(f32[4,16,4,384]{3,2,1,0:T(4,128)S(1)} %bitcast.15, bf16[8,128,384]{2,1,0:T(8,128)(2,1)S(1)} %get-tuple-element.28.weight_ref, f32[336,1,96]{2,1,0:T(1,128)S(1)} %get-tuple-element.29.state_ref), custom_call_target="tpu_custom_call" | custom-call | tf_op jit(solution)/shard_map/pallas_call | solution.py:569
Async XLA Ops:
  3.4 18.1 %all-to-all-start = ((f32[64,8,128]{2,1,0:T(8,128)}), f32[64,8,128]{2,1,0:T(8,128)S(1)}, u32[]{:S(2)}, u32[]{:S(2)}) async-start(f32[64,8,128]{2,1,0:T(8,128)} %get-tuple-element.18), calls=%async_computation | async-start | bytes 524288 | tf_op jit(solution)/shard_map/all_to_all | solution.py:518

commit v12 on v11

--- a/solution.py
+++ b/solution.py
@@ -350,7 +350,8 @@
         last_ref[4, pl.ds(g, 1), :] = cloud_tile(*rows, [tail_ref[g, n] for n in range(4)])
         return carry
 
-    lax.fori_loop(0, groups, level, 0)
+    for g in range(groups):
+        level(g, 0)
     rain_tail = last_ref[4]
     for kk in range(4):
         piece = rain_tail if kk == 0 else pltpu.roll(rain_tail, 128 - kk * TAIL, 1)

time: 66.5 us -> 66.4 us (level)
  no operation moved by 1% of the time
where the time goes in v12:
time: 66.4 us; the launch traced here: 65.7 us
  blocking collectives  39.2 us (59%)
  Pallas kernels  10.3 us (16%)
  starting transfers between devices  9.39 us (14%)
  waiting for transfers between devices  6.23 us (9%)
  between operations  0.67 us (1%)
    all_to_all x1, blocking collectives, shards(): lax.all_to_all(fourier.reshape(NL * NC, 4, 384), ('col', 'lat'), split_ax...  26.6 us
    all_to_all x1, blocking collectives, shards(): lax.all_to_all(rain, ('sec', 'lat'), split_axis=0, concat_axis=0, tiled=T...  12.6 us
    all_to_all x1, starting transfers between devices, shards(): lax.all_to_all(outgoing, ('sec', 'lat'), split_axis=0, concat_axis=0, til...  9.39 us
    all_to_all x1, waiting for transfers between devices, shards(): lax.all_to_all(outgoing, ('sec', 'lat'), split_axis=0, concat_axis=0, til...  6.23 us
    pallas_call x1, Pallas kernels, shards(): call(pack_kernel, (shape((TARGETS, 8, 128), F32), shape((2 * LEVELS, COLS...  2.8 us
    pallas_call x1, Pallas kernels, shards(): call(table_kernel, (shape((2 * MMAX, 384), BF16), shape((SLOTS_OWN, MMAX,...  2.48 us
    pallas_call x1, Pallas kernels, shards(): call(update_kernel, (shape((ROWS, 1, LONS), F32), shape((NC, NL, 4, 384),...  1.83 us
    pallas_call x1, Pallas kernels, shards(): call(cloud_kernel, shape((TARGETS, 4, 128), F32), [VMEM] * 3, [pltpu.VMEM...  1.62 us
  transfers between devices with their start and end apart: 1, of which 1 were waited for; matrix products, arithmetic and copies ran while one was open for 0% of the time, Pallas kernels for 4%

profile of v12, /device:TPU:2, one launch (start us, length us, event | category | flops | bytes accessed | tf_op | source)
XLA Modules:
  0.0 65.7 jit_solution(5303801068866419138)
XLA Ops:
  0.6 2.8 %shard_map.77 = (f32[64,8,128]{2,1,0:T(8,128)}, f32[56,1152]{1,0:T(8,128)S(1)}) custom-call(f32[336,1,96]{2,1,0:T(1,128)} %bitcast.18, f32[336,1,96]{2,1,0:T(1,128)} %bitcast.19, s32[1,1152]{1,0:T(1,128)} %bitcast.20), custom_call_target="tpu_custom_call" | custom-call | tf_op jit(solution)/shard_map/pallas_call | solution.py:504
  3.4 9.4 %all-to-all-start = ((f32[64,8,128]{2,1,0:T(8,128)}), f32[64,8,128]{2,1,0:T(8,128)S(1)}, u32[]{:S(2)}, u32[]{:S(2)}) async-start(f32[64,8,128]{2,1,0:T(8,128)} %get-tuple-element.18), calls=%async_computation | async-start | bytes 524288 | tf_op jit(solution)/shard_map/all_to_all | solution.py:519
  12.8 2.5 %shard_map.78 = (bf16[256,384]{1,0:T(8,128)(2,1)S(1)}, bf16[8,128,384]{2,1,0:T(8,128)(2,1)S(1)}, f32[28,2,4,8,128]{4,3,2,1,0:T(8,128)S(1)}, f32[7,4,8,128]{3,2,1,0:T(8,128)S(1)}, f32[1152,128]{1,0:T(8,128)S(1)}) custom-call(s32[1,128]{1,0:T(1,128)} %bitcast.22, f32[4,256]{1,0:T(4,128)} %constant.2.clone.geom_hbm, s32[1,1152]{1,0:T(1,128)} %bitcast.21, ...), custom_call_target="tpu_custom_call" | custom-call | tf_op jit(solution)/shard_map/pallas_call | solution.py:520
  15.3 6.2 %all-to-all-done.got_ref = f32[64,8,128]{2,1,0:T(8,128)S(1)} async-done(((f32[64,8,128]{2,1,0:T(8,128)}), f32[64,8,128]{2,1,0:T(8,128)S(1)}, u32[]{:S(2)}, u32[]{:S(2)}) %all-to-all-start) | async-done | bytes 262176 | tf_op jit(solution)/shard_map/all_to_all | solution.py:519
  21.6 1.6 %shard_map.79 = f32[64,4,128]{2,1,0:T(4,128)S(1)} custom-call(f32[64,8,128]{2,1,0:T(8,128)S(1)} %all-to-all-done.got_ref, f32[28,2,4,8,128]{4,3,2,1,0:T(8,128)S(1)} %get-tuple-element.22.water_ref, f32[7,4,8,128]{3,2,1,0:T(8,128)S(1)} %get-tuple-element.23.tail_ref), custom_call_target="tpu_custom_call" | custom-call | tf_op jit(solution)/shard_map/pallas_call | solution.py:542
  23.2 12.6 %all_to_all.15.got_ref = f32[64,4,128]{2,1,0:T(4,128)S(1)} all-to-all(f32[64,4,128]{2,1,0:T(4,128)S(1)} %shard_map.79), channel_id=1, replica_groups=mesh['sec'=4,'lat'=16,'col'=4] {'sec','lat'}, dimensions={0} | all-to-all | bytes 262144 | tf_op jit(solution)/shard_map/all_to_all | solution.py:556
  35.8 1.8 %shard_map.80 = (f32[336,1,96]{2,1,0:T(1,128)S(1)}, f32[4,16,4,384]{3,2,1,0:T(4,128)S(1)}) custom-call(f32[64,4,128]{2,1,0:T(4,128)S(1)} %all_to_all.15.got_ref, f32[1152,128]{1,0:T(8,128)S(1)} %get-tuple-element.24.column_ref, f32[56,1152]{1,0:T(8,128)S(1)} %get-tuple-element.25.cols_ref, bf16[256,384]{1,0:T(8,128)(2,1)S(1)} %get-tuple-element.26.trig_ref), custom_call_target="tpu_custom_call" | custom-call | tf_op jit(solution)/shard_map/pallas_call | solution.py:557
  37.6 26.6 %all_to_all.16 = f32[64,4,384]{2,1,0:T(4,128)S(1)} all-to-all(f32[64,4,384]{2,1,0:T(4,128)S(1)} %bitcast.16), channel_id=1, replica_groups=mesh['sec'=4,'lat'=16,'col'=4] {'col','lat'}, dimensions={0} | all-to-all | bytes 786432 | tf_op jit(solution)/shard_map/all_to_all | solution.py:567
  64.2 1.5 %shard_map.81 = (f32[7,8,2,128]{3,2,1,0:T(2,128)}, f32[336,1,96]{2,1,0:T(1,128)}) custom-call(f32[4,16,4,384]{3,2,1,0:T(4,128)S(1)} %bitcast.15, bf16[8,128,384]{2,1,0:T(8,128)(2,1)S(1)} %get-tuple-element.28.weight_ref, f32[336,1,96]{2,1,0:T(1,128)S(1)} %get-tuple-element.29.state_ref), custom_call_target="tpu_custom_call" | custom-call | tf_op jit(solution)/shard_map/pallas_call | solution.py:570
Async XLA Ops:
  3.4 18.1 %all-to-all-start = ((f32[64,8,128]{2,1,0:T(8,128)}), f32[64,8,128]{2,1,0:T(8,128)S(1)}, u32[]{:S(2)}, u32[]{:S(2)}) async-start(f32[64,8,128]{2,1,0:T(8,128)} %get-tuple-element.18), calls=%async_computation | async-start | bytes 524288 | tf_op jit(solution)/shard_map/all_to_all | solution.py:519
